TPU v7x, 32 devices: a whole 2x2x4 slice. The times are simulated.
32 devices in a mesh: fifth: 4 (over y, x), space: 8 (over z, core).
Axes of the slice: x: 2, y: 2, z: 4, core: 2. Of those that a mesh axis runs over, the one named last changes fastest.
Arguments:
- spinor: float32 [8, 24, 8, 512], P('fifth', None, 'space'), may hold values from -6 to 6
- gauge_links: float32 [4, 18, 8, 512], P(None, None, 'space'), may hold values from -1 to 1, as said below
Outputs:
- filtered: float32 [8, 24, 8, 512], P('fifth', None, 'space')
Inputs may be any that keep to these rules, and one draw needn't show every extreme that they name: `gauge_links`: every link is a special unitary 3 x 3 complex matrix.
All inputs are finite; a program needn't handle non-finite values.
Results may differ from a plain program's by a relative error of at most 0.00002.
Values sent between devices are 32-bit elements; how exact they have to be, the bound alone decides.
No kernel may reach another device: no remote copies, remote signals or barrier semaphores. Data moves between devices by JAX's collectives and lax.ppermute only.
A program may use at most 64 MiB of HBM per device.

v0:
```python
import jax
import jax.numpy as jnp
from jax import lax
from jax.sharding import PartitionSpec as P

L = 8
DEGREE = 4


wall_height = 1.8
quark_mass = 0.1
filter_center = 0.5
filter_radius = 8.0
gamma_block = (((1, 1), (0, 1)), ((1, 2), (0, 0)), ((0, 1), (1, 3)), ((0, 0), (1, 0)))
gamma_adjoint = (((1, 3), (0, 3)), ((1, 0), (0, 2)), ((0, 3), (1, 1)), ((0, 0), (1, 0)))


def shifted(value, axis, steps):
    count = lax.axis_size(axis)
    pairs = [(source, (source + steps) % count) for source in range(count)]
    return lax.ppermute(value, axis, pairs)


def swapped(value, axis, distance):
    mask = 2**distance
    pairs = [(source, source ^ mask) for source in range(lax.axis_size(axis))]
    return lax.ppermute(value, axis, pairs)


def times_unit(values, quarter):
    for repeat in range(quarter % 4):
        values = jnp.stack([-values[..., 1, :, :], values[..., 0, :, :]], axis=-3)
    return values


def project(current, direction, parity):
    halves_list = []
    for top_row in range(2):
        source, quarter = gamma_block[direction][top_row]
        blended = times_unit(current[..., 2 + source, :, :, :, :], quarter)
        halves_list.append(current[..., top_row, :, :, :, :] + parity * blended)
    return jnp.stack(halves_list, axis=-5)


def rebuild(half_spinor, direction, parity):
    lower_part = []
    for row_index in range(2):
        source, quarter = gamma_adjoint[direction][row_index]
        lower_part.append(parity * times_unit(half_spinor[..., source, :, :, :, :], quarter))
    return jnp.concatenate([half_spinor, jnp.stack(lower_part, axis=-5)], axis=-5)


def colour_mul(link_matrix, half_spinor, dagger):
    link_re = link_matrix[:, :, 0]
    link_im = link_matrix[:, :, 1]
    if dagger:
        link_re = jnp.swapaxes(link_re, 0, 1)
        link_im = -jnp.swapaxes(link_im, 0, 1)
    result_re = None
    result_im = None
    for column in range(3):
        half_re = half_spinor[..., column : column + 1, 0, :, :]
        half_im = half_spinor[..., column : column + 1, 1, :, :]
        term_re = link_re[:, column] * half_re - link_im[:, column] * half_im
        term_im = link_re[:, column] * half_im + link_im[:, column] * half_re
        if result_re is None:
            result_re, result_im = (term_re, term_im)
        else:
            result_re = result_re + term_re
            result_im = result_im + term_im
    return jnp.stack([result_re, result_im], axis=-3)


def space_shift(values, stride, extent, forward):
    position = jnp.arange(values.shape[-1]) // stride % extent
    if forward:
        inside_roll = jnp.roll(values, -stride, axis=-1)
        outside_roll = jnp.roll(values, (extent - 1) * stride, axis=-1)
        return jnp.where(position == extent - 1, outside_roll, inside_roll)
    inside_roll = jnp.roll(values, stride, axis=-1)
    outside_roll = jnp.roll(values, -(extent - 1) * stride, axis=-1)
    return jnp.where(position == 0, outside_roll, inside_roll)


def space_hops(current, gauge, extent):
    summed = jnp.zeros_like(current)
    for direction in range(3):
        stride = extent**direction
        forward_half = space_shift(project(current, direction, -1.0), stride, extent, True)
        summed = summed + rebuild(
            colour_mul(gauge[direction], forward_half, False), direction, -1.0
        )
        behind = colour_mul(gauge[direction], project(current, direction, 1.0), True)
        summed = summed + rebuild(space_shift(behind, stride, extent, False), direction, 1.0)
    return summed


def chiral_sign(current):
    return jnp.concatenate([current[:, 0:2], -current[:, 2:4]], axis=1)


def on_device(spinor, gauge_links):
    slices = spinor.shape[0]
    time_depth = spinor.shape[2]
    sites = spinor.shape[3]
    start_field = spinor.reshape(slices, 4, 3, 2, time_depth, sites)
    gauge = gauge_links.reshape(4, 3, 3, 2, time_depth, sites)
    time_links = gauge[3]
    space_count = lax.axis_size("space")
    space_place = lax.axis_index("space")
    fifth_count = lax.axis_size("fifth")
    fifth_place = lax.axis_index("fifth")
    low_sign = jnp.where(space_place == 0, -1.0, 1.0)
    high_sign = jnp.where(space_place == space_count - 1, -1.0, 1.0)
    low_mass = jnp.where(fifth_place == 0, -quark_mass, 1.0)
    high_mass = jnp.where(fifth_place == fifth_count - 1, -quark_mass, 1.0)

    def dirac(current):
        hop_sum = space_hops(current, gauge, L)
        projected = project(current, 3, -1.0)
        from_above = shifted(projected, "space", -1) * high_sign
        forward_half = jnp.concatenate([projected[..., 1:, :], from_above], axis=-2)
        carried = colour_mul(time_links, project(current, 3, 1.0), True)
        from_below = shifted(carried, "space", 1) * low_sign
        behind = jnp.concatenate([from_below, carried[..., : time_depth - 1, :]], axis=-2)
        hop_sum = hop_sum + rebuild(colour_mul(time_links, forward_half, False), 3, -1.0)
        hop_sum = hop_sum + rebuild(behind, 3, 1.0)
        lower_chiral = shifted(current[slices - 1 :, 0:2], "fifth", 1) * low_mass
        upper_chiral = shifted(current[0:1, 2:4], "fifth", -1) * high_mass
        down_half = jnp.concatenate([lower_chiral, current[: slices - 1, 0:2]], axis=0)
        up_half = jnp.concatenate([current[1:, 2:4], upper_chiral], axis=0)
        chiral_hop = jnp.concatenate([down_half, up_half], axis=1)
        return (5.0 - wall_height) * current - 0.5 * hop_sum - chiral_hop

    def mirror(current):
        bit_count = lax.axis_size("fifth").bit_length() - 1
        for bit_index in range(bit_count):
            current = swapped(current, "fifth", bit_index)
        return jnp.flip(current, axis=0)

    def apply_hermitian(current):
        return mirror(chiral_sign(dirac(current)))

    previous = start_field
    current = (apply_hermitian(previous) - filter_center * previous) / filter_radius
    for order in range(1, DEGREE):
        following = (
            2.0 * (apply_hermitian(current) - filter_center * current) / filter_radius - previous
        )
        previous, current = (current, following)
    return current.reshape(slices, 24, time_depth, sites)


def solution(mesh):
    placed = (P("fifth", None, "space", None), P(None, None, "space", None))
    return jax.shard_map(
        on_device,
        mesh=mesh,
        in_specs=placed,
        out_specs=P("fifth", None, "space", None),
        check_vma=False,
    )
```

profile of v0, /device:TPU:0, one launch (start us, length us, event | category | flops | bytes accessed | tf_op | source)
XLA Modules:
  0.0 106.9 jit_solution(11686467914903738397)
XLA Ops:
  0.0 1.0 copy.1232
  1.3 0.8 copy-done
  2.5 0.5 collective-permute-start.1
  3.1 4.1 %collective-permute-start = (f32[2,2,3,2,1,512]{5,3,2,0,4,1:T(2,128)S(1)}, f32[2,2,3,2,1,512]{5,3,2,0,4,1:T(2,128)S(1)}, u32[]{:S(2)}, u32[]{:S(2)}) collective-permute-start(f32[2,2,3,2,1,512]{5,3,2,0,4,1:T(2,128)S(1)} %pad_maximum_fusion.35), channel_id=1, source_target_pairs={{0,7},{1,0},{2,1},{3,2},{4,3},{5,4},{6,5},{7,6},{8,15},{9,8},{10,9... | collective-permute-start | bytes 147464 | tf_op jit(solution)/shard_map/ppermute | solution.py:21
  7.2 3.0 %collective-permute-start.3 = (f32[1,2,3,2,1,512]{5,3,2,0,4,1:T(2,128)S(1)}, f32[1,2,3,2,1,512]{5,3,2,0,4,1:T(2,128)S(1)}, u32[]{:S(2)}, u32[]{:S(2)}) collective-permute-start(f32[1,2,3,2,1,512]{5,3,2,0,4,1:T(2,128)S(1)} %get-tuple-element.135), channel_id=1, source_target_pairs={{0,24},{8,0},{16,8},{24,16},{1,25},{9,1},{17,9},{25,17},{2,26},{10... | collective-permute-start | bytes 73736 | tf_op jit(solution)/shard_map/ppermute | solution.py:21
  10.8 0.2 fusion.407
  11.2 0.2 fusion.62
  12.0 0.2 fusion.410
  12.4 0.2 fusion.60
  17.1 0.5 fusion.7
  17.7 2.0 %collective-permute-start.4 = (f32[2,4,3,2,1,512]{5,3,2,0,4,1:T(2,128)S(1)}, f32[2,4,3,2,1,512]{5,3,2,0,4,1:T(2,128)S(1)}, u32[]{:S(2)}, u32[]{:S(2)}) collective-permute-start(f32[2,4,3,2,1,512]{5,3,2,0,4,1:T(2,128)S(1)} %pad_maximum_fusion), channel_id=1, source_target_pairs={{0,8},{8,0},{16,24},{24,16},{1,9},{9,1},{17,25},{25,17},{2,10},{10... | collective-permute-start | bytes 294920 | tf_op jit(solution)/shard_map/ppermute | solution.py:27
  19.7 2.7 %collective-permute-done.4 = f32[2,4,3,2,1,512]{5,3,2,0,4,1:T(2,128)S(1)} collective-permute-done((f32[2,4,3,2,1,512]{5,3,2,0,4,1:T(2,128)S(1)}, f32[2,4,3,2,1,512]{5,3,2,0,4,1:T(2,128)S(1)}, u32[]{:S(2)}, u32[]{:S(2)}) %collective-permute-start.4) | collective-permute-done | bytes 98336 | tf_op jit(solution)/shard_map/ppermute | solution.py:27
  22.3 1.5 %collective-permute-start.5 = (f32[2,4,3,2,1,512]{5,3,2,0,4,1:T(2,128)S(1)}, f32[2,4,3,2,1,512]{5,3,2,0,4,1:T(2,128)S(1)}, u32[]{:S(2)}, u32[]{:S(2)}) collective-permute-start(f32[2,4,3,2,1,512]{5,3,2,0,4,1:T(2,128)S(1)} %collective-permute-done.4), channel_id=1, source_target_pairs={{0,16},{8,24},{16,0},{24,8},{1,17},{9,25},{17,1},{25,9},{2,18},{10... | collective-permute-start | bytes 294920 | tf_op jit(solution)/shard_map/ppermute | solution.py:27
  23.8 3.2 %collective-permute-done.5 = f32[2,4,3,2,1,512]{5,3,2,0,4,1:T(2,128)S(1)} collective-permute-done((f32[2,4,3,2,1,512]{5,3,2,0,4,1:T(2,128)S(1)}, f32[2,4,3,2,1,512]{5,3,2,0,4,1:T(2,128)S(1)}, u32[]{:S(2)}, u32[]{:S(2)}) %collective-permute-start.5) | collective-permute-done | bytes 98336 | tf_op jit(solution)/shard_map/ppermute | solution.py:27
  27.8 0.2 fusion.403
  28.2 0.2 fusion.44
  29.4 0.2 fusion.405
  29.8 0.2 fusion.48
  32.6 0.2 fusion.179
  33.3 0.2 subtract_add_fusion.14
  33.6 2.0 %collective-permute-start.8 = (f32[1,2,3,2,1,512]{5,3,2,0,4,1:T(2,128)S(1)}, f32[1,2,3,2,1,512]{5,3,2,0,4,1:T(2,128)S(1)}, u32[]{:S(2)}, u32[]{:S(2)}) collective-permute-start(f32[1,2,3,2,1,512]{5,3,2,0,4,1:T(2,128)S(1)} %get-tuple-element.106), channel_id=1, source_target_pairs={{0,8},{8,16},{16,24},{24,0},{1,9},{9,17},{17,25},{25,1},{2,10},{10... | collective-permute-start | bytes 73736 | tf_op jit(solution)/shard_map/ppermute | solution.py:21
  35.6 1.0 collective-permute-start.9
  36.6 3.4 %collective-permute-start.6 = (f32[2,2,3,2,1,512]{5,3,2,0,4,1:T(2,128)S(1)}, f32[2,2,3,2,1,512]{5,3,2,0,4,1:T(2,128)S(1)}, u32[]{:S(2)}, u32[]{:S(2)}) collective-permute-start(f32[2,2,3,2,1,512]{5,3,2,0,4,1:T(2,128)S(1)} %pad_maximum_fusion.37), channel_id=1, source_target_pairs={{0,7},{1,0},{2,1},{3,2},{4,3},{5,4},{6,5},{7,6},{8,15},{9,8},{10,9... | collective-permute-start | bytes 147464 | tf_op jit(solution)/shard_map/ppermute | solution.py:21
  40.7 0.2 fusion.10
  41.0 0.7 collective-permute-done.6
  42.2 0.2 fusion.14
  42.5 0.9 collective-permute-start.10
  43.4 3.8 %collective-permute-done.10 = f32[2,4,3,2,1,512]{5,1,4,3,2,0:T(4,128)S(1)} collective-permute-done((f32[2,4,3,2,1,512]{5,1,4,3,2,0:T(4,128)S(1)}, f32[2,4,3,2,1,512]{5,1,4,3,2,0:T(4,128)S(1)}, u32[]{:S(2)}, u32[]{:S(2)}) %collective-permute-start.10) | collective-permute-done | bytes 98336 | tf_op jit(solution)/shard_map/ppermute | solution.py:27
  47.2 1.2 %collective-permute-start.11 = (f32[2,4,3,2,1,512]{5,1,4,3,2,0:T(4,128)S(1)}, f32[2,4,3,2,1,512]{5,1,4,3,2,0:T(4,128)S(1)}, u32[]{:S(2)}, u32[]{:S(2)}) collective-permute-start(f32[2,4,3,2,1,512]{5,1,4,3,2,0:T(4,128)S(1)} %collective-permute-done.10), channel_id=1, source_target_pairs={{0,16},{8,24},{16,0},{24,8},{1,17},{9,25},{17,1},{25,9},{2,18},{10... | collective-permute-start | bytes 294920 | tf_op jit(solution)/shard_map/ppermute | solution.py:27
  48.4 3.4 %collective-permute-done.11 = f32[2,4,3,2,1,512]{5,1,4,3,2,0:T(4,128)S(1)} collective-permute-done((f32[2,4,3,2,1,512]{5,1,4,3,2,0:T(4,128)S(1)}, f32[2,4,3,2,1,512]{5,1,4,3,2,0:T(4,128)S(1)}, u32[]{:S(2)}, u32[]{:S(2)}) %collective-permute-start.11) | collective-permute-done | bytes 98336 | tf_op jit(solution)/shard_map/ppermute | solution.py:27
  53.3 0.2 fusion.398
  53.7 0.2 fusion.37
  54.8 0.2 add_add_fusion.10
  54.9 0.2 fusion.400
  55.3 0.2 fusion.41
  56.8 0.2 subtract_add_fusion.13
  57.1 0.8 collective-permute-start.14
  58.4 3.6 %collective-permute-start.12 = (f32[2,2,3,2,1,512]{5,3,2,0,4,1:T(2,128)S(1)}, f32[2,2,3,2,1,512]{5,3,2,0,4,1:T(2,128)S(1)}, u32[]{:S(2)}, u32[]{:S(2)}) collective-permute-start(f32[2,2,3,2,1,512]{5,3,2,0,4,1:T(2,128)S(1)} %pad_maximum_fusion.39), channel_id=1, source_target_pairs={{0,7},{1,0},{2,1},{3,2},{4,3},{5,4},{6,5},{7,6},{8,15},{9,8},{10,9... | collective-permute-start | bytes 147464 | tf_op jit(solution)/shard_map/ppermute | solution.py:21
  62.2 0.2 fusion.69
  63.1 0.2 fusion.18
  63.4 2.4 %collective-permute-start.15 = (f32[1,2,3,2,1,512]{5,1,4,3,2,0:T(2,128)S(1)}, f32[1,2,3,2,1,512]{5,1,4,3,2,0:T(2,128)S(1)}, u32[]{:S(2)}, u32[]{:S(2)}) collective-permute-start(f32[1,2,3,2,1,512]{5,1,4,3,2,0:T(2,128)S(1)} %get-tuple-element.76), channel_id=1, source_target_pairs={{0,24},{8,0},{16,8},{24,16},{1,25},{9,1},{17,9},{25,17},{2,26},{10... | collective-permute-start | bytes 73736 | tf_op jit(solution)/shard_map/ppermute | solution.py:21
  65.8 1.7 %collective-permute-done.15 = f32[1,2,3,2,1,512]{5,1,4,3,2,0:T(2,128)S(1)} collective-permute-done((f32[1,2,3,2,1,512]{5,1,4,3,2,0:T(2,128)S(1)}, f32[1,2,3,2,1,512]{5,1,4,3,2,0:T(2,128)S(1)}, u32[]{:S(2)}, u32[]{:S(2)}) %collective-permute-start.15) | collective-permute-done | bytes 24608 | tf_op jit(solution)/shard_map/ppermute | solution.py:21
  68.1 0.3 fusion.23
  68.4 3.1 %collective-permute-start.16 = (f32[2,4,3,2,1,512]{5,1,4,3,2,0:T(4,128)S(1)}, f32[2,4,3,2,1,512]{5,1,4,3,2,0:T(4,128)S(1)}, u32[]{:S(2)}, u32[]{:S(2)}) collective-permute-start(f32[2,4,3,2,1,512]{5,1,4,3,2,0:T(4,128)S(1)} %pad_maximum_fusion.3), channel_id=1, source_target_pairs={{0,8},{8,0},{16,24},{24,16},{1,9},{9,1},{17,25},{25,17},{2,10},{10... | collective-permute-start | bytes 294920 | tf_op jit(solution)/shard_map/ppermute | solution.py:27
  71.5 2.6 %collective-permute-done.16 = f32[2,4,3,2,1,512]{5,1,4,3,2,0:T(4,128)S(1)} collective-permute-done((f32[2,4,3,2,1,512]{5,1,4,3,2,0:T(4,128)S(1)}, f32[2,4,3,2,1,512]{5,1,4,3,2,0:T(4,128)S(1)}, u32[]{:S(2)}, u32[]{:S(2)}) %collective-permute-start.16) | collective-permute-done | bytes 98336 | tf_op jit(solution)/shard_map/ppermute | solution.py:27
  74.1 0.8 collective-permute-start.17
  74.9 3.8 %collective-permute-done.17 = f32[2,4,3,2,1,512]{5,1,4,3,2,0:T(4,128)S(1)} collective-permute-done((f32[2,4,3,2,1,512]{5,1,4,3,2,0:T(4,128)S(1)}, f32[2,4,3,2,1,512]{5,1,4,3,2,0:T(4,128)S(1)}, u32[]{:S(2)}, u32[]{:S(2)}) %collective-permute-start.17) | collective-permute-done | bytes 98336 | tf_op jit(solution)/shard_map/ppermute | solution.py:27
  79.6 0.2 fusion.392
  79.9 0.2 fusion.56
  80.7 0.2 fusion.395
  81.0 0.2 fusion.58
  84.4 0.2 fusion.180
  84.6 2.1 %collective-permute-start.20 = (f32[1,2,3,2,1,512]{5,3,2,0,4,1:T(2,128)S(1)}, f32[1,2,3,2,1,512]{5,3,2,0,4,1:T(2,128)S(1)}, u32[]{:S(2)}, u32[]{:S(2)}) collective-permute-start(f32[1,2,3,2,1,512]{5,3,2,0,4,1:T(2,128)S(1)} %copy.2076), channel_id=1, source_target_pairs={{0,8},{8,16},{16,24},{24,0},{1,9},{9,17},{17,25},{25,1},{2,10},{10... | collective-permute-start | bytes 73736 | tf_op jit(solution)/shard_map/ppermute | solution.py:21
  87.1 3.6 %collective-permute-start.18 = (f32[2,2,3,2,1,512]{5,3,2,0,4,1:T(2,128)S(1)}, f32[2,2,3,2,1,512]{5,3,2,0,4,1:T(2,128)S(1)}, u32[]{:S(2)}, u32[]{:S(2)}) collective-permute-start(f32[2,2,3,2,1,512]{5,3,2,0,4,1:T(2,128)S(1)} %pad_maximum_fusion.42), channel_id=1, source_target_pairs={{0,7},{1,0},{2,1},{3,2},{4,3},{5,4},{6,5},{7,6},{8,15},{9,8},{10,9... | collective-permute-start | bytes 147464 | tf_op jit(solution)/shard_map/ppermute | solution.py:21
  91.3 0.2 fusion.26
  91.5 0.2 maximum_add_fusion.7
  91.8 1.0 collective-permute-start.21
  92.7 3.2 %collective-permute-done.21 = f32[1,2,3,2,1,512]{5,1,4,3,2,0:T(2,128)S(1)} collective-permute-done((f32[1,2,3,2,1,512]{5,1,4,3,2,0:T(2,128)S(1)}, f32[1,2,3,2,1,512]{5,1,4,3,2,0:T(2,128)S(1)}, u32[]{:S(2)}, u32[]{:S(2)}) %collective-permute-start.21) | collective-permute-done | bytes 24608 | tf_op jit(solution)/shard_map/ppermute | solution.py:21
  96.4 0.2 fusion.30
  96.7 0.9 collective-permute-start.22
  97.6 3.8 %collective-permute-done.22 = f32[2,4,3,2,1,512]{5,1,4,3,2,0:T(4,128)S(1)} collective-permute-done((f32[2,4,3,2,1,512]{5,1,4,3,2,0:T(4,128)S(1)}, f32[2,4,3,2,1,512]{5,1,4,3,2,0:T(4,128)S(1)}, u32[]{:S(2)}, u32[]{:S(2)}) %collective-permute-start.22) | collective-permute-done | bytes 98336 | tf_op jit(solution)/shard_map/ppermute | solution.py:27
  101.4 0.6 collective-permute-start.23
  102.0 4.0 %collective-permute-done.23 = f32[2,4,3,2,1,512]{5,1,4,3,2,0:T(4,128)S(1)} collective-permute-done((f32[2,4,3,2,1,512]{5,1,4,3,2,0:T(4,128)S(1)}, f32[2,4,3,2,1,512]{5,1,4,3,2,0:T(4,128)S(1)}, u32[]{:S(2)}, u32[]{:S(2)}) %collective-permute-start.23) | collective-permute-done | bytes 98336 | tf_op jit(solution)/shard_map/ppermute | solution.py:27
  106.1 0.7 copy.1852
  (629 shorter events, 22.9 us)
Async XLA Ops:
  1.1 0.9 copy-start
  2.5 14.5 %collective-permute-start.1 = (f32[2,2,3,2,1,512]{5,3,2,0,4,1:T(2,128)S(1)}, f32[2,2,3,2,1,512]{5,3,2,0,4,1:T(2,128)S(1)}, u32[]{:S(2)}, u32[]{:S(2)}) collective-permute-start(f32[2,2,3,2,1,512]{5,3,2,0,4,1:T(2,128)S(1)} %pad_maximum_fusion.36), channel_id=1, source_target_pairs={{0,1},{1,2},{2,3},{3,4},{4,5},{5,6},{6,7},{7,0},{8,9},{9,10},{10,1... | collective-permute-start | bytes 147464 | tf_op jit(solution)/shard_map/ppermute | solution.py:21
  3.1 13.6 %collective-permute-start = (f32[2,2,3,2,1,512]{5,3,2,0,4,1:T(2,128)S(1)}, f32[2,2,3,2,1,512]{5,3,2,0,4,1:T(2,128)S(1)}, u32[]{:S(2)}, u32[]{:S(2)}) collective-permute-start(f32[2,2,3,2,1,512]{5,3,2,0,4,1:T(2,128)S(1)} %pad_maximum_fusion.35), channel_id=1, source_target_pairs={{0,7},{1,0},{2,1},{3,2},{4,3},{5,4},{6,5},{7,6},{8,15},{9,8},{10,9... | collective-permute-start | bytes 147464 | tf_op jit(solution)/shard_map/ppermute | solution.py:21
  7.2 9.4 %collective-permute-start.3 = (f32[1,2,3,2,1,512]{5,3,2,0,4,1:T(2,128)S(1)}, f32[1,2,3,2,1,512]{5,3,2,0,4,1:T(2,128)S(1)}, u32[]{:S(2)}, u32[]{:S(2)}) collective-permute-start(f32[1,2,3,2,1,512]{5,3,2,0,4,1:T(2,128)S(1)} %get-tuple-element.135), channel_id=1, source_target_pairs={{0,24},{8,0},{16,8},{24,16},{1,25},{9,1},{17,9},{25,17},{2,26},{10... | collective-permute-start | bytes 73736 | tf_op jit(solution)/shard_map/ppermute | solution.py:21
  10.2 6.5 %collective-permute-start.2 = (f32[1,2,3,2,1,512]{5,3,2,0,4,1:T(2,128)S(1)}, f32[1,2,3,2,1,512]{5,3,2,0,4,1:T(2,128)S(1)}, u32[]{:S(2)}, u32[]{:S(2)}) collective-permute-start(f32[1,2,3,2,1,512]{5,3,2,0,4,1:T(2,128)S(1)} %get-tuple-element.134), channel_id=1, source_target_pairs={{0,8},{8,16},{16,24},{24,0},{1,9},{9,17},{17,25},{25,1},{2,10},{10... | collective-permute-start | bytes 73736 | tf_op jit(solution)/shard_map/ppermute | solution.py:21
  17.7 4.7 %collective-permute-start.4 = (f32[2,4,3,2,1,512]{5,3,2,0,4,1:T(2,128)S(1)}, f32[2,4,3,2,1,512]{5,3,2,0,4,1:T(2,128)S(1)}, u32[]{:S(2)}, u32[]{:S(2)}) collective-permute-start(f32[2,4,3,2,1,512]{5,3,2,0,4,1:T(2,128)S(1)} %pad_maximum_fusion), channel_id=1, source_target_pairs={{0,8},{8,0},{16,24},{24,16},{1,9},{9,1},{17,25},{25,17},{2,10},{10... | collective-permute-start | bytes 294920 | tf_op jit(solution)/shard_map/ppermute | solution.py:27
  22.3 4.6 %collective-permute-start.5 = (f32[2,4,3,2,1,512]{5,3,2,0,4,1:T(2,128)S(1)}, f32[2,4,3,2,1,512]{5,3,2,0,4,1:T(2,128)S(1)}, u32[]{:S(2)}, u32[]{:S(2)}) collective-permute-start(f32[2,4,3,2,1,512]{5,3,2,0,4,1:T(2,128)S(1)} %collective-permute-done.4), channel_id=1, source_target_pairs={{0,16},{8,24},{16,0},{24,8},{1,17},{9,25},{17,1},{25,9},{2,18},{10... | collective-permute-start | bytes 294920 | tf_op jit(solution)/shard_map/ppermute | solution.py:27
  33.5 8.4 %collective-permute-start.7 = (f32[2,2,3,2,1,512]{5,3,2,0,4,1:T(2,128)S(1)}, f32[2,2,3,2,1,512]{5,3,2,0,4,1:T(2,128)S(1)}, u32[]{:S(2)}, u32[]{:S(2)}) collective-permute-start(f32[2,2,3,2,1,512]{5,3,2,0,4,1:T(2,128)S(1)} %pad_maximum_fusion.38), channel_id=1, source_target_pairs={{0,1},{1,2},{2,3},{3,4},{4,5},{5,6},{6,7},{7,0},{8,9},{9,10},{10,1... | collective-permute-start | bytes 147464 | tf_op jit(solution)/shard_map/ppermute | solution.py:21
  33.6 7.4 %collective-permute-start.8 = (f32[1,2,3,2,1,512]{5,3,2,0,4,1:T(2,128)S(1)}, f32[1,2,3,2,1,512]{5,3,2,0,4,1:T(2,128)S(1)}, u32[]{:S(2)}, u32[]{:S(2)}) collective-permute-start(f32[1,2,3,2,1,512]{5,3,2,0,4,1:T(2,128)S(1)} %get-tuple-element.106), channel_id=1, source_target_pairs={{0,8},{8,16},{16,24},{24,0},{1,9},{9,17},{17,25},{25,1},{2,10},{10... | collective-permute-start | bytes 73736 | tf_op jit(solution)/shard_map/ppermute | solution.py:21
  35.6 5.4 %collective-permute-start.9 = (f32[1,2,3,2,1,512]{5,3,2,0,4,1:T(2,128)S(1)}, f32[1,2,3,2,1,512]{5,3,2,0,4,1:T(2,128)S(1)}, u32[]{:S(2)}, u32[]{:S(2)}) collective-permute-start(f32[1,2,3,2,1,512]{5,3,2,0,4,1:T(2,128)S(1)} %get-tuple-element.107), channel_id=1, source_target_pairs={{0,24},{8,0},{16,8},{24,16},{1,25},{9,1},{17,9},{25,17},{2,26},{10... | collective-permute-start | bytes 73736 | tf_op jit(solution)/shard_map/ppermute | solution.py:21
  36.6 5.1 %collective-permute-start.6 = (f32[2,2,3,2,1,512]{5,3,2,0,4,1:T(2,128)S(1)}, f32[2,2,3,2,1,512]{5,3,2,0,4,1:T(2,128)S(1)}, u32[]{:S(2)}, u32[]{:S(2)}) collective-permute-start(f32[2,2,3,2,1,512]{5,3,2,0,4,1:T(2,128)S(1)} %pad_maximum_fusion.37), channel_id=1, source_target_pairs={{0,7},{1,0},{2,1},{3,2},{4,3},{5,4},{6,5},{7,6},{8,15},{9,8},{10,9... | collective-permute-start | bytes 147464 | tf_op jit(solution)/shard_map/ppermute | solution.py:21
  42.5 4.7 %collective-permute-start.10 = (f32[2,4,3,2,1,512]{5,1,4,3,2,0:T(4,128)S(1)}, f32[2,4,3,2,1,512]{5,1,4,3,2,0:T(4,128)S(1)}, u32[]{:S(2)}, u32[]{:S(2)}) collective-permute-start(f32[2,4,3,2,1,512]{5,1,4,3,2,0:T(4,128)S(1)} %pad_maximum_fusion.2), channel_id=1, source_target_pairs={{0,8},{8,0},{16,24},{24,16},{1,9},{9,1},{17,25},{25,17},{2,10},{10... | collective-permute-start | bytes 294920 | tf_op jit(solution)/shard_map/ppermute | solution.py:27
  47.2 4.6 %collective-permute-start.11 = (f32[2,4,3,2,1,512]{5,1,4,3,2,0:T(4,128)S(1)}, f32[2,4,3,2,1,512]{5,1,4,3,2,0:T(4,128)S(1)}, u32[]{:S(2)}, u32[]{:S(2)}) collective-permute-start(f32[2,4,3,2,1,512]{5,1,4,3,2,0:T(4,128)S(1)} %collective-permute-done.10), channel_id=1, source_target_pairs={{0,16},{8,24},{16,0},{24,8},{1,17},{9,25},{17,1},{25,9},{2,18},{10... | collective-permute-start | bytes 294920 | tf_op jit(solution)/shard_map/ppermute | solution.py:27
  57.1 8.7 %collective-permute-start.14 = (f32[1,2,3,2,1,512]{5,3,2,0,4,1:T(2,128)S(1)}, f32[1,2,3,2,1,512]{5,3,2,0,4,1:T(2,128)S(1)}, u32[]{:S(2)}, u32[]{:S(2)}) collective-permute-start(f32[1,2,3,2,1,512]{5,3,2,0,4,1:T(2,128)S(1)} %copy.2070), channel_id=1, source_target_pairs={{0,8},{8,16},{16,24},{24,0},{1,9},{9,17},{17,25},{25,1},{2,10},{10... | collective-permute-start | bytes 73736 | tf_op jit(solution)/shard_map/ppermute | solution.py:21
  58.3 9.8 %collective-permute-start.13 = (f32[2,2,3,2,1,512]{5,3,2,0,4,1:T(2,128)S(1)}, f32[2,2,3,2,1,512]{5,3,2,0,4,1:T(2,128)S(1)}, u32[]{:S(2)}, u32[]{:S(2)}) collective-permute-start(f32[2,2,3,2,1,512]{5,3,2,0,4,1:T(2,128)S(1)} %pad_maximum_fusion.40), channel_id=1, source_target_pairs={{0,1},{1,2},{2,3},{3,4},{4,5},{5,6},{6,7},{7,0},{8,9},{9,10},{10,1... | collective-permute-start | bytes 147464 | tf_op jit(solution)/shard_map/ppermute | solution.py:21
  58.4 9.2 %collective-permute-start.12 = (f32[2,2,3,2,1,512]{5,3,2,0,4,1:T(2,128)S(1)}, f32[2,2,3,2,1,512]{5,3,2,0,4,1:T(2,128)S(1)}, u32[]{:S(2)}, u32[]{:S(2)}) collective-permute-start(f32[2,2,3,2,1,512]{5,3,2,0,4,1:T(2,128)S(1)} %pad_maximum_fusion.39), channel_id=1, source_target_pairs={{0,7},{1,0},{2,1},{3,2},{4,3},{5,4},{6,5},{7,6},{8,15},{9,8},{10,9... | collective-permute-start | bytes 147464 | tf_op jit(solution)/shard_map/ppermute | solution.py:21
  63.4 4.1 %collective-permute-start.15 = (f32[1,2,3,2,1,512]{5,1,4,3,2,0:T(2,128)S(1)}, f32[1,2,3,2,1,512]{5,1,4,3,2,0:T(2,128)S(1)}, u32[]{:S(2)}, u32[]{:S(2)}) collective-permute-start(f32[1,2,3,2,1,512]{5,1,4,3,2,0:T(2,128)S(1)} %get-tuple-element.76), channel_id=1, source_target_pairs={{0,24},{8,0},{16,8},{24,16},{1,25},{9,1},{17,9},{25,17},{2,26},{10... | collective-permute-start | bytes 73736 | tf_op jit(solution)/shard_map/ppermute | solution.py:21
  68.4 5.7 %collective-permute-start.16 = (f32[2,4,3,2,1,512]{5,1,4,3,2,0:T(4,128)S(1)}, f32[2,4,3,2,1,512]{5,1,4,3,2,0:T(4,128)S(1)}, u32[]{:S(2)}, u32[]{:S(2)}) collective-permute-start(f32[2,4,3,2,1,512]{5,1,4,3,2,0:T(4,128)S(1)} %pad_maximum_fusion.3), channel_id=1, source_target_pairs={{0,8},{8,0},{16,24},{24,16},{1,9},{9,1},{17,25},{25,17},{2,10},{10... | collective-permute-start | bytes 294920 | tf_op jit(solution)/shard_map/ppermute | solution.py:27
  74.1 4.6 %collective-permute-start.17 = (f32[2,4,3,2,1,512]{5,1,4,3,2,0:T(4,128)S(1)}, f32[2,4,3,2,1,512]{5,1,4,3,2,0:T(4,128)S(1)}, u32[]{:S(2)}, u32[]{:S(2)}) collective-permute-start(f32[2,4,3,2,1,512]{5,1,4,3,2,0:T(4,128)S(1)} %collective-permute-done.16), channel_id=1, source_target_pairs={{0,16},{8,24},{16,0},{24,8},{1,17},{9,25},{17,1},{25,9},{2,18},{10... | collective-permute-start | bytes 294920 | tf_op jit(solution)/shard_map/ppermute | solution.py:27
  84.6 8.1 %collective-permute-start.20 = (f32[1,2,3,2,1,512]{5,3,2,0,4,1:T(2,128)S(1)}, f32[1,2,3,2,1,512]{5,3,2,0,4,1:T(2,128)S(1)}, u32[]{:S(2)}, u32[]{:S(2)}) collective-permute-start(f32[1,2,3,2,1,512]{5,3,2,0,4,1:T(2,128)S(1)} %copy.2076), channel_id=1, source_target_pairs={{0,8},{8,16},{16,24},{24,0},{1,9},{9,17},{17,25},{25,1},{2,10},{10... | collective-permute-start | bytes 73736 | tf_op jit(solution)/shard_map/ppermute | solution.py:21
  87.0 9.3 %collective-permute-start.19 = (f32[2,2,3,2,1,512]{5,3,2,0,4,1:T(2,128)S(1)}, f32[2,2,3,2,1,512]{5,3,2,0,4,1:T(2,128)S(1)}, u32[]{:S(2)}, u32[]{:S(2)}) collective-permute-start(f32[2,2,3,2,1,512]{5,3,2,0,4,1:T(2,128)S(1)} %pad_maximum_fusion.43), channel_id=1, source_target_pairs={{0,1},{1,2},{2,3},{3,4},{4,5},{5,6},{6,7},{7,0},{8,9},{9,10},{10,1... | collective-permute-start | bytes 147464 | tf_op jit(solution)/shard_map/ppermute | solution.py:21
  87.1 8.8 %collective-permute-start.18 = (f32[2,2,3,2,1,512]{5,3,2,0,4,1:T(2,128)S(1)}, f32[2,2,3,2,1,512]{5,3,2,0,4,1:T(2,128)S(1)}, u32[]{:S(2)}, u32[]{:S(2)}) collective-permute-start(f32[2,2,3,2,1,512]{5,3,2,0,4,1:T(2,128)S(1)} %pad_maximum_fusion.42), channel_id=1, source_target_pairs={{0,7},{1,0},{2,1},{3,2},{4,3},{5,4},{6,5},{7,6},{8,15},{9,8},{10,9... | collective-permute-start | bytes 147464 | tf_op jit(solution)/shard_map/ppermute | solution.py:21
  91.8 4.1 %collective-permute-start.21 = (f32[1,2,3,2,1,512]{5,1,4,3,2,0:T(2,128)S(1)}, f32[1,2,3,2,1,512]{5,1,4,3,2,0:T(2,128)S(1)}, u32[]{:S(2)}, u32[]{:S(2)}) collective-permute-start(f32[1,2,3,2,1,512]{5,1,4,3,2,0:T(2,128)S(1)} %get-tuple-element.54), channel_id=1, source_target_pairs={{0,24},{8,0},{16,8},{24,16},{1,25},{9,1},{17,9},{25,17},{2,26},{10... | collective-permute-start | bytes 73736 | tf_op jit(solution)/shard_map/ppermute | solution.py:21
  96.7 4.7 %collective-permute-start.22 = (f32[2,4,3,2,1,512]{5,1,4,3,2,0:T(4,128)S(1)}, f32[2,4,3,2,1,512]{5,1,4,3,2,0:T(4,128)S(1)}, u32[]{:S(2)}, u32[]{:S(2)}) collective-permute-start(f32[2,4,3,2,1,512]{5,1,4,3,2,0:T(4,128)S(1)} %pad_maximum_fusion.4), channel_id=1, source_target_pairs={{0,8},{8,0},{16,24},{24,16},{1,9},{9,1},{17,25},{25,17},{2,10},{10... | collective-permute-start | bytes 294920 | tf_op jit(solution)/shard_map/ppermute | solution.py:27
  101.4 4.6 %collective-permute-start.23 = (f32[2,4,3,2,1,512]{5,1,4,3,2,0:T(4,128)S(1)}, f32[2,4,3,2,1,512]{5,1,4,3,2,0:T(4,128)S(1)}, u32[]{:S(2)}, u32[]{:S(2)}) collective-permute-start(f32[2,4,3,2,1,512]{5,1,4,3,2,0:T(4,128)S(1)} %collective-permute-done.22), channel_id=1, source_target_pairs={{0,16},{8,24},{16,0},{24,8},{1,17},{9,25},{17,1},{25,9},{2,18},{10... | collective-permute-start | bytes 294920 | tf_op jit(solution)/shard_map/ppermute | solution.py:27
where the time goes:
time: 107 us
  starting transfers between devices  38.5 us (36%)
  waiting for transfers between devices  32.9 us (31%)
  other arithmetic  24.2 us (23%)
  local copies, waits for them, and re-layouts  6.62 us (6%)
  between operations  4.61 us (4%)
    ppermute x16, starting transfers between devices, shifted(): return lax.ppermute(value, axis, pairs)  27.6 us
    ppermute x8, waiting for transfers between devices, swapped(): return lax.ppermute(value, axis, pairs)  27.3 us
    ppermute x8, starting transfers between devices, swapped(): return lax.ppermute(value, axis, pairs)  10.9 us
    ppermute x16, waiting for transfers between devices, shifted(): return lax.ppermute(value, axis, pairs)  5.59 us
    another operation x41, other arithmetic, colour_mul(): return jnp.stack([result_re, result_im], axis=-3)  2.97 us
    another operation x48, other arithmetic, project(): return jnp.stack(halves_list, axis=-5)  2.93 us
    add x20, other arithmetic, colour_mul(): result_re = result_re + term_re  2.7 us
    concatenate x48, other arithmetic, rebuild(): jnp.concatenate([half_spinor, jnp.stack(lower_part, axis=-5)], axis=-5)  2.17 us
  transfers between devices with their start and end apart: 24, of which 11 were waited for; matrix products, arithmetic and copies ran while one was open for 10% of the time, Pallas kernels for 0%

commit v1 on v0

v1 whole, which is shorter than its diff:
```python
import jax
import jax.numpy as jnp
import numpy as np
from jax import lax
from jax.experimental import pallas as pl
from jax.experimental.pallas import tpu as pltpu
from jax.sharding import PartitionSpec as P

DEGREE = 4
LANES = 128

wall_height = 1.8
quark_mass = 0.1
filter_center = 0.5
filter_radius = 8.0
gamma_block = (((1, 1), (0, 1)), ((1, 2), (0, 0)), ((0, 1), (1, 3)), ((0, 0), (1, 0)))
gamma_adjoint = (((1, 3), (0, 3)), ((1, 0), (0, 2)), ((0, 3), (1, 1)), ((0, 0), (1, 0)))
TIME = 3


def power_coefficients(degree):
    series = np.polynomial.chebyshev.cheb2poly([0.0] * degree + [1.0])
    line = np.polynomial.Polynomial([-filter_center / filter_radius, 1.0 / filter_radius])
    total = np.polynomial.Polynomial([0.0])
    for order, weight in enumerate(series):
        total = total + weight * line**order
    return [float(value) for value in total.coef]


def plus_unit(base, other, quarter, parity):
    turn = (quarter + (2 if parity < 0 else 0)) % 4
    if turn == 0:
        return base[0] + other[0], base[1] + other[1]
    if turn == 1:
        return base[0] - other[1], base[1] + other[0]
    if turn == 2:
        return base[0] - other[0], base[1] - other[1]
    return base[0] + other[1], base[1] - other[0]


def project(field, direction, parity):
    halves = []
    for row in range(2):
        source, quarter = gamma_block[direction][row]
        halves.append(
            [plus_unit(field[row][c], field[2 + source][c], quarter, parity) for c in range(3)]
        )
    return halves


def add_rebuilt(total, half, direction, parity):
    for row in range(2):
        source, quarter = gamma_adjoint[direction][row]
        for c in range(3):
            total[row][c] = (total[row][c][0] + half[row][c][0], total[row][c][1] + half[row][c][1])
            total[2 + row][c] = plus_unit(total[2 + row][c], half[source][c], quarter, parity)


def colour_mul(link, half, dagger):
    result = []
    for spin in range(2):
        rows = []
        for row in range(3):
            total = None
            for column in range(3):
                h_re, h_im = half[spin][column]
                if dagger:
                    l_re, l_im = link[column][row]
                    t_re = l_re * h_re + l_im * h_im
                    t_im = l_re * h_im - l_im * h_re
                else:
                    l_re, l_im = link[row][column]
                    t_re = l_re * h_re - l_im * h_im
                    t_im = l_re * h_im + l_im * h_re
                total = (t_re, t_im) if total is None else (total[0] + t_re, total[1] + t_im)
            rows.append(total)
        result.append(rows)
    return result


class Shape:
    def __init__(self, slices, sites):
        self.slices = slices
        self.sites = sites
        self.blocks = sites // LANES
        self.rows = slices * self.blocks
        self.extent = round(sites ** (1.0 / 3.0))
        assert self.extent**3 == sites and sites % LANES == 0


def index_of(shape, axis):
    return lax.broadcasted_iota(jnp.int32, (shape.rows, LANES), axis)


def turned(value, steps, axis):
    size = value.shape[axis]
    if steps % size == 0:
        return value
    return pltpu.roll(value, (-steps) % size, axis)


def space_shift(shape, stride, forward):
    extent = shape.extent
    group = stride * extent
    sign = 1 if forward else -1
    lane = index_of(shape, 1)
    if LANES % group == 0:
        place = lane // stride % extent
        edge = place == (extent - 1 if forward else 0)
        return lambda v: jnp.where(
            edge, turned(v, -sign * (extent - 1) * stride, 1), turned(v, sign * stride, 1)
        )
    assert group == shape.sites and stride < LANES
    block = index_of(shape, 0) % shape.blocks
    wraps = block == (shape.blocks - 1 if forward else 0)
    stays = lane < LANES - stride if forward else lane >= stride

    def shift(v):
        across = turned(v, sign * stride, 1)
        other = jnp.where(
            wraps, turned(across, -sign * (shape.blocks - 1), 0), turned(across, sign, 0)
        )
        return jnp.where(stays, across, other)

    return shift


def load_field(ref):
    return [[(ref[(s * 3 + c) * 2], ref[(s * 3 + c) * 2 + 1]) for c in range(3)] for s in range(4)]


def load_half(ref):
    return [[(ref[(s * 3 + c) * 2], ref[(s * 3 + c) * 2 + 1]) for c in range(3)] for s in range(2)]


def store_parts(ref, parts, rows=None):
    for s, colours in enumerate(parts):
        for c, pair in enumerate(colours):
            for p, value in enumerate(pair):
                if rows is None:
                    ref[(s * 3 + c) * 2 + p] = value
                else:
                    ref[(s * 3 + c) * 2 + p] = value[rows[0] : rows[1]]


def load_link(ref, direction):
    return [
        [(ref[direction * 18 + (r * 3 + c) * 2], ref[direction * 18 + (r * 3 + c) * 2 + 1]) for c in range(3)]
        for r in range(3)
    ]


def raw_field(shape, ref, mirrored):
    order = range(shape.slices)
    if mirrored:
        order = reversed(order)
    order = list(order)

    def part(index):
        return jnp.concatenate([ref[j, index] for j in order], axis=0)

    return [[(part((s * 3 + c) * 2), part((s * 3 + c) * 2 + 1)) for c in range(3)] for s in range(4)]


def pick(flag, first, second):
    return [
        [tuple(jnp.where(flag, a, b) for a, b in zip(p, q)) for p, q in zip(x, y)]
        for x, y in zip(first, second)
    ]


def send_parts(shape, field, link, even, odd_step, near_ref, far_ref, up_ref, down_ref):
    ahead = project(field, TIME, -1.0)
    behind = colour_mul(link, project(field, TIME, 1.0), True)
    store_parts(far_ref, pick(even, ahead, behind))
    first = (0, shape.blocks)
    last = (shape.rows - shape.blocks, shape.rows)
    upper, lower = field[0:2], field[2:4]
    store_parts(up_ref, lower if odd_step else upper, last)
    store_parts(down_ref, upper if odd_step else lower, first)
    store_parts(near_ref, pick(even, behind, ahead))


def widen_kernel(shape, links_ref, wide_ref):
    for mu in range(4):
        for index in range(18):
            value = links_ref[mu, index]
            wide_ref[mu * 18 + index] = jnp.concatenate([value] * shape.slices, axis=0)


def first_kernel(shape, scalar_ref, spinor_ref, links_ref, field_ref, near_ref, far_ref, up_ref, down_ref):
    even = scalar_ref[4] > 0.5
    field = raw_field(shape, spinor_ref, False)
    store_parts(field_ref, field)

    def link_part(index):
        return jnp.concatenate([links_ref[TIME, index]] * shape.slices, axis=0)

    link = [[(link_part((r * 3 + c) * 2), link_part((r * 3 + c) * 2 + 1)) for c in range(3)] for r in range(3)]
    send_parts(shape, field, link, even, False, near_ref, far_ref, up_ref, down_ref)


def space_kernel(shape, odd_step, field_ref, wide_ref, part_ref):
    field = load_field(field_ref)
    zero = jnp.zeros((shape.rows, LANES), jnp.float32)
    total = [[(zero, zero) for _ in range(3)] for _ in range(4)]
    for mu in range(3):
        stride = shape.extent**mu
        link = load_link(wide_ref, mu)
        ahead = space_shift(shape, stride, True)
        half = project(field, mu, -1.0)
        half = [[tuple(ahead(v) for v in pair) for pair in spin] for spin in half]
        add_rebuilt(total, colour_mul(link, half, False), mu, -1.0)
        behind = space_shift(shape, stride, False)
        half = colour_mul(link, project(field, mu, 1.0), True)
        half = [[tuple(behind(v) for v in pair) for pair in spin] for spin in half]
        add_rebuilt(total, half, mu, 1.0)
    row = index_of(shape, 0)
    inner_low = row >= shape.blocks
    inner_high = row < shape.rows - shape.blocks
    result = []
    for s in range(4):
        from_low = (s < 2) != odd_step
        colours = []
        for c in range(3):
            pair = []
            for p in range(2):
                value = field[s][c][p]
                if from_low:
                    hop = jnp.where(inner_low, turned(value, -shape.blocks, 0), 0.0)
                else:
                    hop = jnp.where(inner_high, turned(value, shape.blocks, 0), 0.0)
                pair.append((5.0 - wall_height) * value - 0.5 * total[s][c][p] - hop)
            colours.append(tuple(pair))
        result.append(colours)
    store_parts(part_ref, result)


def close_kernel(
    shape, odd_step, scale, weight, mirrored, last, scalar_ref, part_ref, wide_ref, start_ref, near_ref, far_ref,
    low_ref, high_ref, *out_refs
):
    even = scalar_ref[4] > 0.5
    low_sign, high_sign = scalar_ref[0], scalar_ref[1]
    low_mass, high_mass = scalar_ref[2], scalar_ref[3]
    link = load_link(wide_ref, TIME)
    near, far = load_half(near_ref), load_half(far_ref)
    ahead = colour_mul(link, pick(even, near, far), False)
    behind = pick(even, far, near)
    zero = jnp.zeros((shape.rows, LANES), jnp.float32)
    total = [[(zero, zero) for _ in range(3)] for _ in range(4)]
    ahead = [[tuple(v * high_sign for v in pair) for pair in spin] for spin in ahead]
    behind = [[tuple(v * low_sign for v in pair) for pair in spin] for spin in behind]
    add_rebuilt(total, ahead, TIME, -1.0)
    add_rebuilt(total, behind, TIME, 1.0)
    start = raw_field(shape, start_ref, mirrored)
    rest = jnp.zeros((shape.rows - shape.blocks, LANES), jnp.float32)
    field = []
    for s in range(4):
        from_low = (s < 2) != odd_step
        sign = scale if s < 2 else -scale
        colours = []
        for c in range(3):
            pair = []
            for p in range(2):
                index = (s * 3 + c) * 2 + p
                half_index = (s % 2 * 3 + c) * 2 + p
                if from_low:
                    hop = jnp.concatenate([low_ref[half_index] * low_mass, rest], axis=0)
                else:
                    hop = jnp.concatenate([rest, high_ref[half_index] * high_mass], axis=0)
                value = part_ref[index] - 0.5 * total[s][c][p] - hop
                pair.append(weight * start[s][c][p] + sign * value)
            colours.append(tuple(pair))
        field.append(colours)
    if last:
        (out_ref,) = out_refs
        for s in range(4):
            for c in range(3):
                for p in range(2):
                    for j in range(shape.slices):
                        out_ref[j, (s * 3 + c) * 2 + p] = field[s][c][p][j * shape.blocks : (j + 1) * shape.blocks]
        return
    field_ref, near_out, far_out, up_ref, down_ref = out_refs
    send_parts(shape, field, link, even, not odd_step, near_out, far_out, up_ref, down_ref)
    store_parts(field_ref, field)


def on_device(spinor, gauge_links):
    slices, _, depth, sites = spinor.shape
    assert depth == 1 and DEGREE % 2 == 0
    shape = Shape(slices, sites)
    rows, blocks = shape.rows, shape.blocks
    space_count = lax.axis_size("space")
    fifth_count = lax.axis_size("fifth")
    assert space_count % 2 == 0
    space_place = lax.axis_index("space")
    fifth_place = lax.axis_index("fifth")
    scalars = jnp.stack(
        [
            jnp.where(space_place == 0, -1.0, 1.0),
            jnp.where(space_place == space_count - 1, -1.0, 1.0),
            jnp.where(fifth_place == 0, -quark_mass, 1.0),
            jnp.where(fifth_place == fifth_count - 1, -quark_mass, 1.0),
            jnp.where(space_place % 2 == 0, 1.0, 0.0),
        ]
    ).astype(jnp.float32)
    near_pairs = [(i, i ^ 1) for i in range(space_count)]
    far_pairs = [(i, (i + (1 if i % 2 else -1)) % space_count) for i in range(space_count)]
    up_pairs = [(i, (i + 1) % fifth_count) for i in range(fifth_count)]
    down_pairs = [(i, (i - 1) % fifth_count) for i in range(fifth_count)]
    mirror_pairs = [(i, fifth_count - 1 - i) for i in range(fifth_count)]

    smem = pl.BlockSpec(memory_space=pltpu.SMEM)
    vmem = pl.BlockSpec(memory_space=pltpu.VMEM)

    def array(*dims):
        return jax.ShapeDtypeStruct(dims, jnp.float32)

    def call(body, out_shape, *operands, with_scalars):
        specs = ([smem] if with_scalars else []) + [vmem] * (len(operands) - with_scalars)
        return pl.pallas_call(
            body,
            out_shape=out_shape,
            in_specs=specs,
            out_specs=jax.tree.map(lambda _: vmem, out_shape),
        )(*operands)

    sends = (array(24, rows, LANES), array(12, rows, LANES), array(12, rows, LANES), array(12, blocks, LANES), array(12, blocks, LANES))
    weights = power_coefficients(DEGREE)

    start = spinor.reshape(slices, 24, blocks, LANES)
    links = gauge_links.reshape(4, 18, blocks, LANES)
    mirrored_start = lax.ppermute(start, "fifth", mirror_pairs)
    field, near, far, up, down = call(
        lambda *refs: first_kernel(shape, *refs), sends, scalars, start, links, with_scalars=1
    )
    wide = None
    for step in range(DEGREE):
        odd_step = step % 2 == 1
        far_in = lax.ppermute(far, "space", far_pairs)
        low_in = lax.ppermute(up, "fifth", up_pairs)
        high_in = lax.ppermute(down, "fifth", down_pairs)
        near_in = lax.ppermute(near, "space", near_pairs)
        if wide is None:
            wide = call(lambda *refs: widen_kernel(shape, *refs), array(72, rows, LANES), links, with_scalars=0)
        part = call(
            lambda *refs, odd_step=odd_step: space_kernel(shape, odd_step, *refs),
            array(24, rows, LANES), field, wide, with_scalars=0,
        )
        last = step == DEGREE - 1
        body = lambda *refs, odd_step=odd_step, step=step, last=last: close_kernel(
            shape, odd_step, weights[DEGREE] if step == 0 else 1.0, weights[DEGREE - 1 - step], not odd_step, last, *refs
        )
        result = call(
            body, array(slices, 24, blocks, LANES) if last else sends,
            scalars, part, wide, start if odd_step else mirrored_start, near_in, far_in, low_in, high_in,
            with_scalars=1,
        )
        if not last:
            field, near, far, up, down = result
    return result.reshape(slices, 24, depth, sites)


def solution(mesh):
    placed = (P("fifth", None, "space", None), P(None, None, "space", None))
    return jax.shard_map(
        on_device,
        mesh=mesh,
        in_specs=placed,
        out_specs=P("fifth", None, "space", None),
        check_vma=False,
    )
```

time: 107 us -> 48.4 us (0.45)
  waiting for transfers between devices: 32.9 us -> 1.47 us
  other arithmetic: 24.2 us -> 0 us
  Pallas kernels: 0 us -> 18.1 us
  starting transfers between devices: 38.5 us -> 22.9 us
  between operations: 4.61 us -> 0.11 us
  local copies, waits for them, and re-layouts: 6.62 us -> 5.47 us
    ppermute x24 -> x17, waiting for transfers between devices: 32.9 us -> 1.47 us  [the longest x4 0.8 us: on_device(): high_in = lax.ppermute(down, 'fifth', down_pairs)]
    pallas_call x0 -> x10, Pallas kernels: none -> 18.1 us  [call(): pl.pallas_call(body, out_shape=out_shape, in_specs=specs, out_specs=jax.t...]
    ppermute x24 -> x17, starting transfers between devices: 38.5 us -> 22.9 us  [the longest x4 7.97 us: on_device(): high_in = lax.ppermute(down, 'fifth', down_pairs)]
    another operation x117 -> x0, other arithmetic: 6.54 us -> none  [the longest x41 2.97 us: colour_mul(): return jnp.stack([result_re, result_im], axis=-3)]
    add x49 -> x0, other arithmetic: 6.51 us -> none  [the longest x20 2.7 us: colour_mul(): result_re = result_re + term_re]
    concatenate x84 -> x0, other arithmetic: 5.14 us -> none  [the longest x48 2.17 us: rebuild(): jnp.concatenate([half_spinor, jnp.stack(lower_part, axis=-5)], axis=-5)]
    unnamed x36 -> x34, local copies, waits for them, and re-layouts: 1.99 us -> 4.85 us
    select_n x15 -> x0, other arithmetic: 1.96 us -> none  [the longest x8 1.04 us: space_shift(): return jnp.where(position == 0, outside_roll, inside_roll)]
  transfers between devices with their start and end apart: 24 -> 17, of which waited for: 11 -> 6; matrix products, arithmetic and copies ran while one was open for 10% -> 1% of each run, Pallas kernels for 0% -> 22%
where the time goes in v1:
time: 48.4 us; the launch traced here: 48 us
  starting transfers between devices  22.9 us (47%)
  Pallas kernels  18.1 us (37%)
  local copies, waits for them, and re-layouts  5.47 us (11%)
  waiting for transfers between devices  1.47 us (3%)
    pallas_call x10, Pallas kernels, call(): pl.pallas_call(body, out_shape=out_shape, in_specs=specs, out_specs=jax.t...  18.1 us
    ppermute x4, starting transfers between devices, on_device(): high_in = lax.ppermute(down, 'fifth', down_pairs)  7.97 us
    ppermute x4, starting transfers between devices, on_device(): far_in = lax.ppermute(far, 'space', far_pairs)  7.25 us
    unnamed x34, local copies, waits for them, and re-layouts  4.85 us
    ppermute x1, starting transfers between devices, on_device(): mirrored_start = lax.ppermute(start, 'fifth', mirror_pairs)  3.92 us
    ppermute x4, starting transfers between devices, on_device(): low_in = lax.ppermute(up, 'fifth', up_pairs)  3.73 us
  transfers between devices with their start and end apart: 17, of which 6 were waited for; matrix products, arithmetic and copies ran while one was open for 1% of the time, Pallas kernels for 22%

profile of v1, /device:TPU:0, one launch (start us, length us, event | category | flops | bytes accessed | tf_op | source)
XLA Modules:
  0.0 48.0 jit_solution(16423460310142946459)
XLA Ops:
  0.0 3.9 %collective-permute-start = (f32[2,24,4,128]{3,2,1,0:T(4,128)}, f32[2,24,4,128]{3,2,1,0:T(4,128)S(1)}, u32[]{:S(2)}, u32[]{:S(2)}) collective-permute-start(f32[2,24,4,128]{3,2,1,0:T(4,128)} %bitcast.8), channel_id=1, source_target_pairs={{0,24},{8,16},{16,8},{24,0},{1,25},{9,17},{17,9},{25,1},{2,26},{10... | collective-permute-start | bytes 294920 | tf_op jit(solution)/shard_map/ppermute | solution.py:334
  3.9 0.6 %stack.23.refs_0_ = f32[5]{0:T(128)} concatenate(f32[1]{0:T(128)} %bitcast, f32[1]{0:T(128)} %bitcast.1, f32[1]{0:T(128)} %bitcast.2, f32[1]{0:T(128)} %bitcast.3, f32[1]{0:T(128)} %bitcast.4), dimensions={0} | concatenate | bytes 40 | tf_op jit(solution)/shard_map/stack | solution.py:299
  4.5 1.7 %shard_map.28 = (f32[24,8,128]{2,1,0:T(8,128)}, f32[12,8,128]{2,1,0:T(8,128)}, f32[12,8,128]{2,1,0:T(8,128)}, f32[12,4,128]{2,1,0:T(4,128)}, f32[12,4,128]{2,1,0:T(4,128)}) custom-call(f32[5]{0:T(128)} %stack.23.refs_0_, f32[2,24,4,128]{3,2,1,0:T(4,128)} %bitcast.9, f32[4,18,4,128]{3,2,1,0:T(4,128)} %bitcast.12), custom_call_target="tpu_custom_call" | custom-call | tf_op jit(solution)/shard_map/pallas_call | solution.py:322
  6.2 0.0 collective-permute-start.1
  6.2 3.7 %collective-permute-start.2 = (f32[12,8,128]{2,1,0:T(8,128)}, f32[12,8,128]{2,1,0:T(8,128)S(1)}, u32[]{:S(2)}, u32[]{:S(2)}) collective-permute-start(f32[12,8,128]{2,1,0:T(8,128)} %get-tuple-element.27), channel_id=1, source_target_pairs={{0,7},{1,2},{2,1},{3,4},{4,3},{5,6},{6,5},{7,0},{8,15},{9,10},{10,... | collective-permute-start | bytes 147464 | tf_op jit(solution)/shard_map/ppermute | solution.py:341
  9.9 0.5 %collective-permute-start.3 = (f32[12,4,128]{2,1,0:T(4,128)}, f32[12,4,128]{2,1,0:T(4,128)S(1)}, u32[]{:S(2)}, u32[]{:S(2)}) collective-permute-start(f32[12,4,128]{2,1,0:T(4,128)} %get-tuple-element.28), channel_id=1, source_target_pairs={{0,8},{8,16},{16,24},{24,0},{1,9},{9,17},{17,25},{25,1},{2,10},{10... | collective-permute-start | bytes 73736 | tf_op jit(solution)/shard_map/ppermute | solution.py:342
  10.5 2.4 %collective-permute-start.4 = (f32[12,4,128]{2,1,0:T(4,128)}, f32[12,4,128]{2,1,0:T(4,128)S(1)}, u32[]{:S(2)}, u32[]{:S(2)}) collective-permute-start(f32[12,4,128]{2,1,0:T(4,128)} %get-tuple-element.29), channel_id=1, source_target_pairs={{0,24},{8,0},{16,8},{24,16},{1,25},{9,1},{17,9},{25,17},{2,26},{10... | collective-permute-start | bytes 73736 | tf_op jit(solution)/shard_map/ppermute | solution.py:343
  12.8 1.6 %shard_map.29.refs_1_.refs_2_ = f32[72,8,128]{2,1,0:T(8,128)} custom-call(f32[4,18,4,128]{3,2,1,0:T(4,128)} %bitcast.13), custom_call_target="tpu_custom_call" | custom-call | tf_op jit(solution)/shard_map/pallas_call | solution.py:322
  14.5 1.9 %shard_map.30.refs_1_ = f32[24,8,128]{2,1,0:T(8,128)} custom-call(f32[24,8,128]{2,1,0:T(8,128)} %get-tuple-element.25.refs_0_, f32[72,8,128]{2,1,0:T(8,128)} %shard_map.29.refs_1_.refs_2_), custom_call_target="tpu_custom_call" | custom-call | tf_op jit(solution)/shard_map/pallas_call | solution.py:322
  16.4 0.0 collective-permute-done.3.refs_6_
  16.4 0.0 collective-permute-done.4.refs_7_
  16.4 0.0 copy-start.10
  16.4 0.0 collective-permute-done.1.refs_4_
  16.4 0.0 copy-start.1
  16.4 0.0 collective-permute-done.2.refs_5_
  16.4 0.0 collective-permute-done.refs_3_
  16.4 0.5 %copy-done.9 = f32[12,4,128]{2,1,0:T(4,128)} copy-done((f32[12,4,128]{2,1,0:T(4,128)}, f32[12,4,128]{2,1,0:T(4,128)S(1)}, u32[]{:S(2)}) %copy-start.9) | copy-done | bytes 24600
  17.0 0.0 copy-done.10
  17.0 0.0 copy-done.1
  17.0 0.0 copy-done.2
  17.0 0.6 %copy-done = f32[2,24,4,128]{3,2,1,0:T(4,128)} copy-done((f32[2,24,4,128]{3,2,1,0:T(4,128)}, f32[2,24,4,128]{3,2,1,0:T(4,128)S(1)}, u32[]{:S(2)}) %copy-start) | copy-done | bytes 98328
  17.7 1.9 %shard_map.31 = (f32[24,8,128]{2,1,0:T(8,128)}, f32[12,8,128]{2,1,0:T(8,128)}, f32[12,8,128]{2,1,0:T(8,128)}, f32[12,4,128]{2,1,0:T(4,128)}, f32[12,4,128]{2,1,0:T(4,128)}) custom-call(f32[5]{0:T(128)} %stack.23.refs_0_, f32[24,8,128]{2,1,0:T(8,128)} %shard_map.30.refs_1_, f32[72,8,128]{2,1,0:T(8,128)} %shard_map.29.refs_1_.refs_2_, ...), custom_call_target="tpu_custom_call" | custom-call | tf_op jit(solution)/shard_map/pallas_call | solution.py:322
  19.5 0.0 collective-permute-start.5
  19.5 0.6 %collective-permute-start.6 = (f32[12,8,128]{2,1,0:T(8,128)}, f32[12,8,128]{2,1,0:T(8,128)S(1)}, u32[]{:S(2)}, u32[]{:S(2)}) collective-permute-start(f32[12,8,128]{2,1,0:T(8,128)} %get-tuple-element.32), channel_id=1, source_target_pairs={{0,7},{1,2},{2,1},{3,4},{4,3},{5,6},{6,5},{7,0},{8,15},{9,10},{10,... | collective-permute-start | bytes 147464 | tf_op jit(solution)/shard_map/ppermute | solution.py:341
  20.1 0.4 collective-permute-start.7
  20.5 2.5 %collective-permute-start.8 = (f32[12,4,128]{2,1,0:T(4,128)}, f32[12,4,128]{2,1,0:T(4,128)S(1)}, u32[]{:S(2)}, u32[]{:S(2)}) collective-permute-start(f32[12,4,128]{2,1,0:T(4,128)} %get-tuple-element.34), channel_id=1, source_target_pairs={{0,24},{8,0},{16,8},{24,16},{1,25},{9,1},{17,9},{25,17},{2,26},{10... | collective-permute-start | bytes 73736 | tf_op jit(solution)/shard_map/ppermute | solution.py:343
  23.0 1.9 %shard_map.32.refs_1_ = f32[24,8,128]{2,1,0:T(8,128)} custom-call(f32[24,8,128]{2,1,0:T(8,128)} %get-tuple-element.30.refs_0_, f32[72,8,128]{2,1,0:T(8,128)} %shard_map.29.refs_1_.refs_2_), custom_call_target="tpu_custom_call" | custom-call | tf_op jit(solution)/shard_map/pallas_call | solution.py:322
  24.9 0.1 collective-permute-done.7.refs_6_
  25.0 0.0 collective-permute-done.8.refs_7_
  25.0 0.0 collective-permute-done.5.refs_4_
  25.0 0.1 collective-permute-done.6.refs_5_
  25.1 0.5 %copy-done.12 = f32[12,4,128]{2,1,0:T(4,128)} copy-done((f32[12,4,128]{2,1,0:T(4,128)}, f32[12,4,128]{2,1,0:T(4,128)S(1)}, u32[]{:S(2)}) %copy-start.12) | copy-done | bytes 24600
  25.6 0.0 copy-done.14
  25.6 0.0 copy-done.4
  25.7 0.6 %copy-done.6 = f32[12,8,128]{2,1,0:T(8,128)} copy-done((f32[12,8,128]{2,1,0:T(8,128)}, f32[12,8,128]{2,1,0:T(8,128)S(1)}, u32[]{:S(2)}) %copy-start.6) | copy-done | bytes 49176
  26.3 1.9 %shard_map.33 = (f32[24,8,128]{2,1,0:T(8,128)}, f32[12,8,128]{2,1,0:T(8,128)}, f32[12,8,128]{2,1,0:T(8,128)}, f32[12,4,128]{2,1,0:T(4,128)}, f32[12,4,128]{2,1,0:T(4,128)}) custom-call(f32[5]{0:T(128)} %stack.23.refs_0_, f32[24,8,128]{2,1,0:T(8,128)} %shard_map.32.refs_1_, f32[72,8,128]{2,1,0:T(8,128)} %shard_map.29.refs_1_.refs_2_, ...), custom_call_target="tpu_custom_call" | custom-call | tf_op jit(solution)/shard_map/pallas_call | solution.py:322
  28.1 0.0 collective-permute-start.9
  28.1 2.4 %collective-permute-start.10 = (f32[12,8,128]{2,1,0:T(8,128)}, f32[12,8,128]{2,1,0:T(8,128)S(1)}, u32[]{:S(2)}, u32[]{:S(2)}) collective-permute-start(f32[12,8,128]{2,1,0:T(8,128)} %get-tuple-element.37), channel_id=1, source_target_pairs={{0,7},{1,2},{2,1},{3,4},{4,3},{5,6},{6,5},{7,0},{8,15},{9,10},{10,... | collective-permute-start | bytes 147464 | tf_op jit(solution)/shard_map/ppermute | solution.py:341
  30.5 1.2 %collective-permute-start.11 = (f32[12,4,128]{2,1,0:T(4,128)}, f32[12,4,128]{2,1,0:T(4,128)S(1)}, u32[]{:S(2)}, u32[]{:S(2)}) collective-permute-start(f32[12,4,128]{2,1,0:T(4,128)} %get-tuple-element.38), channel_id=1, source_target_pairs={{0,8},{8,16},{16,24},{24,0},{1,9},{9,17},{17,25},{25,1},{2,10},{10... | collective-permute-start | bytes 73736 | tf_op jit(solution)/shard_map/ppermute | solution.py:342
  31.8 1.7 %collective-permute-start.12 = (f32[12,4,128]{2,1,0:T(4,128)}, f32[12,4,128]{2,1,0:T(4,128)S(1)}, u32[]{:S(2)}, u32[]{:S(2)}) collective-permute-start(f32[12,4,128]{2,1,0:T(4,128)} %get-tuple-element.39), channel_id=1, source_target_pairs={{0,24},{8,0},{16,8},{24,16},{1,25},{9,1},{17,9},{25,17},{2,26},{10... | collective-permute-start | bytes 73736 | tf_op jit(solution)/shard_map/ppermute | solution.py:343
  33.5 1.9 %shard_map.34.refs_1_ = f32[24,8,128]{2,1,0:T(8,128)} custom-call(f32[24,8,128]{2,1,0:T(8,128)} %get-tuple-element.35.refs_0_, f32[72,8,128]{2,1,0:T(8,128)} %shard_map.29.refs_1_.refs_2_), custom_call_target="tpu_custom_call" | custom-call | tf_op jit(solution)/shard_map/pallas_call | solution.py:322
  35.3 0.3 collective-permute-done.11.refs_6_
  35.6 0.2 collective-permute-done.12.refs_7_
  35.8 0.0 collective-permute-done.9.refs_4_
  35.8 0.0 collective-permute-done.10.refs_5_
  35.8 0.4 copy-done.11
  36.2 0.2 copy-done.13
  36.4 0.0 copy-done.3
  36.4 0.6 %copy-done.5 = f32[12,8,128]{2,1,0:T(8,128)} copy-done((f32[12,8,128]{2,1,0:T(8,128)}, f32[12,8,128]{2,1,0:T(8,128)S(1)}, u32[]{:S(2)}) %copy-start.5) | copy-done | bytes 49176
  37.0 1.8 %shard_map.35 = (f32[24,8,128]{2,1,0:T(8,128)}, f32[12,8,128]{2,1,0:T(8,128)}, f32[12,8,128]{2,1,0:T(8,128)}, f32[12,4,128]{2,1,0:T(4,128)}, f32[12,4,128]{2,1,0:T(4,128)}) custom-call(f32[5]{0:T(128)} %stack.23.refs_0_, f32[24,8,128]{2,1,0:T(8,128)} %shard_map.34.refs_1_, f32[72,8,128]{2,1,0:T(8,128)} %shard_map.29.refs_1_.refs_2_, ...), custom_call_target="tpu_custom_call" | custom-call | tf_op jit(solution)/shard_map/pallas_call | solution.py:322
  38.9 0.0 collective-permute-start.13
  38.9 0.6 %collective-permute-start.14 = (f32[12,8,128]{2,1,0:T(8,128)}, f32[12,8,128]{2,1,0:T(8,128)S(1)}, u32[]{:S(2)}, u32[]{:S(2)}) collective-permute-start(f32[12,8,128]{2,1,0:T(8,128)} %get-tuple-element.42), channel_id=1, source_target_pairs={{0,7},{1,2},{2,1},{3,4},{4,3},{5,6},{6,5},{7,0},{8,15},{9,10},{10,... | collective-permute-start | bytes 147464 | tf_op jit(solution)/shard_map/ppermute | solution.py:341
  39.5 1.5 %collective-permute-start.15 = (f32[12,4,128]{2,1,0:T(4,128)}, f32[12,4,128]{2,1,0:T(4,128)S(1)}, u32[]{:S(2)}, u32[]{:S(2)}) collective-permute-start(f32[12,4,128]{2,1,0:T(4,128)} %get-tuple-element.43), channel_id=1, source_target_pairs={{0,8},{8,16},{16,24},{24,0},{1,9},{9,17},{17,25},{25,1},{2,10},{10... | collective-permute-start | bytes 73736 | tf_op jit(solution)/shard_map/ppermute | solution.py:342
  41.0 1.4 %collective-permute-start.16 = (f32[12,4,128]{2,1,0:T(4,128)}, f32[12,4,128]{2,1,0:T(4,128)S(1)}, u32[]{:S(2)}, u32[]{:S(2)}) collective-permute-start(f32[12,4,128]{2,1,0:T(4,128)} %get-tuple-element.44), channel_id=1, source_target_pairs={{0,24},{8,0},{16,8},{24,16},{1,25},{9,1},{17,9},{25,17},{2,26},{10... | collective-permute-start | bytes 73736 | tf_op jit(solution)/shard_map/ppermute | solution.py:343
  42.4 1.9 %shard_map.36.refs_1_ = f32[24,8,128]{2,1,0:T(8,128)} custom-call(f32[24,8,128]{2,1,0:T(8,128)} %get-tuple-element.40.refs_0_, f32[72,8,128]{2,1,0:T(8,128)} %shard_map.29.refs_1_.refs_2_), custom_call_target="tpu_custom_call" | custom-call | tf_op jit(solution)/shard_map/pallas_call | solution.py:322
  44.2 0.1 collective-permute-done.15.refs_6_
  44.4 0.6 %collective-permute-done.16.refs_7_ = f32[12,4,128]{2,1,0:T(4,128)S(1)} collective-permute-done((f32[12,4,128]{2,1,0:T(4,128)}, f32[12,4,128]{2,1,0:T(4,128)S(1)}, u32[]{:S(2)}, u32[]{:S(2)}) %collective-permute-start.16) | collective-permute-done | bytes 24608 | tf_op jit(solution)/shard_map/ppermute | solution.py:343
  45.0 0.0 collective-permute-done.13.refs_4_
  45.0 0.0 collective-permute-done.14.refs_5_
  45.0 0.0 copy-done.15
  45.0 0.6 %copy-done.16 = f32[12,4,128]{2,1,0:T(4,128)} copy-done((f32[12,4,128]{2,1,0:T(4,128)}, f32[12,4,128]{2,1,0:T(4,128)S(1)}, u32[]{:S(2)}) %copy-start.16) | copy-done | bytes 24600
  45.6 0.0 copy-done.7
  45.6 0.6 %copy-done.8 = f32[12,8,128]{2,1,0:T(8,128)} copy-done((f32[12,8,128]{2,1,0:T(8,128)}, f32[12,8,128]{2,1,0:T(8,128)S(1)}, u32[]{:S(2)}) %copy-start.8) | copy-done | bytes 49176
  46.3 1.8 %shard_map.37 = f32[2,24,4,128]{3,2,1,0:T(4,128)} custom-call(f32[5]{0:T(128)} %stack.23.refs_0_, f32[24,8,128]{2,1,0:T(8,128)} %shard_map.36.refs_1_, f32[72,8,128]{2,1,0:T(8,128)} %shard_map.29.refs_1_.refs_2_, f32[2,24,4,128]{3,2,1,0:T(4,128)} %bitcast.11, f32[12,8,128]{2,1,0:T(8,128)} %copy-done.7, f32[12,8,128]{2,1,0:T(8,128)} %copy-done.8, ...), custom_call_target="tpu_custom_call" | custom-call | tf_op jit(solution)/shard_map/pallas_call | solution.py:322
  (15 shorter events, 0.0 us)
Async XLA Ops:
  0.0 16.4 %collective-permute-start = (f32[2,24,4,128]{3,2,1,0:T(4,128)}, f32[2,24,4,128]{3,2,1,0:T(4,128)S(1)}, u32[]{:S(2)}, u32[]{:S(2)}) collective-permute-start(f32[2,24,4,128]{3,2,1,0:T(4,128)} %bitcast.8), channel_id=1, source_target_pairs={{0,24},{8,16},{16,8},{24,0},{1,25},{9,17},{17,9},{25,1},{2,26},{10... | collective-permute-start | bytes 294920 | tf_op jit(solution)/shard_map/ppermute | solution.py:334
  6.2 10.2 %collective-permute-start.1 = (f32[12,8,128]{2,1,0:T(8,128)}, f32[12,8,128]{2,1,0:T(8,128)S(1)}, u32[]{:S(2)}, u32[]{:S(2)}) collective-permute-start(f32[12,8,128]{2,1,0:T(8,128)} %get-tuple-element.26), channel_id=1, source_target_pairs={{0,1},{1,0},{2,3},{3,2},{4,5},{5,4},{6,7},{7,6},{8,9},{9,8},{10,11... | collective-permute-start | bytes 147464 | tf_op jit(solution)/shard_map/ppermute | solution.py:344
  6.2 10.2 %collective-permute-start.2 = (f32[12,8,128]{2,1,0:T(8,128)}, f32[12,8,128]{2,1,0:T(8,128)S(1)}, u32[]{:S(2)}, u32[]{:S(2)}) collective-permute-start(f32[12,8,128]{2,1,0:T(8,128)} %get-tuple-element.27), channel_id=1, source_target_pairs={{0,7},{1,2},{2,1},{3,4},{4,3},{5,6},{6,5},{7,0},{8,15},{9,10},{10,... | collective-permute-start | bytes 147464 | tf_op jit(solution)/shard_map/ppermute | solution.py:341
  9.9 6.4 %collective-permute-start.3 = (f32[12,4,128]{2,1,0:T(4,128)}, f32[12,4,128]{2,1,0:T(4,128)S(1)}, u32[]{:S(2)}, u32[]{:S(2)}) collective-permute-start(f32[12,4,128]{2,1,0:T(4,128)} %get-tuple-element.28), channel_id=1, source_target_pairs={{0,8},{8,16},{16,24},{24,0},{1,9},{9,17},{17,25},{25,1},{2,10},{10... | collective-permute-start | bytes 73736 | tf_op jit(solution)/shard_map/ppermute | solution.py:342
  10.5 5.9 %collective-permute-start.4 = (f32[12,4,128]{2,1,0:T(4,128)}, f32[12,4,128]{2,1,0:T(4,128)S(1)}, u32[]{:S(2)}, u32[]{:S(2)}) collective-permute-start(f32[12,4,128]{2,1,0:T(4,128)} %get-tuple-element.29), channel_id=1, source_target_pairs={{0,24},{8,0},{16,8},{24,16},{1,25},{9,1},{17,9},{25,17},{2,26},{10... | collective-permute-start | bytes 73736 | tf_op jit(solution)/shard_map/ppermute | solution.py:343
  16.4 0.6 %copy-start.9 = (f32[12,4,128]{2,1,0:T(4,128)}, f32[12,4,128]{2,1,0:T(4,128)S(1)}, u32[]{:S(2)}) copy-start(f32[12,4,128]{2,1,0:T(4,128)S(1)} %collective-permute-done.3.refs_6_) | copy-start | bytes 73732
  16.4 0.6 %copy-start.10 = (f32[12,4,128]{2,1,0:T(4,128)}, f32[12,4,128]{2,1,0:T(4,128)S(1)}, u32[]{:S(2)}) copy-start(f32[12,4,128]{2,1,0:T(4,128)S(1)} %collective-permute-done.4.refs_7_) | copy-start | bytes 73732
  16.4 0.6 %copy-start.1 = (f32[12,8,128]{2,1,0:T(8,128)}, f32[12,8,128]{2,1,0:T(8,128)S(1)}, u32[]{:S(2)}) copy-start(f32[12,8,128]{2,1,0:T(8,128)S(1)} %collective-permute-done.1.refs_4_) | copy-start | bytes 147460
  16.4 0.6 %copy-start.2 = (f32[12,8,128]{2,1,0:T(8,128)}, f32[12,8,128]{2,1,0:T(8,128)S(1)}, u32[]{:S(2)}) copy-start(f32[12,8,128]{2,1,0:T(8,128)S(1)} %collective-permute-done.2.refs_5_) | copy-start | bytes 147460
  17.0 0.6 %copy-start = (f32[2,24,4,128]{3,2,1,0:T(4,128)}, f32[2,24,4,128]{3,2,1,0:T(4,128)S(1)}, u32[]{:S(2)}) copy-start(f32[2,24,4,128]{3,2,1,0:T(4,128)S(1)} %collective-permute-done.refs_3_) | copy-start | bytes 294916
  19.5 5.5 %collective-permute-start.5 = (f32[12,8,128]{2,1,0:T(8,128)}, f32[12,8,128]{2,1,0:T(8,128)S(1)}, u32[]{:S(2)}, u32[]{:S(2)}) collective-permute-start(f32[12,8,128]{2,1,0:T(8,128)} %get-tuple-element.31), channel_id=1, source_target_pairs={{0,1},{1,0},{2,3},{3,2},{4,5},{5,4},{6,7},{7,6},{8,9},{9,8},{10,11... | collective-permute-start | bytes 147464 | tf_op jit(solution)/shard_map/ppermute | solution.py:344
  19.5 5.6 %collective-permute-start.6 = (f32[12,8,128]{2,1,0:T(8,128)}, f32[12,8,128]{2,1,0:T(8,128)S(1)}, u32[]{:S(2)}, u32[]{:S(2)}) collective-permute-start(f32[12,8,128]{2,1,0:T(8,128)} %get-tuple-element.32), channel_id=1, source_target_pairs={{0,7},{1,2},{2,1},{3,4},{4,3},{5,6},{6,5},{7,0},{8,15},{9,10},{10,... | collective-permute-start | bytes 147464 | tf_op jit(solution)/shard_map/ppermute | solution.py:341
  20.1 4.9 %collective-permute-start.7 = (f32[12,4,128]{2,1,0:T(4,128)}, f32[12,4,128]{2,1,0:T(4,128)S(1)}, u32[]{:S(2)}, u32[]{:S(2)}) collective-permute-start(f32[12,4,128]{2,1,0:T(4,128)} %get-tuple-element.33), channel_id=1, source_target_pairs={{0,8},{8,16},{16,24},{24,0},{1,9},{9,17},{17,25},{25,1},{2,10},{10... | collective-permute-start | bytes 73736 | tf_op jit(solution)/shard_map/ppermute | solution.py:342
  20.5 4.5 %collective-permute-start.8 = (f32[12,4,128]{2,1,0:T(4,128)}, f32[12,4,128]{2,1,0:T(4,128)S(1)}, u32[]{:S(2)}, u32[]{:S(2)}) collective-permute-start(f32[12,4,128]{2,1,0:T(4,128)} %get-tuple-element.34), channel_id=1, source_target_pairs={{0,24},{8,0},{16,8},{24,16},{1,25},{9,1},{17,9},{25,17},{2,26},{10... | collective-permute-start | bytes 73736 | tf_op jit(solution)/shard_map/ppermute | solution.py:343
  25.0 0.6 %copy-start.12 = (f32[12,4,128]{2,1,0:T(4,128)}, f32[12,4,128]{2,1,0:T(4,128)S(1)}, u32[]{:S(2)}) copy-start(f32[12,4,128]{2,1,0:T(4,128)S(1)} %collective-permute-done.7.refs_6_) | copy-start | bytes 73732
  25.0 0.6 %copy-start.14 = (f32[12,4,128]{2,1,0:T(4,128)}, f32[12,4,128]{2,1,0:T(4,128)S(1)}, u32[]{:S(2)}) copy-start(f32[12,4,128]{2,1,0:T(4,128)S(1)} %collective-permute-done.8.refs_7_) | copy-start | bytes 73732
  25.0 0.6 %copy-start.4 = (f32[12,8,128]{2,1,0:T(8,128)}, f32[12,8,128]{2,1,0:T(8,128)S(1)}, u32[]{:S(2)}) copy-start(f32[12,8,128]{2,1,0:T(8,128)S(1)} %collective-permute-done.5.refs_4_) | copy-start | bytes 147460
  25.7 0.6 %copy-start.6 = (f32[12,8,128]{2,1,0:T(8,128)}, f32[12,8,128]{2,1,0:T(8,128)S(1)}, u32[]{:S(2)}) copy-start(f32[12,8,128]{2,1,0:T(8,128)S(1)} %collective-permute-done.6.refs_5_) | copy-start | bytes 147460
  28.1 7.7 %collective-permute-start.9 = (f32[12,8,128]{2,1,0:T(8,128)}, f32[12,8,128]{2,1,0:T(8,128)S(1)}, u32[]{:S(2)}, u32[]{:S(2)}) collective-permute-start(f32[12,8,128]{2,1,0:T(8,128)} %get-tuple-element.36), channel_id=1, source_target_pairs={{0,1},{1,0},{2,3},{3,2},{4,5},{5,4},{6,7},{7,6},{8,9},{9,8},{10,11... | collective-permute-start | bytes 147464 | tf_op jit(solution)/shard_map/ppermute | solution.py:344
  28.1 7.7 %collective-permute-start.10 = (f32[12,8,128]{2,1,0:T(8,128)}, f32[12,8,128]{2,1,0:T(8,128)S(1)}, u32[]{:S(2)}, u32[]{:S(2)}) collective-permute-start(f32[12,8,128]{2,1,0:T(8,128)} %get-tuple-element.37), channel_id=1, source_target_pairs={{0,7},{1,2},{2,1},{3,4},{4,3},{5,6},{6,5},{7,0},{8,15},{9,10},{10,... | collective-permute-start | bytes 147464 | tf_op jit(solution)/shard_map/ppermute | solution.py:341
  30.5 5.1 %collective-permute-start.11 = (f32[12,4,128]{2,1,0:T(4,128)}, f32[12,4,128]{2,1,0:T(4,128)S(1)}, u32[]{:S(2)}, u32[]{:S(2)}) collective-permute-start(f32[12,4,128]{2,1,0:T(4,128)} %get-tuple-element.38), channel_id=1, source_target_pairs={{0,8},{8,16},{16,24},{24,0},{1,9},{9,17},{17,25},{25,1},{2,10},{10... | collective-permute-start | bytes 73736 | tf_op jit(solution)/shard_map/ppermute | solution.py:342
  31.8 4.0 %collective-permute-start.12 = (f32[12,4,128]{2,1,0:T(4,128)}, f32[12,4,128]{2,1,0:T(4,128)S(1)}, u32[]{:S(2)}, u32[]{:S(2)}) collective-permute-start(f32[12,4,128]{2,1,0:T(4,128)} %get-tuple-element.39), channel_id=1, source_target_pairs={{0,24},{8,0},{16,8},{24,16},{1,25},{9,1},{17,9},{25,17},{2,26},{10... | collective-permute-start | bytes 73736 | tf_op jit(solution)/shard_map/ppermute | solution.py:343
  35.6 0.6 %copy-start.11 = (f32[12,4,128]{2,1,0:T(4,128)}, f32[12,4,128]{2,1,0:T(4,128)S(1)}, u32[]{:S(2)}) copy-start(f32[12,4,128]{2,1,0:T(4,128)S(1)} %collective-permute-done.11.refs_6_) | copy-start | bytes 73732
  35.8 0.6 %copy-start.13 = (f32[12,4,128]{2,1,0:T(4,128)}, f32[12,4,128]{2,1,0:T(4,128)S(1)}, u32[]{:S(2)}) copy-start(f32[12,4,128]{2,1,0:T(4,128)S(1)} %collective-permute-done.12.refs_7_) | copy-start | bytes 73732
  35.8 0.6 %copy-start.3 = (f32[12,8,128]{2,1,0:T(8,128)}, f32[12,8,128]{2,1,0:T(8,128)S(1)}, u32[]{:S(2)}) copy-start(f32[12,8,128]{2,1,0:T(8,128)S(1)} %collective-permute-done.9.refs_4_) | copy-start | bytes 147460
  36.4 0.6 %copy-start.5 = (f32[12,8,128]{2,1,0:T(8,128)}, f32[12,8,128]{2,1,0:T(8,128)S(1)}, u32[]{:S(2)}) copy-start(f32[12,8,128]{2,1,0:T(8,128)S(1)} %collective-permute-done.10.refs_5_) | copy-start | bytes 147460
  38.9 6.1 %collective-permute-start.13 = (f32[12,8,128]{2,1,0:T(8,128)}, f32[12,8,128]{2,1,0:T(8,128)S(1)}, u32[]{:S(2)}, u32[]{:S(2)}) collective-permute-start(f32[12,8,128]{2,1,0:T(8,128)} %get-tuple-element.41), channel_id=1, source_target_pairs={{0,1},{1,0},{2,3},{3,2},{4,5},{5,4},{6,7},{7,6},{8,9},{9,8},{10,11... | collective-permute-start | bytes 147464 | tf_op jit(solution)/shard_map/ppermute | solution.py:344
  38.9 6.1 %collective-permute-start.14 = (f32[12,8,128]{2,1,0:T(8,128)}, f32[12,8,128]{2,1,0:T(8,128)S(1)}, u32[]{:S(2)}, u32[]{:S(2)}) collective-permute-start(f32[12,8,128]{2,1,0:T(8,128)} %get-tuple-element.42), channel_id=1, source_target_pairs={{0,7},{1,2},{2,1},{3,4},{4,3},{5,6},{6,5},{7,0},{8,15},{9,10},{10,... | collective-permute-start | bytes 147464 | tf_op jit(solution)/shard_map/ppermute | solution.py:341
  39.5 4.9 %collective-permute-start.15 = (f32[12,4,128]{2,1,0:T(4,128)}, f32[12,4,128]{2,1,0:T(4,128)S(1)}, u32[]{:S(2)}, u32[]{:S(2)}) collective-permute-start(f32[12,4,128]{2,1,0:T(4,128)} %get-tuple-element.43), channel_id=1, source_target_pairs={{0,8},{8,16},{16,24},{24,0},{1,9},{9,17},{17,25},{25,1},{2,10},{10... | collective-permute-start | bytes 73736 | tf_op jit(solution)/shard_map/ppermute | solution.py:342
  41.0 4.0 %collective-permute-start.16 = (f32[12,4,128]{2,1,0:T(4,128)}, f32[12,4,128]{2,1,0:T(4,128)S(1)}, u32[]{:S(2)}, u32[]{:S(2)}) collective-permute-start(f32[12,4,128]{2,1,0:T(4,128)} %get-tuple-element.44), channel_id=1, source_target_pairs={{0,24},{8,0},{16,8},{24,16},{1,25},{9,1},{17,9},{25,17},{2,26},{10... | collective-permute-start | bytes 73736 | tf_op jit(solution)/shard_map/ppermute | solution.py:343
  44.4 0.7 %copy-start.15 = (f32[12,4,128]{2,1,0:T(4,128)}, f32[12,4,128]{2,1,0:T(4,128)S(1)}, u32[]{:S(2)}) copy-start(f32[12,4,128]{2,1,0:T(4,128)S(1)} %collective-permute-done.15.refs_6_) | copy-start | bytes 73732
  45.0 0.6 %copy-start.16 = (f32[12,4,128]{2,1,0:T(4,128)}, f32[12,4,128]{2,1,0:T(4,128)S(1)}, u32[]{:S(2)}) copy-start(f32[12,4,128]{2,1,0:T(4,128)S(1)} %collective-permute-done.16.refs_7_) | copy-start | bytes 73732
  45.0 0.6 %copy-start.7 = (f32[12,8,128]{2,1,0:T(8,128)}, f32[12,8,128]{2,1,0:T(8,128)S(1)}, u32[]{:S(2)}) copy-start(f32[12,8,128]{2,1,0:T(8,128)S(1)} %collective-permute-done.13.refs_4_) | copy-start | bytes 147460
  45.6 0.6 %copy-start.8 = (f32[12,8,128]{2,1,0:T(8,128)}, f32[12,8,128]{2,1,0:T(8,128)S(1)}, u32[]{:S(2)}) copy-start(f32[12,8,128]{2,1,0:T(8,128)S(1)} %collective-permute-done.14.refs_5_) | copy-start | bytes 147460

commit v2 on v1

--- a/solution.py
+++ b/solution.py
@@ -8,6 +8,7 @@
 
 DEGREE = 4
 LANES = 128
+VMEM_GRANT = 8 * 2**20
 
 wall_height = 1.8
 quark_mass = 0.1
@@ -169,6 +170,17 @@
     ]
 
 
+class Place:
+    def __init__(self):
+        space, fifth = lax.axis_index("space"), lax.axis_index("fifth")
+        last_space, last_fifth = lax.axis_size("space") - 1, lax.axis_size("fifth") - 1
+        self.even = space % 2 == 0
+        self.low_sign = jnp.where(space == 0, -1.0, 1.0)
+        self.high_sign = jnp.where(space == last_space, -1.0, 1.0)
+        self.low_mass = jnp.where(fifth == 0, -quark_mass, 1.0)
+        self.high_mass = jnp.where(fifth == last_fifth, -quark_mass, 1.0)
+
+
 def send_parts(shape, field, link, even, odd_step, near_ref, far_ref, up_ref, down_ref):
     ahead = project(field, TIME, -1.0)
     behind = colour_mul(link, project(field, TIME, 1.0), True)
@@ -188,8 +200,8 @@
             wide_ref[mu * 18 + index] = jnp.concatenate([value] * shape.slices, axis=0)
 
 
-def first_kernel(shape, scalar_ref, spinor_ref, links_ref, field_ref, near_ref, far_ref, up_ref, down_ref):
-    even = scalar_ref[4] > 0.5
+def first_kernel(shape, spinor_ref, links_ref, field_ref, near_ref, far_ref, up_ref, down_ref):
+    even = Place().even
     field = raw_field(shape, spinor_ref, False)
     store_parts(field_ref, field)
 
@@ -237,20 +249,19 @@
 
 
 def close_kernel(
-    shape, odd_step, scale, weight, mirrored, last, scalar_ref, part_ref, wide_ref, start_ref, near_ref, far_ref,
+    shape, odd_step, scale, weight, mirrored, last, part_ref, wide_ref, start_ref, near_ref, far_ref,
     low_ref, high_ref, *out_refs
 ):
-    even = scalar_ref[4] > 0.5
-    low_sign, high_sign = scalar_ref[0], scalar_ref[1]
-    low_mass, high_mass = scalar_ref[2], scalar_ref[3]
+    place = Place()
+    even = place.even
     link = load_link(wide_ref, TIME)
     near, far = load_half(near_ref), load_half(far_ref)
     ahead = colour_mul(link, pick(even, near, far), False)
     behind = pick(even, far, near)
     zero = jnp.zeros((shape.rows, LANES), jnp.float32)
     total = [[(zero, zero) for _ in range(3)] for _ in range(4)]
-    ahead = [[tuple(v * high_sign for v in pair) for pair in spin] for spin in ahead]
-    behind = [[tuple(v * low_sign for v in pair) for pair in spin] for spin in behind]
+    ahead = [[tuple(v * place.high_sign for v in pair) for pair in spin] for spin in ahead]
+    behind = [[tuple(v * place.low_sign for v in pair) for pair in spin] for spin in behind]
     add_rebuilt(total, ahead, TIME, -1.0)
     add_rebuilt(total, behind, TIME, 1.0)
     start = raw_field(shape, start_ref, mirrored)
@@ -266,9 +277,9 @@
                 index = (s * 3 + c) * 2 + p
                 half_index = (s % 2 * 3 + c) * 2 + p
                 if from_low:
-                    hop = jnp.concatenate([low_ref[half_index] * low_mass, rest], axis=0)
+                    hop = jnp.concatenate([low_ref[half_index] * place.low_mass, rest], axis=0)
                 else:
-                    hop = jnp.concatenate([rest, high_ref[half_index] * high_mass], axis=0)
+                    hop = jnp.concatenate([rest, high_ref[half_index] * place.high_mass], axis=0)
                 value = part_ref[index] - 0.5 * total[s][c][p] - hop
                 pair.append(weight * start[s][c][p] + sign * value)
             colours.append(tuple(pair))
@@ -294,36 +305,24 @@
     space_count = lax.axis_size("space")
     fifth_count = lax.axis_size("fifth")
     assert space_count % 2 == 0
-    space_place = lax.axis_index("space")
-    fifth_place = lax.axis_index("fifth")
-    scalars = jnp.stack(
-        [
-            jnp.where(space_place == 0, -1.0, 1.0),
-            jnp.where(space_place == space_count - 1, -1.0, 1.0),
-            jnp.where(fifth_place == 0, -quark_mass, 1.0),
-            jnp.where(fifth_place == fifth_count - 1, -quark_mass, 1.0),
-            jnp.where(space_place % 2 == 0, 1.0, 0.0),
-        ]
-    ).astype(jnp.float32)
     near_pairs = [(i, i ^ 1) for i in range(space_count)]
     far_pairs = [(i, (i + (1 if i % 2 else -1)) % space_count) for i in range(space_count)]
     up_pairs = [(i, (i + 1) % fifth_count) for i in range(fifth_count)]
     down_pairs = [(i, (i - 1) % fifth_count) for i in range(fifth_count)]
     mirror_pairs = [(i, fifth_count - 1 - i) for i in range(fifth_count)]
 
-    smem = pl.BlockSpec(memory_space=pltpu.SMEM)
     vmem = pl.BlockSpec(memory_space=pltpu.VMEM)
 
     def array(*dims):
         return jax.ShapeDtypeStruct(dims, jnp.float32)
 
-    def call(body, out_shape, *operands, with_scalars):
-        specs = ([smem] if with_scalars else []) + [vmem] * (len(operands) - with_scalars)
+    def call(body, out_shape, *operands):
         return pl.pallas_call(
             body,
             out_shape=out_shape,
-            in_specs=specs,
+            in_specs=[vmem] * len(operands),
             out_specs=jax.tree.map(lambda _: vmem, out_shape),
+            compiler_params=pltpu.CompilerParams(vmem_limit_bytes=VMEM_GRANT),
         )(*operands)
 
     sends = (array(24, rows, LANES), array(12, rows, LANES), array(12, rows, LANES), array(12, blocks, LANES), array(12, blocks, LANES))
@@ -333,7 +332,7 @@
     links = gauge_links.reshape(4, 18, blocks, LANES)
     mirrored_start = lax.ppermute(start, "fifth", mirror_pairs)
     field, near, far, up, down = call(
-        lambda *refs: first_kernel(shape, *refs), sends, scalars, start, links, with_scalars=1
+        lambda *refs: first_kernel(shape, *refs), sends, start, links
     )
     wide = None
     for step in range(DEGREE):
@@ -343,10 +342,10 @@
         high_in = lax.ppermute(down, "fifth", down_pairs)
         near_in = lax.ppermute(near, "space", near_pairs)
         if wide is None:
-            wide = call(lambda *refs: widen_kernel(shape, *refs), array(72, rows, LANES), links, with_scalars=0)
+            wide = call(lambda *refs: widen_kernel(shape, *refs), array(72, rows, LANES), links)
         part = call(
             lambda *refs, odd_step=odd_step: space_kernel(shape, odd_step, *refs),
-            array(24, rows, LANES), field, wide, with_scalars=0,
+            array(24, rows, LANES), field, wide,
         )
         last = step == DEGREE - 1
         body = lambda *refs, odd_step=odd_step, step=step, last=last: close_kernel(
@@ -354,8 +353,7 @@
         )
         result = call(
             body, array(slices, 24, blocks, LANES) if last else sends,
-            scalars, part, wide, start if odd_step else mirrored_start, near_in, far_in, low_in, high_in,
-            with_scalars=1,
+            part, wide, start if odd_step else mirrored_start, near_in, far_in, low_in, high_in,
         )
         if not last:
             field, near, far, up, down = result

time: 48.4 us -> 35.9 us (0.74)
  Pallas kernels: 18.1 us -> 1.93 us
  waiting for transfers between devices: 1.47 us -> 9.39 us
  local copies, waits for them, and re-layouts: 5.47 us -> 1.84 us
    pallas_call x10, Pallas kernels: 18.1 us -> 1.93 us  [call(): pl.pallas_call(body, out_shape=out_shape, in_specs=[vmem] * len(operands)...]
    ppermute x4, waiting for transfers between devices: 0.58 us -> 6.36 us  [on_device(): low_in = lax.ppermute(up, 'fifth', up_pairs)]
    unnamed x34 -> x6, local copies, waits for them, and re-layouts: 4.85 us -> 1.84 us
    ppermute x4, starting transfers between devices: 3.73 us -> 6.3 us  [on_device(): low_in = lax.ppermute(up, 'fifth', up_pairs)]
    ppermute x4, starting transfers between devices: 7.97 us -> 5.4 us  [on_device(): high_in = lax.ppermute(down, 'fifth', down_pairs)]
    ppermute x4, waiting for transfers between devices: 0.8 us -> 3.01 us  [on_device(): high_in = lax.ppermute(down, 'fifth', down_pairs)]
    ppermute x4, starting transfers between devices: 7.25 us -> 6.57 us  [on_device(): far_in = lax.ppermute(far, 'space', far_pairs)]
    another operation x1 -> x0, local copies, waits for them, and re-layouts: 0.62 us -> none  [on_device(): jnp.stack([jnp.where(space_place == 0, -1.0, 1.0), jnp.where(space_place...]
  transfers between devices with their start and end apart: 17 -> 17, of which waited for: 6 -> 7; matrix products, arithmetic and copies ran while one was open for 1% -> 0% of each run, Pallas kernels for 22% -> 3%
where the time goes in v2:
time: 35.9 us; the launch traced here: 35.8 us
  starting transfers between devices  22.5 us (63%)
  waiting for transfers between devices  9.39 us (26%)
  Pallas kernels  1.93 us (5%)
  local copies, waits for them, and re-layouts  1.84 us (5%)
    ppermute x4, starting transfers between devices, on_device(): far_in = lax.ppermute(far, 'space', far_pairs)  6.57 us
    ppermute x4, waiting for transfers between devices, on_device(): low_in = lax.ppermute(up, 'fifth', up_pairs)  6.36 us
    ppermute x4, starting transfers between devices, on_device(): low_in = lax.ppermute(up, 'fifth', up_pairs)  6.3 us
    ppermute x4, starting transfers between devices, on_device(): high_in = lax.ppermute(down, 'fifth', down_pairs)  5.4 us
    ppermute x1, starting transfers between devices, on_device(): mirrored_start = lax.ppermute(start, 'fifth', mirror_pairs)  3.92 us
    ppermute x4, waiting for transfers between devices, on_device(): high_in = lax.ppermute(down, 'fifth', down_pairs)  3.01 us
    pallas_call x10, Pallas kernels, call(): pl.pallas_call(body, out_shape=out_shape, in_specs=[vmem] * len(operands)...  1.93 us
    unnamed x6, local copies, waits for them, and re-layouts  1.84 us
  transfers between devices with their start and end apart: 17, of which 7 were waited for; matrix products, arithmetic and copies ran while one was open for 0% of the time, Pallas kernels for 3%

profile of v2, /device:TPU:0, one launch (start us, length us, event | category | flops | bytes accessed | tf_op | source)
XLA Modules:
  0.0 35.8 jit_solution(11280083952008186901)
XLA Ops:
  0.0 3.9 %collective-permute-start = (f32[2,24,4,128]{3,2,1,0:T(4,128)}, f32[2,24,4,128]{3,2,1,0:T(4,128)S(1)}, u32[]{:S(2)}, u32[]{:S(2)}) collective-permute-start(f32[2,24,4,128]{3,2,1,0:T(4,128)} %bitcast.3), channel_id=1, source_target_pairs={{0,24},{8,16},{16,8},{24,0},{1,25},{9,17},{17,9},{25,1},{2,26},{10... | collective-permute-start | bytes 294920 | tf_op jit(solution)/shard_map/ppermute | solution.py:333
  3.9 0.0 copy-start
  3.9 0.9 %copy-done = f32[2,24,1,512]{3,2,1,0:T(1,128)S(1)} copy-done((f32[2,24,1,512]{3,2,1,0:T(1,128)S(1)}, f32[2,24,1,512]{3,2,1,0:T(1,128)}, u32[]{:S(2)}) %copy-start) | copy-done | bytes 98328
  4.9 0.0 copy-start.2
  4.9 0.9 %copy-done.2 = f32[4,18,1,512]{3,2,1,0:T(1,128)S(1)} copy-done((f32[4,18,1,512]{3,2,1,0:T(1,128)S(1)}, f32[4,18,1,512]{3,2,1,0:T(1,128)}, u32[]{:S(2)}) %copy-start.2) | copy-done | bytes 147480
  5.8 0.1 collective-permute-start.1
  5.9 3.7 %collective-permute-start.2 = (f32[12,8,128]{2,1,0:T(8,128)S(1)}, f32[12,8,128]{2,1,0:T(8,128)S(1)}, u32[]{:S(2)}, u32[]{:S(2)}) collective-permute-start(f32[12,8,128]{2,1,0:T(8,128)S(1)} %get-tuple-element.27), channel_id=1, source_target_pairs={{0,7},{1,2},{2,1},{3,4},{4,3},{5,6},{6,5},{7,0},{8,15},{9,10},{10,... | collective-permute-start | bytes 147464 | tf_op jit(solution)/shard_map/ppermute | solution.py:340
  9.6 0.5 %collective-permute-start.3 = (f32[12,4,128]{2,1,0:T(4,128)S(1)}, f32[12,4,128]{2,1,0:T(4,128)S(1)}, u32[]{:S(2)}, u32[]{:S(2)}) collective-permute-start(f32[12,4,128]{2,1,0:T(4,128)S(1)} %get-tuple-element.28), channel_id=1, source_target_pairs={{0,8},{8,16},{16,24},{24,0},{1,9},{9,17},{17,25},{25,1},{2,10},{10... | collective-permute-start | bytes 73736 | tf_op jit(solution)/shard_map/ppermute | solution.py:341
  10.1 2.4 %collective-permute-start.4 = (f32[12,4,128]{2,1,0:T(4,128)S(1)}, f32[12,4,128]{2,1,0:T(4,128)S(1)}, u32[]{:S(2)}, u32[]{:S(2)}) collective-permute-start(f32[12,4,128]{2,1,0:T(4,128)S(1)} %get-tuple-element.29), channel_id=1, source_target_pairs={{0,24},{8,0},{16,8},{24,16},{1,25},{9,1},{17,9},{25,17},{2,26},{10... | collective-permute-start | bytes 73736 | tf_op jit(solution)/shard_map/ppermute | solution.py:342
  12.6 0.2 shard_map.30.refs_0_
  12.8 1.5 %collective-permute-done.3.refs_5_ = f32[12,4,128]{2,1,0:T(4,128)S(1)} collective-permute-done((f32[12,4,128]{2,1,0:T(4,128)S(1)}, f32[12,4,128]{2,1,0:T(4,128)S(1)}, u32[]{:S(2)}, u32[]{:S(2)}) %collective-permute-start.3) | collective-permute-done | bytes 24608 | tf_op jit(solution)/shard_map/ppermute | solution.py:341
  14.3 0.0 collective-permute-done.4.refs_6_
  14.3 0.0 collective-permute-done.1.refs_3_
  14.3 0.0 collective-permute-done.2.refs_4_
  14.3 0.0 collective-permute-done.refs_2_
  14.3 0.1 shard_map.31
  14.5 0.1 collective-permute-start.5
  14.5 0.6 %collective-permute-start.6 = (f32[12,8,128]{2,1,0:T(8,128)S(1)}, f32[12,8,128]{2,1,0:T(8,128)S(1)}, u32[]{:S(2)}, u32[]{:S(2)}) collective-permute-start(f32[12,8,128]{2,1,0:T(8,128)S(1)} %get-tuple-element.32), channel_id=1, source_target_pairs={{0,7},{1,2},{2,1},{3,4},{4,3},{5,6},{6,5},{7,0},{8,15},{9,10},{10,... | collective-permute-start | bytes 147464 | tf_op jit(solution)/shard_map/ppermute | solution.py:340
  15.2 1.9 %collective-permute-start.7 = (f32[12,4,128]{2,1,0:T(4,128)S(1)}, f32[12,4,128]{2,1,0:T(4,128)S(1)}, u32[]{:S(2)}, u32[]{:S(2)}) collective-permute-start(f32[12,4,128]{2,1,0:T(4,128)S(1)} %get-tuple-element.33), channel_id=1, source_target_pairs={{0,8},{8,16},{16,24},{24,0},{1,9},{9,17},{17,25},{25,1},{2,10},{10... | collective-permute-start | bytes 73736 | tf_op jit(solution)/shard_map/ppermute | solution.py:341
  17.0 1.0 %collective-permute-start.8 = (f32[12,4,128]{2,1,0:T(4,128)S(1)}, f32[12,4,128]{2,1,0:T(4,128)S(1)}, u32[]{:S(2)}, u32[]{:S(2)}) collective-permute-start(f32[12,4,128]{2,1,0:T(4,128)S(1)} %get-tuple-element.34), channel_id=1, source_target_pairs={{0,24},{8,0},{16,8},{24,16},{1,25},{9,1},{17,9},{25,17},{2,26},{10... | collective-permute-start | bytes 73736 | tf_op jit(solution)/shard_map/ppermute | solution.py:342
  18.1 0.0 copy-start.1
  18.1 0.2 shard_map.32.refs_0_
  18.3 1.6 %collective-permute-done.7.refs_5_ = f32[12,4,128]{2,1,0:T(4,128)S(1)} collective-permute-done((f32[12,4,128]{2,1,0:T(4,128)S(1)}, f32[12,4,128]{2,1,0:T(4,128)S(1)}, u32[]{:S(2)}, u32[]{:S(2)}) %collective-permute-start.7) | collective-permute-done | bytes 24608 | tf_op jit(solution)/shard_map/ppermute | solution.py:341
  19.9 1.0 %collective-permute-done.8.refs_6_ = f32[12,4,128]{2,1,0:T(4,128)S(1)} collective-permute-done((f32[12,4,128]{2,1,0:T(4,128)S(1)}, f32[12,4,128]{2,1,0:T(4,128)S(1)}, u32[]{:S(2)}, u32[]{:S(2)}) %collective-permute-start.8) | collective-permute-done | bytes 24608 | tf_op jit(solution)/shard_map/ppermute | solution.py:342
  20.9 0.0 collective-permute-done.5.refs_3_
  20.9 0.0 collective-permute-done.6.refs_4_
  20.9 0.0 copy-done.1
  20.9 0.1 shard_map.33
  21.0 0.1 collective-permute-start.9
  21.1 1.7 %collective-permute-start.10 = (f32[12,8,128]{2,1,0:T(8,128)S(1)}, f32[12,8,128]{2,1,0:T(8,128)S(1)}, u32[]{:S(2)}, u32[]{:S(2)}) collective-permute-start(f32[12,8,128]{2,1,0:T(8,128)S(1)} %get-tuple-element.37), channel_id=1, source_target_pairs={{0,7},{1,2},{2,1},{3,4},{4,3},{5,6},{6,5},{7,0},{8,15},{9,10},{10,... | collective-permute-start | bytes 147464 | tf_op jit(solution)/shard_map/ppermute | solution.py:340
  22.8 1.5 %collective-permute-start.11 = (f32[12,4,128]{2,1,0:T(4,128)S(1)}, f32[12,4,128]{2,1,0:T(4,128)S(1)}, u32[]{:S(2)}, u32[]{:S(2)}) collective-permute-start(f32[12,4,128]{2,1,0:T(4,128)S(1)} %get-tuple-element.38), channel_id=1, source_target_pairs={{0,8},{8,16},{16,24},{24,0},{1,9},{9,17},{17,25},{25,1},{2,10},{10... | collective-permute-start | bytes 73736 | tf_op jit(solution)/shard_map/ppermute | solution.py:341
  24.3 1.4 %collective-permute-start.12 = (f32[12,4,128]{2,1,0:T(4,128)S(1)}, f32[12,4,128]{2,1,0:T(4,128)S(1)}, u32[]{:S(2)}, u32[]{:S(2)}) collective-permute-start(f32[12,4,128]{2,1,0:T(4,128)S(1)} %get-tuple-element.39), channel_id=1, source_target_pairs={{0,24},{8,0},{16,8},{24,16},{1,25},{9,1},{17,9},{25,17},{2,26},{10... | collective-permute-start | bytes 73736 | tf_op jit(solution)/shard_map/ppermute | solution.py:342
  25.7 0.2 shard_map.34.refs_0_
  25.9 1.6 %collective-permute-done.11.refs_5_ = f32[12,4,128]{2,1,0:T(4,128)S(1)} collective-permute-done((f32[12,4,128]{2,1,0:T(4,128)S(1)}, f32[12,4,128]{2,1,0:T(4,128)S(1)}, u32[]{:S(2)}, u32[]{:S(2)}) %collective-permute-start.11) | collective-permute-done | bytes 24608 | tf_op jit(solution)/shard_map/ppermute | solution.py:341
  27.5 0.6 %collective-permute-done.12.refs_6_ = f32[12,4,128]{2,1,0:T(4,128)S(1)} collective-permute-done((f32[12,4,128]{2,1,0:T(4,128)S(1)}, f32[12,4,128]{2,1,0:T(4,128)S(1)}, u32[]{:S(2)}, u32[]{:S(2)}) %collective-permute-start.12) | collective-permute-done | bytes 24608 | tf_op jit(solution)/shard_map/ppermute | solution.py:342
  28.1 0.0 collective-permute-done.9.refs_3_
  28.1 0.0 collective-permute-done.10.refs_4_
  28.1 0.1 shard_map.35
  28.2 0.1 collective-permute-start.13
  28.3 0.6 %collective-permute-start.14 = (f32[12,8,128]{2,1,0:T(8,128)S(1)}, f32[12,8,128]{2,1,0:T(8,128)S(1)}, u32[]{:S(2)}, u32[]{:S(2)}) collective-permute-start(f32[12,8,128]{2,1,0:T(8,128)S(1)} %get-tuple-element.42), channel_id=1, source_target_pairs={{0,7},{1,2},{2,1},{3,4},{4,3},{5,6},{6,5},{7,0},{8,15},{9,10},{10,... | collective-permute-start | bytes 147464 | tf_op jit(solution)/shard_map/ppermute | solution.py:340
  28.8 2.4 %collective-permute-start.15 = (f32[12,4,128]{2,1,0:T(4,128)S(1)}, f32[12,4,128]{2,1,0:T(4,128)S(1)}, u32[]{:S(2)}, u32[]{:S(2)}) collective-permute-start(f32[12,4,128]{2,1,0:T(4,128)S(1)} %get-tuple-element.43), channel_id=1, source_target_pairs={{0,8},{8,16},{16,24},{24,0},{1,9},{9,17},{17,25},{25,1},{2,10},{10... | collective-permute-start | bytes 73736 | tf_op jit(solution)/shard_map/ppermute | solution.py:341
  31.2 0.5 %collective-permute-start.16 = (f32[12,4,128]{2,1,0:T(4,128)S(1)}, f32[12,4,128]{2,1,0:T(4,128)S(1)}, u32[]{:S(2)}, u32[]{:S(2)}) collective-permute-start(f32[12,4,128]{2,1,0:T(4,128)S(1)} %get-tuple-element.44), channel_id=1, source_target_pairs={{0,24},{8,0},{16,8},{24,16},{1,25},{9,1},{17,9},{25,17},{2,26},{10... | collective-permute-start | bytes 73736 | tf_op jit(solution)/shard_map/ppermute | solution.py:342
  31.8 0.2 shard_map.36.refs_0_
  32.0 1.6 %collective-permute-done.15.refs_5_ = f32[12,4,128]{2,1,0:T(4,128)S(1)} collective-permute-done((f32[12,4,128]{2,1,0:T(4,128)S(1)}, f32[12,4,128]{2,1,0:T(4,128)S(1)}, u32[]{:S(2)}, u32[]{:S(2)}) %collective-permute-start.15) | collective-permute-done | bytes 24608 | tf_op jit(solution)/shard_map/ppermute | solution.py:341
  33.6 1.5 %collective-permute-done.16.refs_6_ = f32[12,4,128]{2,1,0:T(4,128)S(1)} collective-permute-done((f32[12,4,128]{2,1,0:T(4,128)S(1)}, f32[12,4,128]{2,1,0:T(4,128)S(1)}, u32[]{:S(2)}, u32[]{:S(2)}) %collective-permute-start.16) | collective-permute-done | bytes 24608 | tf_op jit(solution)/shard_map/ppermute | solution.py:342
  35.0 0.0 collective-permute-done.13.refs_3_
  35.0 0.0 collective-permute-done.14.refs_4_
  35.1 0.7 %shard_map.37 = f32[2,24,4,128]{3,2,1,0:T(4,128)} custom-call(f32[24,8,128]{2,1,0:T(8,128)S(1)} %shard_map.36.refs_0_, f32[72,8,128]{2,1,0:T(8,128)S(1)} %shard_map.29.refs_1_, f32[2,24,4,128]{3,2,1,0:T(4,128)S(1)} %bitcast.6, f32[12,8,128]{2,1,0:T(8,128)S(1)} %collective-permute-done.13.refs_3_, f32[12,8,128]{2,1,0:T(8,128)S(1)} %collective-permute-done.14.refs_4_, ...), custom_call_target="tpu_custom_call" | custom-call | tf_op jit(solution)/shard_map/pallas_call | solution.py:320
  (2 shorter events, 0.1 us)
Async XLA Ops:
  0.0 14.3 %collective-permute-start = (f32[2,24,4,128]{3,2,1,0:T(4,128)}, f32[2,24,4,128]{3,2,1,0:T(4,128)S(1)}, u32[]{:S(2)}, u32[]{:S(2)}) collective-permute-start(f32[2,24,4,128]{3,2,1,0:T(4,128)} %bitcast.3), channel_id=1, source_target_pairs={{0,24},{8,16},{16,8},{24,0},{1,25},{9,17},{17,9},{25,1},{2,26},{10... | collective-permute-start | bytes 294920 | tf_op jit(solution)/shard_map/ppermute | solution.py:333
  3.9 0.9 %copy-start = (f32[2,24,1,512]{3,2,1,0:T(1,128)S(1)}, f32[2,24,1,512]{3,2,1,0:T(1,128)}, u32[]{:S(2)}) copy-start(f32[2,24,1,512]{3,2,1,0:T(1,128)} %param.2) | copy-start | bytes 294916
  4.9 0.9 %copy-start.2 = (f32[4,18,1,512]{3,2,1,0:T(1,128)S(1)}, f32[4,18,1,512]{3,2,1,0:T(1,128)}, u32[]{:S(2)}) copy-start(f32[4,18,1,512]{3,2,1,0:T(1,128)} %param.3) | copy-start | bytes 442372
  5.8 8.5 %collective-permute-start.1 = (f32[12,8,128]{2,1,0:T(8,128)S(1)}, f32[12,8,128]{2,1,0:T(8,128)S(1)}, u32[]{:S(2)}, u32[]{:S(2)}) collective-permute-start(f32[12,8,128]{2,1,0:T(8,128)S(1)} %get-tuple-element.26), channel_id=1, source_target_pairs={{0,1},{1,0},{2,3},{3,2},{4,5},{5,4},{6,7},{7,6},{8,9},{9,8},{10,11... | collective-permute-start | bytes 147464 | tf_op jit(solution)/shard_map/ppermute | solution.py:343
  5.9 8.4 %collective-permute-start.2 = (f32[12,8,128]{2,1,0:T(8,128)S(1)}, f32[12,8,128]{2,1,0:T(8,128)S(1)}, u32[]{:S(2)}, u32[]{:S(2)}) collective-permute-start(f32[12,8,128]{2,1,0:T(8,128)S(1)} %get-tuple-element.27), channel_id=1, source_target_pairs={{0,7},{1,2},{2,1},{3,4},{4,3},{5,6},{6,5},{7,0},{8,15},{9,10},{10,... | collective-permute-start | bytes 147464 | tf_op jit(solution)/shard_map/ppermute | solution.py:340
  9.6 4.7 %collective-permute-start.3 = (f32[12,4,128]{2,1,0:T(4,128)S(1)}, f32[12,4,128]{2,1,0:T(4,128)S(1)}, u32[]{:S(2)}, u32[]{:S(2)}) collective-permute-start(f32[12,4,128]{2,1,0:T(4,128)S(1)} %get-tuple-element.28), channel_id=1, source_target_pairs={{0,8},{8,16},{16,24},{24,0},{1,9},{9,17},{17,25},{25,1},{2,10},{10... | collective-permute-start | bytes 73736 | tf_op jit(solution)/shard_map/ppermute | solution.py:341
  10.1 4.2 %collective-permute-start.4 = (f32[12,4,128]{2,1,0:T(4,128)S(1)}, f32[12,4,128]{2,1,0:T(4,128)S(1)}, u32[]{:S(2)}, u32[]{:S(2)}) collective-permute-start(f32[12,4,128]{2,1,0:T(4,128)S(1)} %get-tuple-element.29), channel_id=1, source_target_pairs={{0,24},{8,0},{16,8},{24,16},{1,25},{9,1},{17,9},{25,17},{2,26},{10... | collective-permute-start | bytes 73736 | tf_op jit(solution)/shard_map/ppermute | solution.py:342
  14.5 6.4 %collective-permute-start.5 = (f32[12,8,128]{2,1,0:T(8,128)S(1)}, f32[12,8,128]{2,1,0:T(8,128)S(1)}, u32[]{:S(2)}, u32[]{:S(2)}) collective-permute-start(f32[12,8,128]{2,1,0:T(8,128)S(1)} %get-tuple-element.31), channel_id=1, source_target_pairs={{0,1},{1,0},{2,3},{3,2},{4,5},{5,4},{6,7},{7,6},{8,9},{9,8},{10,11... | collective-permute-start | bytes 147464 | tf_op jit(solution)/shard_map/ppermute | solution.py:343
  14.5 6.3 %collective-permute-start.6 = (f32[12,8,128]{2,1,0:T(8,128)S(1)}, f32[12,8,128]{2,1,0:T(8,128)S(1)}, u32[]{:S(2)}, u32[]{:S(2)}) collective-permute-start(f32[12,8,128]{2,1,0:T(8,128)S(1)} %get-tuple-element.32), channel_id=1, source_target_pairs={{0,7},{1,2},{2,1},{3,4},{4,3},{5,6},{6,5},{7,0},{8,15},{9,10},{10,... | collective-permute-start | bytes 147464 | tf_op jit(solution)/shard_map/ppermute | solution.py:340
  15.2 4.7 %collective-permute-start.7 = (f32[12,4,128]{2,1,0:T(4,128)S(1)}, f32[12,4,128]{2,1,0:T(4,128)S(1)}, u32[]{:S(2)}, u32[]{:S(2)}) collective-permute-start(f32[12,4,128]{2,1,0:T(4,128)S(1)} %get-tuple-element.33), channel_id=1, source_target_pairs={{0,8},{8,16},{16,24},{24,0},{1,9},{9,17},{17,25},{25,1},{2,10},{10... | collective-permute-start | bytes 73736 | tf_op jit(solution)/shard_map/ppermute | solution.py:341
  17.0 3.8 %collective-permute-start.8 = (f32[12,4,128]{2,1,0:T(4,128)S(1)}, f32[12,4,128]{2,1,0:T(4,128)S(1)}, u32[]{:S(2)}, u32[]{:S(2)}) collective-permute-start(f32[12,4,128]{2,1,0:T(4,128)S(1)} %get-tuple-element.34), channel_id=1, source_target_pairs={{0,24},{8,0},{16,8},{24,16},{1,25},{9,1},{17,9},{25,17},{2,26},{10... | collective-permute-start | bytes 73736 | tf_op jit(solution)/shard_map/ppermute | solution.py:342
  18.1 2.8 %copy-start.1 = (f32[2,24,1,512]{3,2,1,0:T(1,128)S(1)}, f32[2,24,1,512]{3,2,1,0:T(1,128)}, u32[]{:S(2)}) copy-start(f32[2,24,1,512]{3,2,1,0:T(1,128)} %param.2) | copy-start | bytes 294916
  21.0 7.1 %collective-permute-start.9 = (f32[12,8,128]{2,1,0:T(8,128)S(1)}, f32[12,8,128]{2,1,0:T(8,128)S(1)}, u32[]{:S(2)}, u32[]{:S(2)}) collective-permute-start(f32[12,8,128]{2,1,0:T(8,128)S(1)} %get-tuple-element.36), channel_id=1, source_target_pairs={{0,1},{1,0},{2,3},{3,2},{4,5},{5,4},{6,7},{7,6},{8,9},{9,8},{10,11... | collective-permute-start | bytes 147464 | tf_op jit(solution)/shard_map/ppermute | solution.py:343
  21.1 7.0 %collective-permute-start.10 = (f32[12,8,128]{2,1,0:T(8,128)S(1)}, f32[12,8,128]{2,1,0:T(8,128)S(1)}, u32[]{:S(2)}, u32[]{:S(2)}) collective-permute-start(f32[12,8,128]{2,1,0:T(8,128)S(1)} %get-tuple-element.37), channel_id=1, source_target_pairs={{0,7},{1,2},{2,1},{3,4},{4,3},{5,6},{6,5},{7,0},{8,15},{9,10},{10,... | collective-permute-start | bytes 147464 | tf_op jit(solution)/shard_map/ppermute | solution.py:340
  22.8 4.8 %collective-permute-start.11 = (f32[12,4,128]{2,1,0:T(4,128)S(1)}, f32[12,4,128]{2,1,0:T(4,128)S(1)}, u32[]{:S(2)}, u32[]{:S(2)}) collective-permute-start(f32[12,4,128]{2,1,0:T(4,128)S(1)} %get-tuple-element.38), channel_id=1, source_target_pairs={{0,8},{8,16},{16,24},{24,0},{1,9},{9,17},{17,25},{25,1},{2,10},{10... | collective-permute-start | bytes 73736 | tf_op jit(solution)/shard_map/ppermute | solution.py:341
  24.3 3.8 %collective-permute-start.12 = (f32[12,4,128]{2,1,0:T(4,128)S(1)}, f32[12,4,128]{2,1,0:T(4,128)S(1)}, u32[]{:S(2)}, u32[]{:S(2)}) collective-permute-start(f32[12,4,128]{2,1,0:T(4,128)S(1)} %get-tuple-element.39), channel_id=1, source_target_pairs={{0,24},{8,0},{16,8},{24,16},{1,25},{9,1},{17,9},{25,17},{2,26},{10... | collective-permute-start | bytes 73736 | tf_op jit(solution)/shard_map/ppermute | solution.py:342
  28.2 6.8 %collective-permute-start.13 = (f32[12,8,128]{2,1,0:T(8,128)S(1)}, f32[12,8,128]{2,1,0:T(8,128)S(1)}, u32[]{:S(2)}, u32[]{:S(2)}) collective-permute-start(f32[12,8,128]{2,1,0:T(8,128)S(1)} %get-tuple-element.41), channel_id=1, source_target_pairs={{0,1},{1,0},{2,3},{3,2},{4,5},{5,4},{6,7},{7,6},{8,9},{9,8},{10,11... | collective-permute-start | bytes 147464 | tf_op jit(solution)/shard_map/ppermute | solution.py:343
  28.3 6.8 %collective-permute-start.14 = (f32[12,8,128]{2,1,0:T(8,128)S(1)}, f32[12,8,128]{2,1,0:T(8,128)S(1)}, u32[]{:S(2)}, u32[]{:S(2)}) collective-permute-start(f32[12,8,128]{2,1,0:T(8,128)S(1)} %get-tuple-element.42), channel_id=1, source_target_pairs={{0,7},{1,2},{2,1},{3,4},{4,3},{5,6},{6,5},{7,0},{8,15},{9,10},{10,... | collective-permute-start | bytes 147464 | tf_op jit(solution)/shard_map/ppermute | solution.py:340
  28.8 4.7 %collective-permute-start.15 = (f32[12,4,128]{2,1,0:T(4,128)S(1)}, f32[12,4,128]{2,1,0:T(4,128)S(1)}, u32[]{:S(2)}, u32[]{:S(2)}) collective-permute-start(f32[12,4,128]{2,1,0:T(4,128)S(1)} %get-tuple-element.43), channel_id=1, source_target_pairs={{0,8},{8,16},{16,24},{24,0},{1,9},{9,17},{17,25},{25,1},{2,10},{10... | collective-permute-start | bytes 73736 | tf_op jit(solution)/shard_map/ppermute | solution.py:341
  31.2 3.8 %collective-permute-start.16 = (f32[12,4,128]{2,1,0:T(4,128)S(1)}, f32[12,4,128]{2,1,0:T(4,128)S(1)}, u32[]{:S(2)}, u32[]{:S(2)}) collective-permute-start(f32[12,4,128]{2,1,0:T(4,128)S(1)} %get-tuple-element.44), channel_id=1, source_target_pairs={{0,24},{8,0},{16,8},{24,16},{1,25},{9,1},{17,9},{25,17},{2,26},{10... | collective-permute-start | bytes 73736 | tf_op jit(solution)/shard_map/ppermute | solution.py:342

commit v3 on v2

--- a/solution.py
+++ b/solution.py
@@ -9,6 +9,7 @@
 DEGREE = 4
 LANES = 128
 VMEM_GRANT = 8 * 2**20
+TABLE_FLOPS = 10**8
 
 wall_height = 1.8
 quark_mass = 0.1
@@ -163,6 +164,10 @@
     return [[(part((s * 3 + c) * 2), part((s * 3 + c) * 2 + 1)) for c in range(3)] for s in range(4)]
 
 
+def cut(parts, low, high):
+    return [[tuple(v[low:high] for v in pair) for pair in spin] for spin in parts]
+
+
 def pick(flag, first, second):
     return [
         [tuple(jnp.where(flag, a, b) for a, b in zip(p, q)) for p, q in zip(x, y)]
@@ -175,22 +180,24 @@
         space, fifth = lax.axis_index("space"), lax.axis_index("fifth")
         last_space, last_fifth = lax.axis_size("space") - 1, lax.axis_size("fifth") - 1
         self.even = space % 2 == 0
+        self.fifth_even = fifth % 2 == 0
         self.low_sign = jnp.where(space == 0, -1.0, 1.0)
         self.high_sign = jnp.where(space == last_space, -1.0, 1.0)
         self.low_mass = jnp.where(fifth == 0, -quark_mass, 1.0)
         self.high_mass = jnp.where(fifth == last_fifth, -quark_mass, 1.0)
 
 
-def send_parts(shape, field, link, even, odd_step, near_ref, far_ref, up_ref, down_ref):
+def send_parts(shape, field, link, place, odd_step, near_ref, far_ref, side_ref, across_ref):
     ahead = project(field, TIME, -1.0)
     behind = colour_mul(link, project(field, TIME, 1.0), True)
-    store_parts(far_ref, pick(even, ahead, behind))
-    first = (0, shape.blocks)
-    last = (shape.rows - shape.blocks, shape.rows)
+    store_parts(far_ref, pick(place.even, ahead, behind))
     upper, lower = field[0:2], field[2:4]
-    store_parts(up_ref, lower if odd_step else upper, last)
-    store_parts(down_ref, upper if odd_step else lower, first)
-    store_parts(near_ref, pick(even, behind, ahead))
+    up = cut(lower if odd_step else upper, shape.rows - shape.blocks, shape.rows)
+    down = cut(upper if odd_step else lower, 0, shape.blocks)
+    if across_ref is not None:
+        store_parts(across_ref, pick(place.fifth_even, down, up))
+    store_parts(side_ref, pick(place.fifth_even, up, down))
+    store_parts(near_ref, pick(place.even, behind, ahead))
 
 
 def widen_kernel(shape, links_ref, wide_ref):
@@ -200,16 +207,30 @@
             wide_ref[mu * 18 + index] = jnp.concatenate([value] * shape.slices, axis=0)
 
 
-def first_kernel(shape, spinor_ref, links_ref, field_ref, near_ref, far_ref, up_ref, down_ref):
-    even = Place().even
-    field = raw_field(shape, spinor_ref, False)
-    store_parts(field_ref, field)
-
-    def link_part(index):
-        return jnp.concatenate([links_ref[TIME, index]] * shape.slices, axis=0)
-
-    link = [[(link_part((r * 3 + c) * 2), link_part((r * 3 + c) * 2 + 1)) for c in range(3)] for r in range(3)]
-    send_parts(shape, field, link, even, False, near_ref, far_ref, up_ref, down_ref)
+def table_kernel(table_ref):
+    place = Place()
+    even = jnp.where(place.even, 1.0, 0.0)
+    values = (even, place.low_sign, place.high_sign, place.low_mass, place.high_mass)
+    for row, value in enumerate(values):
+        table_ref[row : row + 1] = jnp.full((1, LANES), value, jnp.float32)
+    table_ref[len(values) :] = jnp.zeros((8 - len(values), LANES), jnp.float32)
+
+
+def first_kernel(shape, spinor_ref, links_ref, table_ref, field_ref, near_ref, far_ref, side_ref, across_ref, link_ref, sems):
+    copies = []
+    for j in range(shape.slices):
+        part = pl.ds(j * shape.blocks, shape.blocks)
+        copies.append((spinor_ref.at[j], field_ref.at[:, part]))
+        copies.append((links_ref.at[TIME], link_ref.at[:, part]))
+    copies = [pltpu.make_async_copy(a, b, sems.at[i]) for i, (a, b) in enumerate(copies)]
+    for copy in copies:
+        copy.start()
+    for copy in copies:
+        copy.wait()
+    place = Place()
+    place.even = table_ref[0:1] > 0.5
+    field, link = load_field(field_ref), load_link(link_ref, 0)
+    send_parts(shape, field, link, place, False, near_ref, far_ref, side_ref, across_ref)
 
 
 def space_kernel(shape, odd_step, field_ref, wide_ref, part_ref):
@@ -249,8 +270,7 @@
 
 
 def close_kernel(
-    shape, odd_step, scale, weight, mirrored, last, part_ref, wide_ref, start_ref, near_ref, far_ref,
-    low_ref, high_ref, *out_refs
+    shape, odd_step, scale, weight, last, part_ref, wide_ref, start_ref, near_ref, far_ref, side_ref, across_ref, out_refs
 ):
     place = Place()
     even = place.even
@@ -264,7 +284,16 @@
     behind = [[tuple(v * place.low_sign for v in pair) for pair in spin] for spin in behind]
     add_rebuilt(total, ahead, TIME, -1.0)
     add_rebuilt(total, behind, TIME, 1.0)
-    start = raw_field(shape, start_ref, mirrored)
+    start = load_field(start_ref) if odd_step else raw_field(shape, start_ref, True)
+    side = load_half(side_ref)
+    if across_ref is None:
+        final = [[tuple(start_ref[shape.slices - 1, (s * 3 + c) * 2 + p] for p in range(2)) for c in range(3)] for s in range(2)]
+        first = [[tuple(start_ref[0, (s * 3 + c) * 2 + p] for p in range(2)) for c in range(3)] for s in range(2, 4)]
+        across = pick(place.fifth_even, final, first)
+    else:
+        across = load_half(across_ref)
+    low = pick(place.fifth_even, across, side)
+    high = pick(place.fifth_even, side, across)
     rest = jnp.zeros((shape.rows - shape.blocks, LANES), jnp.float32)
     field = []
     for s in range(4):
@@ -275,11 +304,10 @@
             pair = []
             for p in range(2):
                 index = (s * 3 + c) * 2 + p
-                half_index = (s % 2 * 3 + c) * 2 + p
                 if from_low:
-                    hop = jnp.concatenate([low_ref[half_index] * place.low_mass, rest], axis=0)
+                    hop = jnp.concatenate([low[s % 2][c][p] * place.low_mass, rest], axis=0)
                 else:
-                    hop = jnp.concatenate([rest, high_ref[half_index] * place.high_mass], axis=0)
+                    hop = jnp.concatenate([rest, high[s % 2][c][p] * place.high_mass], axis=0)
                 value = part_ref[index] - 0.5 * total[s][c][p] - hop
                 pair.append(weight * start[s][c][p] + sign * value)
             colours.append(tuple(pair))
@@ -292,71 +320,82 @@
                     for j in range(shape.slices):
                         out_ref[j, (s * 3 + c) * 2 + p] = field[s][c][p][j * shape.blocks : (j + 1) * shape.blocks]
         return
-    field_ref, near_out, far_out, up_ref, down_ref = out_refs
-    send_parts(shape, field, link, even, not odd_step, near_out, far_out, up_ref, down_ref)
+    field_ref, near_out, far_out, side_out, across_out = out_refs
+    send_parts(shape, field, link, place, not odd_step, near_out, far_out, side_out, across_out)
     store_parts(field_ref, field)
 
 
 def on_device(spinor, gauge_links):
     slices, _, depth, sites = spinor.shape
-    assert depth == 1 and DEGREE % 2 == 0
+    space_count = lax.axis_size("space")
+    fifth_count = lax.axis_size("fifth")
+    assert depth == 1 and DEGREE % 2 == 0 and space_count % 2 == 0 and fifth_count % 2 == 0
     shape = Shape(slices, sites)
     rows, blocks = shape.rows, shape.blocks
-    space_count = lax.axis_size("space")
-    fifth_count = lax.axis_size("fifth")
-    assert space_count % 2 == 0
     near_pairs = [(i, i ^ 1) for i in range(space_count)]
     far_pairs = [(i, (i + (1 if i % 2 else -1)) % space_count) for i in range(space_count)]
-    up_pairs = [(i, (i + 1) % fifth_count) for i in range(fifth_count)]
-    down_pairs = [(i, (i - 1) % fifth_count) for i in range(fifth_count)]
+    side_pairs = [(i, i ^ 1) for i in range(fifth_count)]
+    across_pairs = [(i, (i + (1 if i % 2 else -1)) % fifth_count) for i in range(fifth_count)]
     mirror_pairs = [(i, fifth_count - 1 - i) for i in range(fifth_count)]
+    first_across = across_pairs != mirror_pairs
 
     vmem = pl.BlockSpec(memory_space=pltpu.VMEM)
+    hbm = pl.BlockSpec(memory_space=pltpu.HBM)
 
     def array(*dims):
         return jax.ShapeDtypeStruct(dims, jnp.float32)
 
-    def call(body, out_shape, *operands):
+    def call(body, out_shape, *operands, operand_specs=None, scratch=()):
         return pl.pallas_call(
             body,
             out_shape=out_shape,
-            in_specs=[vmem] * len(operands),
+            in_specs=operand_specs or [vmem] * len(operands),
             out_specs=jax.tree.map(lambda _: vmem, out_shape),
+            scratch_shapes=scratch,
             compiler_params=pltpu.CompilerParams(vmem_limit_bytes=VMEM_GRANT),
         )(*operands)
 
-    sends = (array(24, rows, LANES), array(12, rows, LANES), array(12, rows, LANES), array(12, blocks, LANES), array(12, blocks, LANES))
+    whole, half, edge = array(24, rows, LANES), array(12, rows, LANES), array(12, blocks, LANES)
     weights = power_coefficients(DEGREE)
-
     start = spinor.reshape(slices, 24, blocks, LANES)
     links = gauge_links.reshape(4, 18, blocks, LANES)
-    mirrored_start = lax.ppermute(start, "fifth", mirror_pairs)
-    field, near, far, up, down = call(
-        lambda *refs: first_kernel(shape, *refs), sends, start, links
-    )
-    wide = None
+    table = pl.pallas_call(
+        table_kernel,
+        out_shape=array(8, LANES),
+        out_specs=vmem,
+        cost_estimate=pl.CostEstimate(flops=TABLE_FLOPS, bytes_accessed=4096, transcendentals=0),
+        compiler_params=pltpu.CompilerParams(vmem_limit_bytes=VMEM_GRANT),
+    )()
+    mirrored = lax.ppermute(start, "fifth", mirror_pairs)
+
+    def first(spinor_ref, links_ref, table_ref, field_ref, near_ref, far_ref, side_ref, *rest):
+        across_ref = rest[0] if first_across else None
+        first_kernel(shape, spinor_ref, links_ref, table_ref, field_ref, near_ref, far_ref, side_ref, across_ref, *rest[-2:])
+
+    sends = (whole, half, half, edge) + ((edge,) if first_across else ())
+    scratch = (pltpu.VMEM((18, rows, LANES), jnp.float32), pltpu.SemaphoreType.DMA((2 * slices,)))
+    origin, near, far, side, *across = call(first, sends, start, links, table, operand_specs=(hbm, hbm, vmem), scratch=scratch)
+    field, wide = origin, None
     for step in range(DEGREE):
-        odd_step = step % 2 == 1
+        odd_step, last = step % 2 == 1, step == DEGREE - 1
         far_in = lax.ppermute(far, "space", far_pairs)
-        low_in = lax.ppermute(up, "fifth", up_pairs)
-        high_in = lax.ppermute(down, "fifth", down_pairs)
+        across_in = [lax.ppermute(value, "fifth", across_pairs) for value in across]
+        side_in = lax.ppermute(side, "fifth", side_pairs)
         near_in = lax.ppermute(near, "space", near_pairs)
         if wide is None:
             wide = call(lambda *refs: widen_kernel(shape, *refs), array(72, rows, LANES), links)
-        part = call(
-            lambda *refs, odd_step=odd_step: space_kernel(shape, odd_step, *refs),
-            array(24, rows, LANES), field, wide,
-        )
-        last = step == DEGREE - 1
-        body = lambda *refs, odd_step=odd_step, step=step, last=last: close_kernel(
-            shape, odd_step, weights[DEGREE] if step == 0 else 1.0, weights[DEGREE - 1 - step], not odd_step, last, *refs
-        )
-        result = call(
-            body, array(slices, 24, blocks, LANES) if last else sends,
-            part, wide, start if odd_step else mirrored_start, near_in, far_in, low_in, high_in,
-        )
-        if not last:
-            field, near, far, up, down = result
+        part = call(lambda *refs, odd=odd_step: space_kernel(shape, odd, *refs), whole, field, wide)
+        scale = weights[DEGREE] if step == 0 else 1.0
+
+        def close(*refs, step=step, odd=odd_step, last=last, scale=scale, count=len(across)):
+            across_ref = refs[6] if count else None
+            close_kernel(shape, odd, scale, weights[DEGREE - 1 - step], last, *refs[:6], across_ref, refs[6 + count :])
+
+        operands = (part, wide, origin if odd_step else mirrored, near_in, far_in, side_in, *across_in)
+        if last:
+            result = call(close, array(slices, 24, blocks, LANES), *operands)
+        else:
+            field, near, far, side, *across = call(close, (whole, half, half, edge, edge), *operands)
     return result.reshape(slices, 24, depth, sites)
 
 

time: 35.9 us -> 33.7 us (0.939)
  starting transfers between devices: 22.5 us -> 18.6 us
  waiting for transfers between devices: 9.39 us -> 12.8 us
  local copies, waits for them, and re-layouts: 1.84 us -> 0.01 us
    ppermute x9 -> x8, starting transfers between devices: 15.6 us -> 10.8 us  [the longest x1 3.92 us: on_device(): mirrored = lax.ppermute(start, 'fifth', mirror_pairs)]
    ppermute x9 -> x8, waiting for transfers between devices: 9.37 us -> 12.8 us  [the longest x4 7.53 us: on_device(): side_in = lax.ppermute(side, 'fifth', side_pairs)]
    unnamed x6 -> x4, local copies, waits for them, and re-layouts: 1.84 us -> 0.01 us
    ppermute x4, starting transfers between devices: 6.57 us -> 7.48 us  [on_device(): far_in = lax.ppermute(far, 'space', far_pairs)]
    pallas_call x10 -> x11, Pallas kernels: 1.93 us -> 2.05 us  [the longest x10 2.04 us: call(): pl.pallas_call(body, out_shape=out_shape, in_specs=operand_specs or [vmem...]
  transfers between devices with their start and end apart: 17 -> 16, of which waited for: 7 -> 7; matrix products, arithmetic and copies ran while one was open for 0% -> 0% of each run, Pallas kernels for 3% -> 3%
where the time goes in v3:
time: 33.7 us; the launch traced here: 33.6 us
  starting transfers between devices  18.6 us (55%)
  waiting for transfers between devices  12.8 us (38%)
  Pallas kernels  2.05 us (6%)
    ppermute x4, waiting for transfers between devices, on_device(): side_in = lax.ppermute(side, 'fifth', side_pairs)  7.53 us
    ppermute x4, starting transfers between devices, on_device(): far_in = lax.ppermute(far, 'space', far_pairs)  7.48 us
    ppermute x3, waiting for transfers between devices, on_device(): across_in = [lax.ppermute(value, 'fifth', across_pairs) for value in across]  5.23 us
    ppermute x1, starting transfers between devices, on_device(): mirrored = lax.ppermute(start, 'fifth', mirror_pairs)  3.92 us
    ppermute x3, starting transfers between devices, on_device(): across_in = [lax.ppermute(value, 'fifth', across_pairs) for value in across]  3.8 us
    ppermute x4, starting transfers between devices, on_device(): side_in = lax.ppermute(side, 'fifth', side_pairs)  3.1 us
    pallas_call x10, Pallas kernels, call(): pl.pallas_call(body, out_shape=out_shape, in_specs=operand_specs or [vmem...  2.04 us
  transfers between devices with their start and end apart: 16, of which 7 were waited for; matrix products, arithmetic and copies ran while one was open for 0% of the time, Pallas kernels for 3%

profile of v3, /device:TPU:0, one launch (start us, length us, event | category | flops | bytes accessed | tf_op | source)
XLA Modules:
  0.0 33.6 jit_solution(10572825893453847201)
XLA Ops:
  0.0 0.0 copy-start
  0.0 0.0 copy-start.1
  0.0 3.9 %collective-permute-start = (f32[2,24,4,128]{3,2,1,0:T(4,128)}, f32[2,24,4,128]{3,2,1,0:T(4,128)S(1)}, u32[]{:S(2)}, u32[]{:S(2)}) collective-permute-start(f32[2,24,4,128]{3,2,1,0:T(4,128)} %bitcast.5), channel_id=1, source_target_pairs={{0,24},{8,16},{16,8},{24,0},{1,25},{9,17},{17,9},{25,1},{2,26},{10... | collective-permute-start | bytes 294920 | tf_op jit(solution)/shard_map/ppermute | solution.py:369
  3.9 0.0 copy-done
  3.9 0.0 copy-done.1
  4.0 0.1 shard_map.29
  4.1 0.1 collective-permute-start.1
  4.1 3.7 %collective-permute-start.2 = (f32[12,8,128]{2,1,0:T(8,128)S(1)}, f32[12,8,128]{2,1,0:T(8,128)S(1)}, u32[]{:S(2)}, u32[]{:S(2)}) collective-permute-start(f32[12,8,128]{2,1,0:T(8,128)S(1)} %get-tuple-element.26), channel_id=1, source_target_pairs={{0,7},{1,2},{2,1},{3,4},{4,3},{5,6},{6,5},{7,0},{8,15},{9,10},{10,... | collective-permute-start | bytes 147464 | tf_op jit(solution)/shard_map/ppermute | solution.py:381
  7.8 0.5 %collective-permute-start.3 = (f32[12,4,128]{2,1,0:T(4,128)S(1)}, f32[12,4,128]{2,1,0:T(4,128)S(1)}, u32[]{:S(2)}, u32[]{:S(2)}) collective-permute-start(f32[12,4,128]{2,1,0:T(4,128)S(1)} %get-tuple-element.27), channel_id=1, source_target_pairs={{0,8},{8,0},{16,24},{24,16},{1,9},{9,1},{17,25},{25,17},{2,10},{10... | collective-permute-start | bytes 73736 | tf_op jit(solution)/shard_map/ppermute | solution.py:383
  8.4 0.2 shard_map.31.refs_0_
  8.6 3.0 %collective-permute-done.3.refs_5_ = f32[12,4,128]{2,1,0:T(4,128)S(1)} collective-permute-done((f32[12,4,128]{2,1,0:T(4,128)S(1)}, f32[12,4,128]{2,1,0:T(4,128)S(1)}, u32[]{:S(2)}, u32[]{:S(2)}) %collective-permute-start.3) | collective-permute-done | bytes 24608 | tf_op jit(solution)/shard_map/ppermute | solution.py:383
  11.7 0.0 collective-permute-done.1.refs_3_
  11.7 0.0 collective-permute-done.2.refs_4_
  11.7 0.0 collective-permute-done.refs_2_
  11.7 0.1 shard_map.32
  11.8 0.1 collective-permute-start.4
  11.9 1.5 %collective-permute-start.5 = (f32[12,8,128]{2,1,0:T(8,128)S(1)}, f32[12,8,128]{2,1,0:T(8,128)S(1)}, u32[]{:S(2)}, u32[]{:S(2)}) collective-permute-start(f32[12,8,128]{2,1,0:T(8,128)S(1)} %get-tuple-element.30), channel_id=1, source_target_pairs={{0,7},{1,2},{2,1},{3,4},{4,3},{5,6},{6,5},{7,0},{8,15},{9,10},{10,... | collective-permute-start | bytes 147464 | tf_op jit(solution)/shard_map/ppermute | solution.py:381
  13.4 0.5 %collective-permute-start.6 = (f32[12,4,128]{2,1,0:T(4,128)S(1)}, f32[12,4,128]{2,1,0:T(4,128)S(1)}, u32[]{:S(2)}, u32[]{:S(2)}) collective-permute-start(f32[12,4,128]{2,1,0:T(4,128)S(1)} %get-tuple-element.31), channel_id=1, source_target_pairs={{0,8},{8,0},{16,24},{24,16},{1,9},{9,1},{17,25},{25,17},{2,10},{10... | collective-permute-start | bytes 73736 | tf_op jit(solution)/shard_map/ppermute | solution.py:383
  14.0 1.4 %collective-permute-start.7 = (f32[12,4,128]{2,1,0:T(4,128)S(1)}, f32[12,4,128]{2,1,0:T(4,128)S(1)}, u32[]{:S(2)}, u32[]{:S(2)}) collective-permute-start(f32[12,4,128]{2,1,0:T(4,128)S(1)} %get-tuple-element.32), channel_id=1, source_target_pairs={{0,24},{8,16},{16,8},{24,0},{1,25},{9,17},{17,9},{25,1},{2,26},{10... | collective-permute-start | bytes 73736 | tf_op jit(solution)/shard_map/ppermute | solution.py:382
  15.4 0.2 shard_map.33.refs_0_
  15.6 1.6 %collective-permute-done.6.refs_5_ = f32[12,4,128]{2,1,0:T(4,128)S(1)} collective-permute-done((f32[12,4,128]{2,1,0:T(4,128)S(1)}, f32[12,4,128]{2,1,0:T(4,128)S(1)}, u32[]{:S(2)}, u32[]{:S(2)}) %collective-permute-start.6) | collective-permute-done | bytes 24608 | tf_op jit(solution)/shard_map/ppermute | solution.py:383
  17.3 1.4 %collective-permute-done.7.refs_6_ = f32[12,4,128]{2,1,0:T(4,128)S(1)} collective-permute-done((f32[12,4,128]{2,1,0:T(4,128)S(1)}, f32[12,4,128]{2,1,0:T(4,128)S(1)}, u32[]{:S(2)}, u32[]{:S(2)}) %collective-permute-start.7) | collective-permute-done | bytes 24608 | tf_op jit(solution)/shard_map/ppermute | solution.py:382
  18.7 0.0 collective-permute-done.4.refs_3_
  18.7 0.0 collective-permute-done.5.refs_4_
  18.7 0.1 shard_map.34
  18.8 0.1 collective-permute-start.8
  18.9 0.7 %collective-permute-start.9 = (f32[12,8,128]{2,1,0:T(8,128)S(1)}, f32[12,8,128]{2,1,0:T(8,128)S(1)}, u32[]{:S(2)}, u32[]{:S(2)}) collective-permute-start(f32[12,8,128]{2,1,0:T(8,128)S(1)} %get-tuple-element.35), channel_id=1, source_target_pairs={{0,7},{1,2},{2,1},{3,4},{4,3},{5,6},{6,5},{7,0},{8,15},{9,10},{10,... | collective-permute-start | bytes 147464 | tf_op jit(solution)/shard_map/ppermute | solution.py:381
  19.6 1.5 %collective-permute-start.10 = (f32[12,4,128]{2,1,0:T(4,128)S(1)}, f32[12,4,128]{2,1,0:T(4,128)S(1)}, u32[]{:S(2)}, u32[]{:S(2)}) collective-permute-start(f32[12,4,128]{2,1,0:T(4,128)S(1)} %get-tuple-element.36), channel_id=1, source_target_pairs={{0,8},{8,0},{16,24},{24,16},{1,9},{9,1},{17,25},{25,17},{2,10},{10... | collective-permute-start | bytes 73736 | tf_op jit(solution)/shard_map/ppermute | solution.py:383
  21.1 0.9 %collective-permute-start.11 = (f32[12,4,128]{2,1,0:T(4,128)S(1)}, f32[12,4,128]{2,1,0:T(4,128)S(1)}, u32[]{:S(2)}, u32[]{:S(2)}) collective-permute-start(f32[12,4,128]{2,1,0:T(4,128)S(1)} %get-tuple-element.37), channel_id=1, source_target_pairs={{0,24},{8,16},{16,8},{24,0},{1,25},{9,17},{17,9},{25,1},{2,26},{10... | collective-permute-start | bytes 73736 | tf_op jit(solution)/shard_map/ppermute | solution.py:382
  22.0 0.2 shard_map.35.refs_0_
  22.2 1.2 %collective-permute-done.10.refs_5_ = f32[12,4,128]{2,1,0:T(4,128)S(1)} collective-permute-done((f32[12,4,128]{2,1,0:T(4,128)S(1)}, f32[12,4,128]{2,1,0:T(4,128)S(1)}, u32[]{:S(2)}, u32[]{:S(2)}) %collective-permute-start.10) | collective-permute-done | bytes 24608 | tf_op jit(solution)/shard_map/ppermute | solution.py:383
  23.4 2.4 %collective-permute-done.11.refs_6_ = f32[12,4,128]{2,1,0:T(4,128)S(1)} collective-permute-done((f32[12,4,128]{2,1,0:T(4,128)S(1)}, f32[12,4,128]{2,1,0:T(4,128)S(1)}, u32[]{:S(2)}, u32[]{:S(2)}) %collective-permute-start.11) | collective-permute-done | bytes 24608 | tf_op jit(solution)/shard_map/ppermute | solution.py:382
  25.8 0.0 collective-permute-done.8.refs_3_
  25.8 0.0 collective-permute-done.9.refs_4_
  25.8 0.1 shard_map.36
  26.0 0.1 collective-permute-start.12
  26.0 1.5 %collective-permute-start.13 = (f32[12,8,128]{2,1,0:T(8,128)S(1)}, f32[12,8,128]{2,1,0:T(8,128)S(1)}, u32[]{:S(2)}, u32[]{:S(2)}) collective-permute-start(f32[12,8,128]{2,1,0:T(8,128)S(1)} %get-tuple-element.40), channel_id=1, source_target_pairs={{0,7},{1,2},{2,1},{3,4},{4,3},{5,6},{6,5},{7,0},{8,15},{9,10},{10,... | collective-permute-start | bytes 147464 | tf_op jit(solution)/shard_map/ppermute | solution.py:381
  27.6 0.5 %collective-permute-start.14 = (f32[12,4,128]{2,1,0:T(4,128)S(1)}, f32[12,4,128]{2,1,0:T(4,128)S(1)}, u32[]{:S(2)}, u32[]{:S(2)}) collective-permute-start(f32[12,4,128]{2,1,0:T(4,128)S(1)} %get-tuple-element.41), channel_id=1, source_target_pairs={{0,8},{8,0},{16,24},{24,16},{1,9},{9,1},{17,25},{25,17},{2,10},{10... | collective-permute-start | bytes 73736 | tf_op jit(solution)/shard_map/ppermute | solution.py:383
  28.1 1.4 %collective-permute-start.15 = (f32[12,4,128]{2,1,0:T(4,128)S(1)}, f32[12,4,128]{2,1,0:T(4,128)S(1)}, u32[]{:S(2)}, u32[]{:S(2)}) collective-permute-start(f32[12,4,128]{2,1,0:T(4,128)S(1)} %get-tuple-element.42), channel_id=1, source_target_pairs={{0,24},{8,16},{16,8},{24,0},{1,25},{9,17},{17,9},{25,1},{2,26},{10... | collective-permute-start | bytes 73736 | tf_op jit(solution)/shard_map/ppermute | solution.py:382
  29.5 0.2 shard_map.37.refs_0_
  29.8 1.7 %collective-permute-done.14.refs_5_ = f32[12,4,128]{2,1,0:T(4,128)S(1)} collective-permute-done((f32[12,4,128]{2,1,0:T(4,128)S(1)}, f32[12,4,128]{2,1,0:T(4,128)S(1)}, u32[]{:S(2)}, u32[]{:S(2)}) %collective-permute-start.14) | collective-permute-done | bytes 24608 | tf_op jit(solution)/shard_map/ppermute | solution.py:383
  31.4 1.4 %collective-permute-done.15.refs_6_ = f32[12,4,128]{2,1,0:T(4,128)S(1)} collective-permute-done((f32[12,4,128]{2,1,0:T(4,128)S(1)}, f32[12,4,128]{2,1,0:T(4,128)S(1)}, u32[]{:S(2)}, u32[]{:S(2)}) %collective-permute-start.15) | collective-permute-done | bytes 24608 | tf_op jit(solution)/shard_map/ppermute | solution.py:382
  32.8 0.0 collective-permute-done.12.refs_3_
  32.8 0.0 collective-permute-done.13.refs_4_
  32.8 0.7 %shard_map.38 = f32[2,24,4,128]{3,2,1,0:T(4,128)} custom-call(f32[24,8,128]{2,1,0:T(8,128)S(1)} %shard_map.37.refs_0_, f32[72,8,128]{2,1,0:T(8,128)S(1)} %shard_map.30.refs_1_, f32[24,8,128]{2,1,0:T(8,128)S(1)} %get-tuple-element.24.refs_0_.refs_2_, f32[12,8,128]{2,1,0:T(8,128)S(1)} %collective-permute-done.12.refs_3_, ...), custom_call_target="tpu_custom_call" | custom-call | tf_op jit(solution)/shard_map/pallas_call | solution.py:349
  (2 shorter events, 0.0 us)
Async XLA Ops:
  0.0 3.9 %copy-start = (f32[4,18,1,512]{3,2,1,0:T(1,128)S(1)}, f32[4,18,1,512]{3,2,1,0:T(1,128)}, u32[]{:S(2)}) copy-start(f32[4,18,1,512]{3,2,1,0:T(1,128)} %param.3) | copy-start | bytes 442372
  0.0 3.9 %copy-start.1 = (f32[2,24,1,512]{3,2,1,0:T(1,128)S(1)}, f32[2,24,1,512]{3,2,1,0:T(1,128)}, u32[]{:S(2)}) copy-start(f32[2,24,1,512]{3,2,1,0:T(1,128)} %param.2) | copy-start | bytes 294916
  0.0 11.7 %collective-permute-start = (f32[2,24,4,128]{3,2,1,0:T(4,128)}, f32[2,24,4,128]{3,2,1,0:T(4,128)S(1)}, u32[]{:S(2)}, u32[]{:S(2)}) collective-permute-start(f32[2,24,4,128]{3,2,1,0:T(4,128)} %bitcast.5), channel_id=1, source_target_pairs={{0,24},{8,16},{16,8},{24,0},{1,25},{9,17},{17,9},{25,1},{2,26},{10... | collective-permute-start | bytes 294920 | tf_op jit(solution)/shard_map/ppermute | solution.py:369
  4.1 7.6 %collective-permute-start.1 = (f32[12,8,128]{2,1,0:T(8,128)S(1)}, f32[12,8,128]{2,1,0:T(8,128)S(1)}, u32[]{:S(2)}, u32[]{:S(2)}) collective-permute-start(f32[12,8,128]{2,1,0:T(8,128)S(1)} %get-tuple-element.25), channel_id=1, source_target_pairs={{0,1},{1,0},{2,3},{3,2},{4,5},{5,4},{6,7},{7,6},{8,9},{9,8},{10,11... | collective-permute-start | bytes 147464 | tf_op jit(solution)/shard_map/ppermute | solution.py:384
  4.1 7.5 %collective-permute-start.2 = (f32[12,8,128]{2,1,0:T(8,128)S(1)}, f32[12,8,128]{2,1,0:T(8,128)S(1)}, u32[]{:S(2)}, u32[]{:S(2)}) collective-permute-start(f32[12,8,128]{2,1,0:T(8,128)S(1)} %get-tuple-element.26), channel_id=1, source_target_pairs={{0,7},{1,2},{2,1},{3,4},{4,3},{5,6},{6,5},{7,0},{8,15},{9,10},{10,... | collective-permute-start | bytes 147464 | tf_op jit(solution)/shard_map/ppermute | solution.py:381
  7.8 3.8 %collective-permute-start.3 = (f32[12,4,128]{2,1,0:T(4,128)S(1)}, f32[12,4,128]{2,1,0:T(4,128)S(1)}, u32[]{:S(2)}, u32[]{:S(2)}) collective-permute-start(f32[12,4,128]{2,1,0:T(4,128)S(1)} %get-tuple-element.27), channel_id=1, source_target_pairs={{0,8},{8,0},{16,24},{24,16},{1,9},{9,1},{17,25},{25,17},{2,10},{10... | collective-permute-start | bytes 73736 | tf_op jit(solution)/shard_map/ppermute | solution.py:383
  11.8 6.9 %collective-permute-start.4 = (f32[12,8,128]{2,1,0:T(8,128)S(1)}, f32[12,8,128]{2,1,0:T(8,128)S(1)}, u32[]{:S(2)}, u32[]{:S(2)}) collective-permute-start(f32[12,8,128]{2,1,0:T(8,128)S(1)} %get-tuple-element.29), channel_id=1, source_target_pairs={{0,1},{1,0},{2,3},{3,2},{4,5},{5,4},{6,7},{7,6},{8,9},{9,8},{10,11... | collective-permute-start | bytes 147464 | tf_op jit(solution)/shard_map/ppermute | solution.py:384
  11.9 6.8 %collective-permute-start.5 = (f32[12,8,128]{2,1,0:T(8,128)S(1)}, f32[12,8,128]{2,1,0:T(8,128)S(1)}, u32[]{:S(2)}, u32[]{:S(2)}) collective-permute-start(f32[12,8,128]{2,1,0:T(8,128)S(1)} %get-tuple-element.30), channel_id=1, source_target_pairs={{0,7},{1,2},{2,1},{3,4},{4,3},{5,6},{6,5},{7,0},{8,15},{9,10},{10,... | collective-permute-start | bytes 147464 | tf_op jit(solution)/shard_map/ppermute | solution.py:381
  13.4 3.8 %collective-permute-start.6 = (f32[12,4,128]{2,1,0:T(4,128)S(1)}, f32[12,4,128]{2,1,0:T(4,128)S(1)}, u32[]{:S(2)}, u32[]{:S(2)}) collective-permute-start(f32[12,4,128]{2,1,0:T(4,128)S(1)} %get-tuple-element.31), channel_id=1, source_target_pairs={{0,8},{8,0},{16,24},{24,16},{1,9},{9,1},{17,25},{25,17},{2,10},{10... | collective-permute-start | bytes 73736 | tf_op jit(solution)/shard_map/ppermute | solution.py:383
  14.0 4.7 %collective-permute-start.7 = (f32[12,4,128]{2,1,0:T(4,128)S(1)}, f32[12,4,128]{2,1,0:T(4,128)S(1)}, u32[]{:S(2)}, u32[]{:S(2)}) collective-permute-start(f32[12,4,128]{2,1,0:T(4,128)S(1)} %get-tuple-element.32), channel_id=1, source_target_pairs={{0,24},{8,16},{16,8},{24,0},{1,25},{9,17},{17,9},{25,1},{2,26},{10... | collective-permute-start | bytes 73736 | tf_op jit(solution)/shard_map/ppermute | solution.py:382
  18.8 7.0 %collective-permute-start.8 = (f32[12,8,128]{2,1,0:T(8,128)S(1)}, f32[12,8,128]{2,1,0:T(8,128)S(1)}, u32[]{:S(2)}, u32[]{:S(2)}) collective-permute-start(f32[12,8,128]{2,1,0:T(8,128)S(1)} %get-tuple-element.34), channel_id=1, source_target_pairs={{0,1},{1,0},{2,3},{3,2},{4,5},{5,4},{6,7},{7,6},{8,9},{9,8},{10,11... | collective-permute-start | bytes 147464 | tf_op jit(solution)/shard_map/ppermute | solution.py:384
  18.9 6.9 %collective-permute-start.9 = (f32[12,8,128]{2,1,0:T(8,128)S(1)}, f32[12,8,128]{2,1,0:T(8,128)S(1)}, u32[]{:S(2)}, u32[]{:S(2)}) collective-permute-start(f32[12,8,128]{2,1,0:T(8,128)S(1)} %get-tuple-element.35), channel_id=1, source_target_pairs={{0,7},{1,2},{2,1},{3,4},{4,3},{5,6},{6,5},{7,0},{8,15},{9,10},{10,... | collective-permute-start | bytes 147464 | tf_op jit(solution)/shard_map/ppermute | solution.py:381
  19.6 3.8 %collective-permute-start.10 = (f32[12,4,128]{2,1,0:T(4,128)S(1)}, f32[12,4,128]{2,1,0:T(4,128)S(1)}, u32[]{:S(2)}, u32[]{:S(2)}) collective-permute-start(f32[12,4,128]{2,1,0:T(4,128)S(1)} %get-tuple-element.36), channel_id=1, source_target_pairs={{0,8},{8,0},{16,24},{24,16},{1,9},{9,1},{17,25},{25,17},{2,10},{10... | collective-permute-start | bytes 73736 | tf_op jit(solution)/shard_map/ppermute | solution.py:383
  21.1 4.7 %collective-permute-start.11 = (f32[12,4,128]{2,1,0:T(4,128)S(1)}, f32[12,4,128]{2,1,0:T(4,128)S(1)}, u32[]{:S(2)}, u32[]{:S(2)}) collective-permute-start(f32[12,4,128]{2,1,0:T(4,128)S(1)} %get-tuple-element.37), channel_id=1, source_target_pairs={{0,24},{8,16},{16,8},{24,0},{1,25},{9,17},{17,9},{25,1},{2,26},{10... | collective-permute-start | bytes 73736 | tf_op jit(solution)/shard_map/ppermute | solution.py:382
  26.0 6.9 %collective-permute-start.12 = (f32[12,8,128]{2,1,0:T(8,128)S(1)}, f32[12,8,128]{2,1,0:T(8,128)S(1)}, u32[]{:S(2)}, u32[]{:S(2)}) collective-permute-start(f32[12,8,128]{2,1,0:T(8,128)S(1)} %get-tuple-element.39), channel_id=1, source_target_pairs={{0,1},{1,0},{2,3},{3,2},{4,5},{5,4},{6,7},{7,6},{8,9},{9,8},{10,11... | collective-permute-start | bytes 147464 | tf_op jit(solution)/shard_map/ppermute | solution.py:384
  26.0 6.8 %collective-permute-start.13 = (f32[12,8,128]{2,1,0:T(8,128)S(1)}, f32[12,8,128]{2,1,0:T(8,128)S(1)}, u32[]{:S(2)}, u32[]{:S(2)}) collective-permute-start(f32[12,8,128]{2,1,0:T(8,128)S(1)} %get-tuple-element.40), channel_id=1, source_target_pairs={{0,7},{1,2},{2,1},{3,4},{4,3},{5,6},{6,5},{7,0},{8,15},{9,10},{10,... | collective-permute-start | bytes 147464 | tf_op jit(solution)/shard_map/ppermute | solution.py:381
  27.6 3.8 %collective-permute-start.14 = (f32[12,4,128]{2,1,0:T(4,128)S(1)}, f32[12,4,128]{2,1,0:T(4,128)S(1)}, u32[]{:S(2)}, u32[]{:S(2)}) collective-permute-start(f32[12,4,128]{2,1,0:T(4,128)S(1)} %get-tuple-element.41), channel_id=1, source_target_pairs={{0,8},{8,0},{16,24},{24,16},{1,9},{9,1},{17,25},{25,17},{2,10},{10... | collective-permute-start | bytes 73736 | tf_op jit(solution)/shard_map/ppermute | solution.py:383
  28.1 4.7 %collective-permute-start.15 = (f32[12,4,128]{2,1,0:T(4,128)S(1)}, f32[12,4,128]{2,1,0:T(4,128)S(1)}, u32[]{:S(2)}, u32[]{:S(2)}) collective-permute-start(f32[12,4,128]{2,1,0:T(4,128)S(1)} %get-tuple-element.42), channel_id=1, source_target_pairs={{0,24},{8,16},{16,8},{24,0},{1,25},{9,17},{17,9},{25,1},{2,26},{10... | collective-permute-start | bytes 73736 | tf_op jit(solution)/shard_map/ppermute | solution.py:382

commit v4 on v3

--- a/solution.py
+++ b/solution.py
@@ -233,8 +233,7 @@
     send_parts(shape, field, link, place, False, near_ref, far_ref, side_ref, across_ref)
 
 
-def space_kernel(shape, odd_step, field_ref, wide_ref, part_ref):
-    field = load_field(field_ref)
+def space_hops(shape, field, wide_ref):
     zero = jnp.zeros((shape.rows, LANES), jnp.float32)
     total = [[(zero, zero) for _ in range(3)] for _ in range(4)]
     for mu in range(3):
@@ -248,6 +247,12 @@
         half = colour_mul(link, project(field, mu, 1.0), True)
         half = [[tuple(behind(v) for v in pair) for pair in spin] for spin in half]
         add_rebuilt(total, half, mu, 1.0)
+    return total
+
+
+def space_kernel(shape, odd_step, field_ref, wide_ref, part_ref):
+    field = load_field(field_ref)
+    total = space_hops(shape, field, wide_ref)
     row = index_of(shape, 0)
     inner_low = row >= shape.blocks
     inner_high = row < shape.rows - shape.blocks
@@ -269,8 +274,94 @@
     store_parts(part_ref, result)
 
 
+def raw_slice(ref, j):
+    return [[tuple(ref[j, (s * 3 + c) * 2 + p] for p in range(2)) for c in range(3)] for s in range(4)]
+
+
+def neighbour_slice(shape, place, ref):
+    return pick(place.fifth_even, raw_slice(ref, shape.slices - 1), raw_slice(ref, 0))
+
+
+def own_edge(shape, place, ref):
+    field = load_field(ref)
+    first = cut(field, 0, shape.blocks)
+    last = cut(field, shape.rows - shape.blocks, shape.rows)
+    return pick(place.fifth_even, first, last)
+
+
+def neighbour_kernel(shape, mirror_ref, origin_ref, wide_ref, part_ref):
+    place = Place()
+    near = neighbour_slice(shape, place, mirror_ref)
+    beyond = pick(place.fifth_even, raw_slice(mirror_ref, shape.slices - 2), raw_slice(mirror_ref, 1))
+    edge = own_edge(shape, place, origin_ref)
+    mass = jnp.where(place.fifth_even, place.low_mass, place.high_mass)
+    edge = [[tuple(v * mass for v in pair) for pair in spin] for spin in edge]
+    below = pick(place.fifth_even, beyond, edge)
+    above = pick(place.fifth_even, edge, beyond)
+    field = [[tuple(jnp.concatenate([v] * shape.slices, axis=0) for v in pair) for pair in spin] for spin in near]
+    total = cut(space_hops(shape, field, wide_ref), 0, shape.blocks)
+    result = []
+    for s in range(4):
+        hop = below if s < 2 else above
+        result.append(
+            [
+                tuple((5.0 - wall_height) * near[s][c][p] - 0.5 * total[s][c][p] - hop[s][c][p] for p in range(2))
+                for c in range(3)
+            ]
+        )
+    store_parts(part_ref, result)
+
+
+def store_packed(shape, ref, parts):
+    for s, colours in enumerate(parts):
+        for c, pair in enumerate(colours):
+            for p, value in enumerate(pair):
+                place, row = divmod((s * 3 + c) * 2 + p, shape.slices)
+                ref[12 + place, row * shape.blocks : (row + 1) * shape.blocks] = value
+
+
+def load_packed(shape, ref):
+    def part(index):
+        place, row = divmod(index, shape.slices)
+        return ref[12 + place, row * shape.blocks : (row + 1) * shape.blocks]
+
+    return [[tuple(part((s * 3 + c) * 2 + p) for p in range(2)) for c in range(3)] for s in range(2)]
+
+
+def send_neighbour(shape, place, mirror_ref, link, near_ref, far_ref):
+    field = neighbour_slice(shape, place, mirror_ref)
+    ahead = project(field, TIME, -1.0)
+    behind = colour_mul(cut(link, 0, shape.blocks), project(field, TIME, 1.0), True)
+    store_packed(shape, far_ref, pick(place.even, ahead, behind))
+    store_packed(shape, near_ref, pick(place.even, behind, ahead))
+
+
+def computed_across(shape, place, link, near_ref, far_ref, part_ref, origin_ref, scale, weight):
+    near, far = load_packed(shape, near_ref), load_packed(shape, far_ref)
+    ahead = colour_mul(cut(link, 0, shape.blocks), pick(place.even, near, far), False)
+    behind = pick(place.even, far, near)
+    ahead = [[tuple(v * place.high_sign for v in pair) for pair in spin] for spin in ahead]
+    behind = [[tuple(v * place.low_sign for v in pair) for pair in spin] for spin in behind]
+    zero = jnp.zeros((shape.blocks, LANES), jnp.float32)
+    total = [[(zero, zero) for _ in range(3)] for _ in range(4)]
+    add_rebuilt(total, ahead, TIME, -1.0)
+    add_rebuilt(total, behind, TIME, 1.0)
+    start, part = own_edge(shape, place, origin_ref), load_field(part_ref)
+    result = []
+    for s in range(4):
+        sign = scale if s < 2 else -scale
+        result.append(
+            [
+                tuple(weight * start[s][c][p] + sign * (part[s][c][p] - 0.5 * total[s][c][p]) for p in range(2))
+                for c in range(3)
+            ]
+        )
+    return pick(place.fifth_even, result[2:4], result[0:2])
+
+
 def close_kernel(
-    shape, odd_step, scale, weight, last, part_ref, wide_ref, start_ref, near_ref, far_ref, side_ref, across_ref, out_refs
+    shape, odd_step, scale, weight, last, part_ref, wide_ref, start_ref, near_ref, far_ref, side_ref, across_ref,
+    neighbour, out_refs
 ):
     place = Place()
     even = place.even
@@ -286,7 +377,9 @@
     add_rebuilt(total, behind, TIME, 1.0)
     start = load_field(start_ref) if odd_step else raw_field(shape, start_ref, True)
     side = load_half(side_ref)
-    if across_ref is None:
+    if neighbour is not None:
+        across = computed_across(shape, place, link, near_ref, far_ref, neighbour[0], start_ref, *neighbour[1:])
+    elif across_ref is None:
         final = [[tuple(start_ref[shape.slices - 1, (s * 3 + c) * 2 + p] for p in range(2)) for c in range(3)] for s in range(2)]
         first = [[tuple(start_ref[0, (s * 3 + c) * 2 + p] for p in range(2)) for c in range(3)] for s in range(2, 4)]
         across = pick(place.fifth_even, final, first)
@@ -320,8 +413,11 @@
                     for j in range(shape.slices):
                         out_ref[j, (s * 3 + c) * 2 + p] = field[s][c][p][j * shape.blocks : (j + 1) * shape.blocks]
         return
-    field_ref, near_out, far_out, side_out, across_out = out_refs
+    field_ref, near_out, far_out, side_out, *across_out = out_refs
+    across_out = across_out[0] if across_out else None
     send_parts(shape, field, link, place, not odd_step, near_out, far_out, side_out, across_out)
+    if across_out is None:
+        send_neighbour(shape, place, start_ref, link, near_out, far_out)
     store_parts(field_ref, field)
 
 
@@ -337,7 +433,7 @@
     side_pairs = [(i, i ^ 1) for i in range(fifth_count)]
     across_pairs = [(i, (i + (1 if i % 2 else -1)) % fifth_count) for i in range(fifth_count)]
     mirror_pairs = [(i, fifth_count - 1 - i) for i in range(fifth_count)]
-    first_across = across_pairs != mirror_pairs
+    first_across = across_pairs != mirror_pairs or slices < 2
 
     vmem = pl.BlockSpec(memory_space=pltpu.VMEM)
     hbm = pl.BlockSpec(memory_space=pltpu.HBM)
@@ -386,14 +482,24 @@
             wide = call(lambda *refs: widen_kernel(shape, *refs), array(72, rows, LANES), links)
         part = call(lambda *refs, odd=odd_step: space_kernel(shape, odd, *refs), whole, field, wide)
         scale = weights[DEGREE] if step == 0 else 1.0
-
-        def close(*refs, step=step, odd=odd_step, last=last, scale=scale, count=len(across)):
-            across_ref = refs[6] if count else None
-            close_kernel(shape, odd, scale, weights[DEGREE - 1 - step], last, *refs[:6], across_ref, refs[6 + count :])
-
-        operands = (part, wide, origin if odd_step else mirrored, near_in, far_in, side_in, *across_in)
+        computed = step == 1 and not first_across
+        if computed:
+            extra = (call(lambda *refs: neighbour_kernel(shape, *refs), array(24, blocks, LANES), mirrored, origin, wide),)
+        else:
+            extra = tuple(across_in)
+
+        def close(*refs, step=step, odd=odd_step, last=last, scale=scale, computed=computed, count=len(extra)):
+            across_ref = refs[6] if count and not computed else None
+            neighbour = (refs[6], weights[DEGREE], weights[DEGREE - 1]) if computed else None
+            weight = weights[DEGREE - 1 - step]
+            close_kernel(shape, odd, scale, weight, last, *refs[:6], across_ref, neighbour, refs[6 + count :])
+
+        operands = (part, wide, origin if odd_step else mirrored, near_in, far_in, side_in, *extra)
         if last:
             result = call(close, array(slices, 24, blocks, LANES), *operands)
+        elif step == 0 and not first_across:
+            more = array(12 + -(-12 // slices), rows, LANES)
+            field, near, far, side, *across = call(close, (whole, more, more, edge), *operands)
         else:
             field, near, far, side, *across = call(close, (whole, half, half, edge, edge), *operands)
     return result.reshape(slices, 24, depth, sites)

time: 33.7 us -> 32.6 us (0.967)
  starting transfers between devices: 18.6 us -> 17.2 us
  Pallas kernels: 2.05 us -> 2.39 us
    ppermute x3 -> x2, starting transfers between devices: 3.8 us -> 2.37 us  [on_device(): across_in = [lax.ppermute(value, 'fifth', across_pairs) for value in across]]
    ppermute x3 -> x2, waiting for transfers between devices: 5.23 us -> 3.81 us  [on_device(): across_in = [lax.ppermute(value, 'fifth', across_pairs) for value in across]]
    ppermute x4, waiting for transfers between devices: 7.53 us -> 8.68 us  [on_device(): side_in = lax.ppermute(side, 'fifth', side_pairs)]
    pallas_call x10 -> x11, Pallas kernels: 2.04 us -> 2.39 us  [call(): pl.pallas_call(body, out_shape=out_shape, in_specs=operand_specs or [vmem...]
  transfers between devices with their start and end apart: 16 -> 15, of which waited for: 7 -> 7; matrix products, arithmetic and copies ran while one was open for 0% -> 0% of each run, Pallas kernels for 3% -> 4%
where the time goes in v4:
time: 32.6 us; the launch traced here: 32.5 us
  starting transfers between devices  17.2 us (53%)
  waiting for transfers between devices  12.8 us (39%)
  Pallas kernels  2.39 us (7%)
    ppermute x4, waiting for transfers between devices, on_device(): side_in = lax.ppermute(side, 'fifth', side_pairs)  8.68 us
    ppermute x4, starting transfers between devices, on_device(): far_in = lax.ppermute(far, 'space', far_pairs)  7.49 us
    ppermute x1, starting transfers between devices, on_device(): mirrored = lax.ppermute(start, 'fifth', mirror_pairs)  3.92 us
    ppermute x2, waiting for transfers between devices, on_device(): across_in = [lax.ppermute(value, 'fifth', across_pairs) for value in across]  3.81 us
    ppermute x4, starting transfers between devices, on_device(): side_in = lax.ppermute(side, 'fifth', side_pairs)  3.1 us
    pallas_call x11, Pallas kernels, call(): pl.pallas_call(body, out_shape=out_shape, in_specs=operand_specs or [vmem...  2.39 us
    ppermute x2, starting transfers between devices, on_device(): across_in = [lax.ppermute(value, 'fifth', across_pairs) for value in across]  2.37 us
  transfers between devices with their start and end apart: 15, of which 7 were waited for; matrix products, arithmetic and copies ran while one was open for 0% of the time, Pallas kernels for 4%

profile of v4, /device:TPU:0, one launch (start us, length us, event | category | flops | bytes accessed | tf_op | source)
XLA Modules:
  0.0 32.5 jit_solution(702967721681392721)
XLA Ops:
  0.0 0.0 copy-start
  0.0 0.0 copy-start.1
  0.0 3.9 %collective-permute-start = (f32[2,24,4,128]{3,2,1,0:T(4,128)}, f32[2,24,4,128]{3,2,1,0:T(4,128)S(1)}, u32[]{:S(2)}, u32[]{:S(2)}) collective-permute-start(f32[2,24,4,128]{3,2,1,0:T(4,128)} %bitcast.5), channel_id=1, source_target_pairs={{0,24},{8,16},{16,8},{24,0},{1,25},{9,17},{17,9},{25,1},{2,26},{10... | collective-permute-start | bytes 294920 | tf_op jit(solution)/shard_map/ppermute | solution.py:465
  3.9 0.0 copy-done
  3.9 0.0 copy-done.1
  4.0 0.1 shard_map.29
  4.1 0.1 collective-permute-start.1
  4.1 3.7 %collective-permute-start.2 = (f32[12,8,128]{2,1,0:T(8,128)S(1)}, f32[12,8,128]{2,1,0:T(8,128)S(1)}, u32[]{:S(2)}, u32[]{:S(2)}) collective-permute-start(f32[12,8,128]{2,1,0:T(8,128)S(1)} %get-tuple-element.25), channel_id=1, source_target_pairs={{0,7},{1,2},{2,1},{3,4},{4,3},{5,6},{6,5},{7,0},{8,15},{9,10},{10,... | collective-permute-start | bytes 147464 | tf_op jit(solution)/shard_map/ppermute | solution.py:477
  7.8 0.5 %collective-permute-start.3 = (f32[12,4,128]{2,1,0:T(4,128)S(1)}, f32[12,4,128]{2,1,0:T(4,128)S(1)}, u32[]{:S(2)}, u32[]{:S(2)}) collective-permute-start(f32[12,4,128]{2,1,0:T(4,128)S(1)} %get-tuple-element.26), channel_id=1, source_target_pairs={{0,8},{8,0},{16,24},{24,16},{1,9},{9,1},{17,25},{25,17},{2,10},{10... | collective-permute-start | bytes 73736 | tf_op jit(solution)/shard_map/ppermute | solution.py:479
  8.4 0.2 shard_map.31.refs_0_
  8.6 3.0 %collective-permute-done.3.refs_5_ = f32[12,4,128]{2,1,0:T(4,128)S(1)} collective-permute-done((f32[12,4,128]{2,1,0:T(4,128)S(1)}, f32[12,4,128]{2,1,0:T(4,128)S(1)}, u32[]{:S(2)}, u32[]{:S(2)}) %collective-permute-start.3) | collective-permute-done | bytes 24608 | tf_op jit(solution)/shard_map/ppermute | solution.py:479
  11.7 0.0 collective-permute-done.1.refs_3_
  11.7 0.0 collective-permute-done.2.refs_4_
  11.7 0.0 collective-permute-done.refs_2_.refs_0_
  11.7 0.1 shard_map.32
  11.8 0.1 collective-permute-start.4
  11.9 1.5 %collective-permute-start.5 = (f32[18,8,128]{2,1,0:T(8,128)S(1)}, f32[18,8,128]{2,1,0:T(8,128)S(1)}, u32[]{:S(2)}, u32[]{:S(2)}) collective-permute-start(f32[18,8,128]{2,1,0:T(8,128)S(1)} %get-tuple-element.29), channel_id=1, source_target_pairs={{0,7},{1,2},{2,1},{3,4},{4,3},{5,6},{6,5},{7,0},{8,15},{9,10},{10,... | collective-permute-start | bytes 221192 | tf_op jit(solution)/shard_map/ppermute | solution.py:477
  13.5 0.5 %collective-permute-start.6 = (f32[12,4,128]{2,1,0:T(4,128)S(1)}, f32[12,4,128]{2,1,0:T(4,128)S(1)}, u32[]{:S(2)}, u32[]{:S(2)}) collective-permute-start(f32[12,4,128]{2,1,0:T(4,128)S(1)} %get-tuple-element.30), channel_id=1, source_target_pairs={{0,8},{8,0},{16,24},{24,16},{1,9},{9,1},{17,25},{25,17},{2,10},{10... | collective-permute-start | bytes 73736 | tf_op jit(solution)/shard_map/ppermute | solution.py:479
  14.0 0.2 shard_map.33.refs_0_
  14.2 0.2 shard_map.34.refs_6_
  14.5 2.8 %collective-permute-done.6.refs_5_ = f32[12,4,128]{2,1,0:T(4,128)S(1)} collective-permute-done((f32[12,4,128]{2,1,0:T(4,128)S(1)}, f32[12,4,128]{2,1,0:T(4,128)S(1)}, u32[]{:S(2)}, u32[]{:S(2)}) %collective-permute-start.6) | collective-permute-done | bytes 24608 | tf_op jit(solution)/shard_map/ppermute | solution.py:479
  17.3 0.0 collective-permute-done.4.refs_3_
  17.3 0.3 collective-permute-done.5.refs_4_
  17.6 0.2 shard_map.35
  17.7 0.1 collective-permute-start.7
  17.8 1.5 %collective-permute-start.8 = (f32[12,8,128]{2,1,0:T(8,128)S(1)}, f32[12,8,128]{2,1,0:T(8,128)S(1)}, u32[]{:S(2)}, u32[]{:S(2)}) collective-permute-start(f32[12,8,128]{2,1,0:T(8,128)S(1)} %get-tuple-element.33), channel_id=1, source_target_pairs={{0,7},{1,2},{2,1},{3,4},{4,3},{5,6},{6,5},{7,0},{8,15},{9,10},{10,... | collective-permute-start | bytes 147464 | tf_op jit(solution)/shard_map/ppermute | solution.py:477
  19.3 0.5 %collective-permute-start.9 = (f32[12,4,128]{2,1,0:T(4,128)S(1)}, f32[12,4,128]{2,1,0:T(4,128)S(1)}, u32[]{:S(2)}, u32[]{:S(2)}) collective-permute-start(f32[12,4,128]{2,1,0:T(4,128)S(1)} %get-tuple-element.34), channel_id=1, source_target_pairs={{0,8},{8,0},{16,24},{24,16},{1,9},{9,1},{17,25},{25,17},{2,10},{10... | collective-permute-start | bytes 73736 | tf_op jit(solution)/shard_map/ppermute | solution.py:479
  19.9 1.4 %collective-permute-start.10 = (f32[12,4,128]{2,1,0:T(4,128)S(1)}, f32[12,4,128]{2,1,0:T(4,128)S(1)}, u32[]{:S(2)}, u32[]{:S(2)}) collective-permute-start(f32[12,4,128]{2,1,0:T(4,128)S(1)} %get-tuple-element.35), channel_id=1, source_target_pairs={{0,24},{8,16},{16,8},{24,0},{1,25},{9,17},{17,9},{25,1},{2,26},{10... | collective-permute-start | bytes 73736 | tf_op jit(solution)/shard_map/ppermute | solution.py:478
  21.3 0.2 shard_map.36.refs_0_
  21.5 1.6 %collective-permute-done.9.refs_5_ = f32[12,4,128]{2,1,0:T(4,128)S(1)} collective-permute-done((f32[12,4,128]{2,1,0:T(4,128)S(1)}, f32[12,4,128]{2,1,0:T(4,128)S(1)}, u32[]{:S(2)}, u32[]{:S(2)}) %collective-permute-start.9) | collective-permute-done | bytes 24608 | tf_op jit(solution)/shard_map/ppermute | solution.py:479
  23.2 1.4 %collective-permute-done.10.refs_6_ = f32[12,4,128]{2,1,0:T(4,128)S(1)} collective-permute-done((f32[12,4,128]{2,1,0:T(4,128)S(1)}, f32[12,4,128]{2,1,0:T(4,128)S(1)}, u32[]{:S(2)}, u32[]{:S(2)}) %collective-permute-start.10) | collective-permute-done | bytes 24608 | tf_op jit(solution)/shard_map/ppermute | solution.py:478
  24.6 0.0 collective-permute-done.7.refs_3_
  24.6 0.0 collective-permute-done.8.refs_4_
  24.6 0.1 shard_map.37
  24.7 0.1 collective-permute-start.11
  24.8 0.7 %collective-permute-start.12 = (f32[12,8,128]{2,1,0:T(8,128)S(1)}, f32[12,8,128]{2,1,0:T(8,128)S(1)}, u32[]{:S(2)}, u32[]{:S(2)}) collective-permute-start(f32[12,8,128]{2,1,0:T(8,128)S(1)} %get-tuple-element.38), channel_id=1, source_target_pairs={{0,7},{1,2},{2,1},{3,4},{4,3},{5,6},{6,5},{7,0},{8,15},{9,10},{10,... | collective-permute-start | bytes 147464 | tf_op jit(solution)/shard_map/ppermute | solution.py:477
  25.5 1.5 %collective-permute-start.13 = (f32[12,4,128]{2,1,0:T(4,128)S(1)}, f32[12,4,128]{2,1,0:T(4,128)S(1)}, u32[]{:S(2)}, u32[]{:S(2)}) collective-permute-start(f32[12,4,128]{2,1,0:T(4,128)S(1)} %get-tuple-element.39), channel_id=1, source_target_pairs={{0,8},{8,0},{16,24},{24,16},{1,9},{9,1},{17,25},{25,17},{2,10},{10... | collective-permute-start | bytes 73736 | tf_op jit(solution)/shard_map/ppermute | solution.py:479
  27.0 0.9 %collective-permute-start.14 = (f32[12,4,128]{2,1,0:T(4,128)S(1)}, f32[12,4,128]{2,1,0:T(4,128)S(1)}, u32[]{:S(2)}, u32[]{:S(2)}) collective-permute-start(f32[12,4,128]{2,1,0:T(4,128)S(1)} %get-tuple-element.40), channel_id=1, source_target_pairs={{0,24},{8,16},{16,8},{24,0},{1,25},{9,17},{17,9},{25,1},{2,26},{10... | collective-permute-start | bytes 73736 | tf_op jit(solution)/shard_map/ppermute | solution.py:478
  28.0 0.2 shard_map.38.refs_0_
  28.2 1.2 %collective-permute-done.13.refs_5_ = f32[12,4,128]{2,1,0:T(4,128)S(1)} collective-permute-done((f32[12,4,128]{2,1,0:T(4,128)S(1)}, f32[12,4,128]{2,1,0:T(4,128)S(1)}, u32[]{:S(2)}, u32[]{:S(2)}) %collective-permute-start.13) | collective-permute-done | bytes 24608 | tf_op jit(solution)/shard_map/ppermute | solution.py:479
  29.4 2.4 %collective-permute-done.14.refs_6_ = f32[12,4,128]{2,1,0:T(4,128)S(1)} collective-permute-done((f32[12,4,128]{2,1,0:T(4,128)S(1)}, f32[12,4,128]{2,1,0:T(4,128)S(1)}, u32[]{:S(2)}, u32[]{:S(2)}) %collective-permute-start.14) | collective-permute-done | bytes 24608 | tf_op jit(solution)/shard_map/ppermute | solution.py:478
  31.7 0.0 collective-permute-done.11.refs_3_
  31.7 0.0 collective-permute-done.12.refs_4_
  31.7 0.7 %shard_map.39 = f32[2,24,4,128]{3,2,1,0:T(4,128)} custom-call(f32[24,8,128]{2,1,0:T(8,128)S(1)} %shard_map.38.refs_0_, f32[72,8,128]{2,1,0:T(8,128)S(1)} %shard_map.30.refs_1_.refs_2_, f32[24,8,128]{2,1,0:T(8,128)S(1)} %get-tuple-element.23.refs_0_.refs_1_.refs_2_, f32[12,8,128]{2,1,0:T(8,128)S(1)} %collective-permute-done.11.refs_3_, ...), custom_call_target="tpu_custom_call" | custom-call | tf_op jit(solution)/shard_map/pallas_call | solution.py:445
  (2 shorter events, 0.0 us)
Async XLA Ops:
  0.0 3.9 %copy-start = (f32[4,18,1,512]{3,2,1,0:T(1,128)S(1)}, f32[4,18,1,512]{3,2,1,0:T(1,128)}, u32[]{:S(2)}) copy-start(f32[4,18,1,512]{3,2,1,0:T(1,128)} %param.3) | copy-start | bytes 442372
  0.0 3.9 %copy-start.1 = (f32[2,24,1,512]{3,2,1,0:T(1,128)S(1)}, f32[2,24,1,512]{3,2,1,0:T(1,128)}, u32[]{:S(2)}) copy-start(f32[2,24,1,512]{3,2,1,0:T(1,128)} %param.2) | copy-start | bytes 294916
  0.0 11.7 %collective-permute-start = (f32[2,24,4,128]{3,2,1,0:T(4,128)}, f32[2,24,4,128]{3,2,1,0:T(4,128)S(1)}, u32[]{:S(2)}, u32[]{:S(2)}) collective-permute-start(f32[2,24,4,128]{3,2,1,0:T(4,128)} %bitcast.5), channel_id=1, source_target_pairs={{0,24},{8,16},{16,8},{24,0},{1,25},{9,17},{17,9},{25,1},{2,26},{10... | collective-permute-start | bytes 294920 | tf_op jit(solution)/shard_map/ppermute | solution.py:465
  4.1 7.6 %collective-permute-start.1 = (f32[12,8,128]{2,1,0:T(8,128)S(1)}, f32[12,8,128]{2,1,0:T(8,128)S(1)}, u32[]{:S(2)}, u32[]{:S(2)}) collective-permute-start(f32[12,8,128]{2,1,0:T(8,128)S(1)} %get-tuple-element.24), channel_id=1, source_target_pairs={{0,1},{1,0},{2,3},{3,2},{4,5},{5,4},{6,7},{7,6},{8,9},{9,8},{10,11... | collective-permute-start | bytes 147464 | tf_op jit(solution)/shard_map/ppermute | solution.py:480
  4.1 7.5 %collective-permute-start.2 = (f32[12,8,128]{2,1,0:T(8,128)S(1)}, f32[12,8,128]{2,1,0:T(8,128)S(1)}, u32[]{:S(2)}, u32[]{:S(2)}) collective-permute-start(f32[12,8,128]{2,1,0:T(8,128)S(1)} %get-tuple-element.25), channel_id=1, source_target_pairs={{0,7},{1,2},{2,1},{3,4},{4,3},{5,6},{6,5},{7,0},{8,15},{9,10},{10,... | collective-permute-start | bytes 147464 | tf_op jit(solution)/shard_map/ppermute | solution.py:477
  7.8 3.8 %collective-permute-start.3 = (f32[12,4,128]{2,1,0:T(4,128)S(1)}, f32[12,4,128]{2,1,0:T(4,128)S(1)}, u32[]{:S(2)}, u32[]{:S(2)}) collective-permute-start(f32[12,4,128]{2,1,0:T(4,128)S(1)} %get-tuple-element.26), channel_id=1, source_target_pairs={{0,8},{8,0},{16,24},{24,16},{1,9},{9,1},{17,25},{25,17},{2,10},{10... | collective-permute-start | bytes 73736 | tf_op jit(solution)/shard_map/ppermute | solution.py:479
  11.8 5.4 %collective-permute-start.4 = (f32[18,8,128]{2,1,0:T(8,128)S(1)}, f32[18,8,128]{2,1,0:T(8,128)S(1)}, u32[]{:S(2)}, u32[]{:S(2)}) collective-permute-start(f32[18,8,128]{2,1,0:T(8,128)S(1)} %get-tuple-element.28), channel_id=1, source_target_pairs={{0,1},{1,0},{2,3},{3,2},{4,5},{5,4},{6,7},{7,6},{8,9},{9,8},{10,11... | collective-permute-start | bytes 221192 | tf_op jit(solution)/shard_map/ppermute | solution.py:480
  11.9 5.6 %collective-permute-start.5 = (f32[18,8,128]{2,1,0:T(8,128)S(1)}, f32[18,8,128]{2,1,0:T(8,128)S(1)}, u32[]{:S(2)}, u32[]{:S(2)}) collective-permute-start(f32[18,8,128]{2,1,0:T(8,128)S(1)} %get-tuple-element.29), channel_id=1, source_target_pairs={{0,7},{1,2},{2,1},{3,4},{4,3},{5,6},{6,5},{7,0},{8,15},{9,10},{10,... | collective-permute-start | bytes 221192 | tf_op jit(solution)/shard_map/ppermute | solution.py:477
  13.5 3.8 %collective-permute-start.6 = (f32[12,4,128]{2,1,0:T(4,128)S(1)}, f32[12,4,128]{2,1,0:T(4,128)S(1)}, u32[]{:S(2)}, u32[]{:S(2)}) collective-permute-start(f32[12,4,128]{2,1,0:T(4,128)S(1)} %get-tuple-element.30), channel_id=1, source_target_pairs={{0,8},{8,0},{16,24},{24,16},{1,9},{9,1},{17,25},{25,17},{2,10},{10... | collective-permute-start | bytes 73736 | tf_op jit(solution)/shard_map/ppermute | solution.py:479
  17.7 6.9 %collective-permute-start.7 = (f32[12,8,128]{2,1,0:T(8,128)S(1)}, f32[12,8,128]{2,1,0:T(8,128)S(1)}, u32[]{:S(2)}, u32[]{:S(2)}) collective-permute-start(f32[12,8,128]{2,1,0:T(8,128)S(1)} %get-tuple-element.32), channel_id=1, source_target_pairs={{0,1},{1,0},{2,3},{3,2},{4,5},{5,4},{6,7},{7,6},{8,9},{9,8},{10,11... | collective-permute-start | bytes 147464 | tf_op jit(solution)/shard_map/ppermute | solution.py:480
  17.8 6.8 %collective-permute-start.8 = (f32[12,8,128]{2,1,0:T(8,128)S(1)}, f32[12,8,128]{2,1,0:T(8,128)S(1)}, u32[]{:S(2)}, u32[]{:S(2)}) collective-permute-start(f32[12,8,128]{2,1,0:T(8,128)S(1)} %get-tuple-element.33), channel_id=1, source_target_pairs={{0,7},{1,2},{2,1},{3,4},{4,3},{5,6},{6,5},{7,0},{8,15},{9,10},{10,... | collective-permute-start | bytes 147464 | tf_op jit(solution)/shard_map/ppermute | solution.py:477
  19.3 3.8 %collective-permute-start.9 = (f32[12,4,128]{2,1,0:T(4,128)S(1)}, f32[12,4,128]{2,1,0:T(4,128)S(1)}, u32[]{:S(2)}, u32[]{:S(2)}) collective-permute-start(f32[12,4,128]{2,1,0:T(4,128)S(1)} %get-tuple-element.34), channel_id=1, source_target_pairs={{0,8},{8,0},{16,24},{24,16},{1,9},{9,1},{17,25},{25,17},{2,10},{10... | collective-permute-start | bytes 73736 | tf_op jit(solution)/shard_map/ppermute | solution.py:479
  19.9 4.7 %collective-permute-start.10 = (f32[12,4,128]{2,1,0:T(4,128)S(1)}, f32[12,4,128]{2,1,0:T(4,128)S(1)}, u32[]{:S(2)}, u32[]{:S(2)}) collective-permute-start(f32[12,4,128]{2,1,0:T(4,128)S(1)} %get-tuple-element.35), channel_id=1, source_target_pairs={{0,24},{8,16},{16,8},{24,0},{1,25},{9,17},{17,9},{25,1},{2,26},{10... | collective-permute-start | bytes 73736 | tf_op jit(solution)/shard_map/ppermute | solution.py:478
  24.7 7.0 %collective-permute-start.11 = (f32[12,8,128]{2,1,0:T(8,128)S(1)}, f32[12,8,128]{2,1,0:T(8,128)S(1)}, u32[]{:S(2)}, u32[]{:S(2)}) collective-permute-start(f32[12,8,128]{2,1,0:T(8,128)S(1)} %get-tuple-element.37), channel_id=1, source_target_pairs={{0,1},{1,0},{2,3},{3,2},{4,5},{5,4},{6,7},{7,6},{8,9},{9,8},{10,11... | collective-permute-start | bytes 147464 | tf_op jit(solution)/shard_map/ppermute | solution.py:480
  24.8 6.9 %collective-permute-start.12 = (f32[12,8,128]{2,1,0:T(8,128)S(1)}, f32[12,8,128]{2,1,0:T(8,128)S(1)}, u32[]{:S(2)}, u32[]{:S(2)}) collective-permute-start(f32[12,8,128]{2,1,0:T(8,128)S(1)} %get-tuple-element.38), channel_id=1, source_target_pairs={{0,7},{1,2},{2,1},{3,4},{4,3},{5,6},{6,5},{7,0},{8,15},{9,10},{10,... | collective-permute-start | bytes 147464 | tf_op jit(solution)/shard_map/ppermute | solution.py:477
  25.5 3.8 %collective-permute-start.13 = (f32[12,4,128]{2,1,0:T(4,128)S(1)}, f32[12,4,128]{2,1,0:T(4,128)S(1)}, u32[]{:S(2)}, u32[]{:S(2)}) collective-permute-start(f32[12,4,128]{2,1,0:T(4,128)S(1)} %get-tuple-element.39), channel_id=1, source_target_pairs={{0,8},{8,0},{16,24},{24,16},{1,9},{9,1},{17,25},{25,17},{2,10},{10... | collective-permute-start | bytes 73736 | tf_op jit(solution)/shard_map/ppermute | solution.py:479
  27.0 4.7 %collective-permute-start.14 = (f32[12,4,128]{2,1,0:T(4,128)S(1)}, f32[12,4,128]{2,1,0:T(4,128)S(1)}, u32[]{:S(2)}, u32[]{:S(2)}) collective-permute-start(f32[12,4,128]{2,1,0:T(4,128)S(1)} %get-tuple-element.40), channel_id=1, source_target_pairs={{0,24},{8,16},{16,8},{24,0},{1,25},{9,17},{17,9},{25,1},{2,26},{10... | collective-permute-start | bytes 73736 | tf_op jit(solution)/shard_map/ppermute | solution.py:478

commit v5 on v4

--- a/solution.py
+++ b/solution.py
@@ -274,12 +274,17 @@
     store_parts(part_ref, result)
 
 
-def raw_slice(ref, j):
-    return [[tuple(ref[j, (s * 3 + c) * 2 + p] for p in range(2)) for c in range(3)] for s in range(4)]
+def slice_of(shape, ref, j):
+    def part(index):
+        if len(ref.shape) == 4:
+            return ref[j, index]
+        return ref[index, j * shape.blocks : (j + 1) * shape.blocks]
+
+    return [[tuple(part((s * 3 + c) * 2 + p) for p in range(2)) for c in range(3)] for s in range(4)]
 
 
 def neighbour_slice(shape, place, ref):
-    return pick(place.fifth_even, raw_slice(ref, shape.slices - 1), raw_slice(ref, 0))
+    return pick(place.fifth_even, slice_of(shape, ref, shape.slices - 1), slice_of(shape, ref, 0))
 
 
 def own_edge(shape, place, ref):
@@ -289,11 +294,11 @@
     return pick(place.fifth_even, first, last)
 
 
-def neighbour_kernel(shape, mirror_ref, origin_ref, wide_ref, part_ref):
+def neighbour_kernel(shape, across_ref, field_ref, wide_ref, part_ref):
     place = Place()
-    near = neighbour_slice(shape, place, mirror_ref)
-    beyond = pick(place.fifth_even, raw_slice(mirror_ref, shape.slices - 2), raw_slice(mirror_ref, 1))
-    edge = own_edge(shape, place, origin_ref)
+    near = neighbour_slice(shape, place, across_ref)
+    beyond = pick(place.fifth_even, slice_of(shape, across_ref, shape.slices - 2), slice_of(shape, across_ref, 1))
+    edge = own_edge(shape, place, field_ref)
     mass = jnp.where(place.fifth_even, place.low_mass, place.high_mass)
     edge = [[tuple(v * mass for v in pair) for pair in spin] for spin in edge]
     below = pick(place.fifth_even, beyond, edge)
@@ -328,8 +333,8 @@
     return [[tuple(part((s * 3 + c) * 2 + p) for p in range(2)) for c in range(3)] for s in range(2)]
 
 
-def send_neighbour(shape, place, mirror_ref, link, near_ref, far_ref):
-    field = neighbour_slice(shape, place, mirror_ref)
+def send_neighbour(shape, place, across_ref, link, near_ref, far_ref):
+    field = neighbour_slice(shape, place, across_ref)
     ahead = project(field, TIME, -1.0)
     behind = colour_mul(cut(link, 0, shape.blocks), project(field, TIME, 1.0), True)
     store_packed(shape, far_ref, pick(place.even, ahead, behind))
@@ -379,10 +384,9 @@
     side = load_half(side_ref)
     if neighbour is not None:
         across = computed_across(shape, place, link, near_ref, far_ref, neighbour[0], start_ref, *neighbour[1:])
-    elif across_ref is None:
-        final = [[tuple(start_ref[shape.slices - 1, (s * 3 + c) * 2 + p] for p in range(2)) for c in range(3)] for s in range(2)]
-        first = [[tuple(start_ref[0, (s * 3 + c) * 2 + p] for p in range(2)) for c in range(3)] for s in range(2, 4)]
-        across = pick(place.fifth_even, final, first)
+    elif 24 in across_ref.shape[:2]:
+        final, first = slice_of(shape, across_ref, shape.slices - 1), slice_of(shape, across_ref, 0)
+        across = pick(place.fifth_even, final[0:2], first[2:4])
     else:
         across = load_half(across_ref)
     low = pick(place.fifth_even, across, side)
@@ -416,8 +420,8 @@
     field_ref, near_out, far_out, side_out, *across_out = out_refs
     across_out = across_out[0] if across_out else None
     send_parts(shape, field, link, place, not odd_step, near_out, far_out, side_out, across_out)
-    if across_out is None:
-        send_neighbour(shape, place, start_ref, link, near_out, far_out)
+    if across_out is None and not odd_step:
+        send_neighbour(shape, place, across_ref, link, near_out, far_out)
     store_parts(field_ref, field)
 
 
@@ -471,9 +475,11 @@
     sends = (whole, half, half, edge) + ((edge,) if first_across else ())
     scratch = (pltpu.VMEM((18, rows, LANES), jnp.float32), pltpu.SemaphoreType.DMA((2 * slices,)))
     origin, near, far, side, *across = call(first, sends, start, links, table, operand_specs=(hbm, hbm, vmem), scratch=scratch)
-    field, wide = origin, None
+    field, wide, across_whole = origin, None, mirrored
     for step in range(DEGREE):
         odd_step, last = step % 2 == 1, step == DEGREE - 1
+        if not first_across:
+            across = [field] if step > 0 and not odd_step else []
         far_in = lax.ppermute(far, "space", far_pairs)
         across_in = [lax.ppermute(value, "fifth", across_pairs) for value in across]
         side_in = lax.ppermute(side, "fifth", side_pairs)
@@ -482,26 +488,31 @@
             wide = call(lambda *refs: widen_kernel(shape, *refs), array(72, rows, LANES), links)
         part = call(lambda *refs, odd=odd_step: space_kernel(shape, odd, *refs), whole, field, wide)
         scale = weights[DEGREE] if step == 0 else 1.0
-        computed = step == 1 and not first_across
+        computed = odd_step and not first_across
         if computed:
-            extra = (call(lambda *refs: neighbour_kernel(shape, *refs), array(24, blocks, LANES), mirrored, origin, wide),)
+            extra = call(
+                lambda *refs: neighbour_kernel(shape, *refs), array(24, blocks, LANES), across_whole, across_field, wide
+            )
+        elif first_across:
+            (extra,) = across_in
         else:
-            extra = tuple(across_in)
-
-        def close(*refs, step=step, odd=odd_step, last=last, scale=scale, computed=computed, count=len(extra)):
-            across_ref = refs[6] if count and not computed else None
-            neighbour = (refs[6], weights[DEGREE], weights[DEGREE - 1]) if computed else None
+            across_whole = across_in[0] if step > 0 else mirrored
+            extra, across_field = across_whole, field
+
+        def close(*refs, step=step, odd=odd_step, last=last, scale=scale, computed=computed):
+            across_ref = None if computed else refs[6]
+            neighbour = (refs[6], weights[DEGREE] if step == 1 else 1.0, weights[DEGREE - step]) if computed else None
             weight = weights[DEGREE - 1 - step]
-            close_kernel(shape, odd, scale, weight, last, *refs[:6], across_ref, neighbour, refs[6 + count :])
-
-        operands = (part, wide, origin if odd_step else mirrored, near_in, far_in, side_in, *extra)
+            close_kernel(shape, odd, scale, weight, last, *refs[:6], across_ref, neighbour, refs[7:])
+
+        operands = (part, wide, origin if odd_step else mirrored, near_in, far_in, side_in, extra)
         if last:
             result = call(close, array(slices, 24, blocks, LANES), *operands)
-        elif step == 0 and not first_across:
-            more = array(12 + -(-12 // slices), rows, LANES)
-            field, near, far, side, *across = call(close, (whole, more, more, edge), *operands)
+        elif first_across:
+            field, near, far, side, *across = call(close, (whole, half, half, edge, edge), *operands)
         else:
-            field, near, far, side, *across = call(close, (whole, half, half, edge, edge), *operands)
+            message = half if odd_step else array(12 + -(-12 // slices), rows, LANES)
+            field, near, far, side = call(close, (whole, message, message, edge), *operands)
     return result.reshape(slices, 24, depth, sites)
 
 

time: 32.6 us -> 30.8 us (0.945)
  starting transfers between devices: 17.2 us -> 16 us
  waiting for transfers between devices: 12.8 us -> 11.9 us
    ppermute x2 -> x1, waiting for transfers between devices: 3.81 us -> 0.01 us  [on_device(): across_in = [lax.ppermute(value, 'fifth', across_pairs) for value in across]]
    ppermute x4, waiting for transfers between devices: 8.68 us -> 10.8 us  [on_device(): side_in = lax.ppermute(side, 'fifth', side_pairs)]
    ppermute x2 -> x1, starting transfers between devices: 2.37 us -> 1 us  [on_device(): across_in = [lax.ppermute(value, 'fifth', across_pairs) for value in across]]
    ppermute x4, waiting for transfers between devices: 0.28 us -> 1.13 us  [on_device(): far_in = lax.ppermute(far, 'space', far_pairs)]
    pallas_call x11 -> x12, Pallas kernels: 2.39 us -> 2.67 us  [call(): pl.pallas_call(body, out_shape=out_shape, in_specs=operand_specs or [vmem...]
  transfers between devices with their start and end apart: 15 -> 14, of which waited for: 7 -> 7; matrix products, arithmetic and copies ran while one was open for 0% -> 0% of each run, Pallas kernels for 4% -> 5%
where the time goes in v5:
time: 30.8 us; the launch traced here: 30.7 us
  starting transfers between devices  16 us (52%)
  waiting for transfers between devices  11.9 us (39%)
  Pallas kernels  2.67 us (9%)
    ppermute x4, waiting for transfers between devices, on_device(): side_in = lax.ppermute(side, 'fifth', side_pairs)  10.8 us
    ppermute x4, starting transfers between devices, on_device(): far_in = lax.ppermute(far, 'space', far_pairs)  7.68 us
    ppermute x1, starting transfers between devices, on_device(): mirrored = lax.ppermute(start, 'fifth', mirror_pairs)  3.92 us
    ppermute x4, starting transfers between devices, on_device(): side_in = lax.ppermute(side, 'fifth', side_pairs)  3.14 us
    pallas_call x12, Pallas kernels, call(): pl.pallas_call(body, out_shape=out_shape, in_specs=operand_specs or [vmem...  2.67 us
    ppermute x4, waiting for transfers between devices, on_device(): far_in = lax.ppermute(far, 'space', far_pairs)  1.13 us
    ppermute x1, starting transfers between devices, on_device(): across_in = [lax.ppermute(value, 'fifth', across_pairs) for value in across]  1 us
  transfers between devices with their start and end apart: 14, of which 7 were waited for; matrix products, arithmetic and copies ran while one was open for 0% of the time, Pallas kernels for 5%

profile of v5, /device:TPU:0, one launch (start us, length us, event | category | flops | bytes accessed | tf_op | source)
XLA Modules:
  0.0 30.7 jit_solution(3133388947654124703)
XLA Ops:
  0.0 0.0 copy-start
  0.0 0.0 copy-start.1
  0.0 3.9 %collective-permute-start = (f32[2,24,4,128]{3,2,1,0:T(4,128)}, f32[2,24,4,128]{3,2,1,0:T(4,128)S(1)}, u32[]{:S(2)}, u32[]{:S(2)}) collective-permute-start(f32[2,24,4,128]{3,2,1,0:T(4,128)} %bitcast.5), channel_id=1, source_target_pairs={{0,24},{8,16},{16,8},{24,0},{1,25},{9,17},{17,9},{25,1},{2,26},{10... | collective-permute-start | bytes 294920 | tf_op jit(solution)/shard_map/ppermute | solution.py:469
  3.9 0.0 copy-done
  3.9 0.0 copy-done.1
  4.0 0.1 shard_map.29
  4.1 0.1 collective-permute-start.1
  4.1 3.7 %collective-permute-start.2 = (f32[12,8,128]{2,1,0:T(8,128)S(1)}, f32[12,8,128]{2,1,0:T(8,128)S(1)}, u32[]{:S(2)}, u32[]{:S(2)}) collective-permute-start(f32[12,8,128]{2,1,0:T(8,128)S(1)} %get-tuple-element.23), channel_id=1, source_target_pairs={{0,7},{1,2},{2,1},{3,4},{4,3},{5,6},{6,5},{7,0},{8,15},{9,10},{10,... | collective-permute-start | bytes 147464 | tf_op jit(solution)/shard_map/ppermute | solution.py:483
  7.8 0.5 %collective-permute-start.3 = (f32[12,4,128]{2,1,0:T(4,128)S(1)}, f32[12,4,128]{2,1,0:T(4,128)S(1)}, u32[]{:S(2)}, u32[]{:S(2)}) collective-permute-start(f32[12,4,128]{2,1,0:T(4,128)S(1)} %get-tuple-element.24), channel_id=1, source_target_pairs={{0,8},{8,0},{16,24},{24,16},{1,9},{9,1},{17,25},{25,17},{2,10},{10... | collective-permute-start | bytes 73736 | tf_op jit(solution)/shard_map/ppermute | solution.py:485
  8.4 0.2 shard_map.31.refs_0_
  8.6 3.0 %collective-permute-done.3.refs_5_ = f32[12,4,128]{2,1,0:T(4,128)S(1)} collective-permute-done((f32[12,4,128]{2,1,0:T(4,128)S(1)}, f32[12,4,128]{2,1,0:T(4,128)S(1)}, u32[]{:S(2)}, u32[]{:S(2)}) %collective-permute-start.3) | collective-permute-done | bytes 24608 | tf_op jit(solution)/shard_map/ppermute | solution.py:485
  11.7 0.0 collective-permute-done.1.refs_3_
  11.7 0.0 collective-permute-done.2.refs_4_
  11.7 0.0 collective-permute-done.refs_2_.refs_6_.refs_0_
  11.7 0.1 shard_map.32
  11.8 0.1 collective-permute-start.4
  11.9 1.5 %collective-permute-start.5 = (f32[18,8,128]{2,1,0:T(8,128)S(1)}, f32[18,8,128]{2,1,0:T(8,128)S(1)}, u32[]{:S(2)}, u32[]{:S(2)}) collective-permute-start(f32[18,8,128]{2,1,0:T(8,128)S(1)} %get-tuple-element.27), channel_id=1, source_target_pairs={{0,7},{1,2},{2,1},{3,4},{4,3},{5,6},{6,5},{7,0},{8,15},{9,10},{10,... | collective-permute-start | bytes 221192 | tf_op jit(solution)/shard_map/ppermute | solution.py:483
  13.5 0.5 %collective-permute-start.6 = (f32[12,4,128]{2,1,0:T(4,128)S(1)}, f32[12,4,128]{2,1,0:T(4,128)S(1)}, u32[]{:S(2)}, u32[]{:S(2)}) collective-permute-start(f32[12,4,128]{2,1,0:T(4,128)S(1)} %get-tuple-element.28), channel_id=1, source_target_pairs={{0,8},{8,0},{16,24},{24,16},{1,9},{9,1},{17,25},{25,17},{2,10},{10... | collective-permute-start | bytes 73736 | tf_op jit(solution)/shard_map/ppermute | solution.py:485
  14.0 0.2 shard_map.33.refs_0_
  14.2 0.2 shard_map.34.refs_6_
  14.5 2.8 %collective-permute-done.6.refs_5_ = f32[12,4,128]{2,1,0:T(4,128)S(1)} collective-permute-done((f32[12,4,128]{2,1,0:T(4,128)S(1)}, f32[12,4,128]{2,1,0:T(4,128)S(1)}, u32[]{:S(2)}, u32[]{:S(2)}) %collective-permute-start.6) | collective-permute-done | bytes 24608 | tf_op jit(solution)/shard_map/ppermute | solution.py:485
  17.3 0.0 collective-permute-done.4.refs_3_
  17.3 0.3 collective-permute-done.5.refs_4_
  17.6 0.2 shard_map.35
  17.7 1.0 %collective-permute-start.10 = (f32[24,8,128]{2,1,0:T(8,128)S(1)}, f32[24,8,128]{2,1,0:T(8,128)S(1)}, u32[]{:S(2)}, u32[]{:S(2)}) collective-permute-start(f32[24,8,128]{2,1,0:T(8,128)S(1)} %get-tuple-element.29.refs_0_.refs_1_), channel_id=1, source_target_pairs={{0,24},{8,16},{16,8},{24,0},{1,25},{9,17},{17,9},{25,1},{2,26},{10... | collective-permute-start | bytes 294920 | tf_op jit(solution)/shard_map/ppermute | solution.py:484
  18.7 0.0 collective-permute-start.7
  18.7 1.2 %collective-permute-start.8 = (f32[12,8,128]{2,1,0:T(8,128)S(1)}, f32[12,8,128]{2,1,0:T(8,128)S(1)}, u32[]{:S(2)}, u32[]{:S(2)}) collective-permute-start(f32[12,8,128]{2,1,0:T(8,128)S(1)} %get-tuple-element.31), channel_id=1, source_target_pairs={{0,7},{1,2},{2,1},{3,4},{4,3},{5,6},{6,5},{7,0},{8,15},{9,10},{10,... | collective-permute-start | bytes 147464 | tf_op jit(solution)/shard_map/ppermute | solution.py:483
  19.9 1.0 %collective-permute-start.9 = (f32[12,4,128]{2,1,0:T(4,128)S(1)}, f32[12,4,128]{2,1,0:T(4,128)S(1)}, u32[]{:S(2)}, u32[]{:S(2)}) collective-permute-start(f32[12,4,128]{2,1,0:T(4,128)S(1)} %get-tuple-element.32), channel_id=1, source_target_pairs={{0,8},{8,0},{16,24},{24,16},{1,9},{9,1},{17,25},{25,17},{2,10},{10... | collective-permute-start | bytes 73736 | tf_op jit(solution)/shard_map/ppermute | solution.py:485
  21.0 0.2 shard_map.36.refs_0_
  21.2 2.6 %collective-permute-done.9.refs_5_ = f32[12,4,128]{2,1,0:T(4,128)S(1)} collective-permute-done((f32[12,4,128]{2,1,0:T(4,128)S(1)}, f32[12,4,128]{2,1,0:T(4,128)S(1)}, u32[]{:S(2)}, u32[]{:S(2)}) %collective-permute-start.9) | collective-permute-done | bytes 24608 | tf_op jit(solution)/shard_map/ppermute | solution.py:485
  23.8 0.0 collective-permute-done.7.refs_3_
  23.8 0.3 collective-permute-done.8.refs_4_
  24.0 0.0 collective-permute-done.10.refs_6_.refs_0_
  24.0 0.1 shard_map.37
  24.2 0.1 collective-permute-start.11
  24.3 1.3 %collective-permute-start.12 = (f32[18,8,128]{2,1,0:T(8,128)S(1)}, f32[18,8,128]{2,1,0:T(8,128)S(1)}, u32[]{:S(2)}, u32[]{:S(2)}) collective-permute-start(f32[18,8,128]{2,1,0:T(8,128)S(1)} %get-tuple-element.35), channel_id=1, source_target_pairs={{0,7},{1,2},{2,1},{3,4},{4,3},{5,6},{6,5},{7,0},{8,15},{9,10},{10,... | collective-permute-start | bytes 221192 | tf_op jit(solution)/shard_map/ppermute | solution.py:483
  25.5 1.0 %collective-permute-start.13 = (f32[12,4,128]{2,1,0:T(4,128)S(1)}, f32[12,4,128]{2,1,0:T(4,128)S(1)}, u32[]{:S(2)}, u32[]{:S(2)}) collective-permute-start(f32[12,4,128]{2,1,0:T(4,128)S(1)} %get-tuple-element.36), channel_id=1, source_target_pairs={{0,8},{8,0},{16,24},{24,16},{1,9},{9,1},{17,25},{25,17},{2,10},{10... | collective-permute-start | bytes 73736 | tf_op jit(solution)/shard_map/ppermute | solution.py:485
  26.6 0.2 shard_map.38.refs_0_
  26.8 0.2 shard_map.39.refs_6_
  27.0 2.3 %collective-permute-done.13.refs_5_ = f32[12,4,128]{2,1,0:T(4,128)S(1)} collective-permute-done((f32[12,4,128]{2,1,0:T(4,128)S(1)}, f32[12,4,128]{2,1,0:T(4,128)S(1)}, u32[]{:S(2)}, u32[]{:S(2)}) %collective-permute-start.13) | collective-permute-done | bytes 24608 | tf_op jit(solution)/shard_map/ppermute | solution.py:485
  29.4 0.0 collective-permute-done.11.refs_3_
  29.4 0.6 %collective-permute-done.12.refs_4_ = f32[18,8,128]{2,1,0:T(8,128)S(1)} collective-permute-done((f32[18,8,128]{2,1,0:T(8,128)S(1)}, f32[18,8,128]{2,1,0:T(8,128)S(1)}, u32[]{:S(2)}, u32[]{:S(2)}) %collective-permute-start.12) | collective-permute-done | bytes 73760 | tf_op jit(solution)/shard_map/ppermute | solution.py:483
  29.9 0.8 %shard_map.40 = f32[2,24,4,128]{3,2,1,0:T(4,128)} custom-call(f32[24,8,128]{2,1,0:T(8,128)S(1)} %shard_map.38.refs_0_, f32[72,8,128]{2,1,0:T(8,128)S(1)} %shard_map.30.refs_1_.refs_2_, f32[24,8,128]{2,1,0:T(8,128)S(1)} %get-tuple-element.21.refs_0_.refs_1_.refs_2_, f32[18,8,128]{2,1,0:T(8,128)S(1)} %collective-permute-done.11.refs_3_, ...), custom_call_target="tpu_custom_call" | custom-call | tf_op jit(solution)/shard_map/pallas_call | solution.py:449
  (2 shorter events, 0.0 us)
Async XLA Ops:
  0.0 3.9 %copy-start = (f32[4,18,1,512]{3,2,1,0:T(1,128)S(1)}, f32[4,18,1,512]{3,2,1,0:T(1,128)}, u32[]{:S(2)}) copy-start(f32[4,18,1,512]{3,2,1,0:T(1,128)} %param.3) | copy-start | bytes 442372
  0.0 3.9 %copy-start.1 = (f32[2,24,1,512]{3,2,1,0:T(1,128)S(1)}, f32[2,24,1,512]{3,2,1,0:T(1,128)}, u32[]{:S(2)}) copy-start(f32[2,24,1,512]{3,2,1,0:T(1,128)} %param.2) | copy-start | bytes 294916
  0.0 11.7 %collective-permute-start = (f32[2,24,4,128]{3,2,1,0:T(4,128)}, f32[2,24,4,128]{3,2,1,0:T(4,128)S(1)}, u32[]{:S(2)}, u32[]{:S(2)}) collective-permute-start(f32[2,24,4,128]{3,2,1,0:T(4,128)} %bitcast.5), channel_id=1, source_target_pairs={{0,24},{8,16},{16,8},{24,0},{1,25},{9,17},{17,9},{25,1},{2,26},{10... | collective-permute-start | bytes 294920 | tf_op jit(solution)/shard_map/ppermute | solution.py:469
  4.1 7.6 %collective-permute-start.1 = (f32[12,8,128]{2,1,0:T(8,128)S(1)}, f32[12,8,128]{2,1,0:T(8,128)S(1)}, u32[]{:S(2)}, u32[]{:S(2)}) collective-permute-start(f32[12,8,128]{2,1,0:T(8,128)S(1)} %get-tuple-element.22), channel_id=1, source_target_pairs={{0,1},{1,0},{2,3},{3,2},{4,5},{5,4},{6,7},{7,6},{8,9},{9,8},{10,11... | collective-permute-start | bytes 147464 | tf_op jit(solution)/shard_map/ppermute | solution.py:486
  4.1 7.5 %collective-permute-start.2 = (f32[12,8,128]{2,1,0:T(8,128)S(1)}, f32[12,8,128]{2,1,0:T(8,128)S(1)}, u32[]{:S(2)}, u32[]{:S(2)}) collective-permute-start(f32[12,8,128]{2,1,0:T(8,128)S(1)} %get-tuple-element.23), channel_id=1, source_target_pairs={{0,7},{1,2},{2,1},{3,4},{4,3},{5,6},{6,5},{7,0},{8,15},{9,10},{10,... | collective-permute-start | bytes 147464 | tf_op jit(solution)/shard_map/ppermute | solution.py:483
  7.8 3.8 %collective-permute-start.3 = (f32[12,4,128]{2,1,0:T(4,128)S(1)}, f32[12,4,128]{2,1,0:T(4,128)S(1)}, u32[]{:S(2)}, u32[]{:S(2)}) collective-permute-start(f32[12,4,128]{2,1,0:T(4,128)S(1)} %get-tuple-element.24), channel_id=1, source_target_pairs={{0,8},{8,0},{16,24},{24,16},{1,9},{9,1},{17,25},{25,17},{2,10},{10... | collective-permute-start | bytes 73736 | tf_op jit(solution)/shard_map/ppermute | solution.py:485
  11.8 5.4 %collective-permute-start.4 = (f32[18,8,128]{2,1,0:T(8,128)S(1)}, f32[18,8,128]{2,1,0:T(8,128)S(1)}, u32[]{:S(2)}, u32[]{:S(2)}) collective-permute-start(f32[18,8,128]{2,1,0:T(8,128)S(1)} %get-tuple-element.26), channel_id=1, source_target_pairs={{0,1},{1,0},{2,3},{3,2},{4,5},{5,4},{6,7},{7,6},{8,9},{9,8},{10,11... | collective-permute-start | bytes 221192 | tf_op jit(solution)/shard_map/ppermute | solution.py:486
  11.9 5.6 %collective-permute-start.5 = (f32[18,8,128]{2,1,0:T(8,128)S(1)}, f32[18,8,128]{2,1,0:T(8,128)S(1)}, u32[]{:S(2)}, u32[]{:S(2)}) collective-permute-start(f32[18,8,128]{2,1,0:T(8,128)S(1)} %get-tuple-element.27), channel_id=1, source_target_pairs={{0,7},{1,2},{2,1},{3,4},{4,3},{5,6},{6,5},{7,0},{8,15},{9,10},{10,... | collective-permute-start | bytes 221192 | tf_op jit(solution)/shard_map/ppermute | solution.py:483
  13.5 3.8 %collective-permute-start.6 = (f32[12,4,128]{2,1,0:T(4,128)S(1)}, f32[12,4,128]{2,1,0:T(4,128)S(1)}, u32[]{:S(2)}, u32[]{:S(2)}) collective-permute-start(f32[12,4,128]{2,1,0:T(4,128)S(1)} %get-tuple-element.28), channel_id=1, source_target_pairs={{0,8},{8,0},{16,24},{24,16},{1,9},{9,1},{17,25},{25,17},{2,10},{10... | collective-permute-start | bytes 73736 | tf_op jit(solution)/shard_map/ppermute | solution.py:485
  17.7 6.3 %collective-permute-start.10 = (f32[24,8,128]{2,1,0:T(8,128)S(1)}, f32[24,8,128]{2,1,0:T(8,128)S(1)}, u32[]{:S(2)}, u32[]{:S(2)}) collective-permute-start(f32[24,8,128]{2,1,0:T(8,128)S(1)} %get-tuple-element.29.refs_0_.refs_1_), channel_id=1, source_target_pairs={{0,24},{8,16},{16,8},{24,0},{1,25},{9,17},{17,9},{25,1},{2,26},{10... | collective-permute-start | bytes 294920 | tf_op jit(solution)/shard_map/ppermute | solution.py:484
  18.7 5.0 %collective-permute-start.7 = (f32[12,8,128]{2,1,0:T(8,128)S(1)}, f32[12,8,128]{2,1,0:T(8,128)S(1)}, u32[]{:S(2)}, u32[]{:S(2)}) collective-permute-start(f32[12,8,128]{2,1,0:T(8,128)S(1)} %get-tuple-element.30), channel_id=1, source_target_pairs={{0,1},{1,0},{2,3},{3,2},{4,5},{5,4},{6,7},{7,6},{8,9},{9,8},{10,11... | collective-permute-start | bytes 147464 | tf_op jit(solution)/shard_map/ppermute | solution.py:486
  18.7 5.3 %collective-permute-start.8 = (f32[12,8,128]{2,1,0:T(8,128)S(1)}, f32[12,8,128]{2,1,0:T(8,128)S(1)}, u32[]{:S(2)}, u32[]{:S(2)}) collective-permute-start(f32[12,8,128]{2,1,0:T(8,128)S(1)} %get-tuple-element.31), channel_id=1, source_target_pairs={{0,7},{1,2},{2,1},{3,4},{4,3},{5,6},{6,5},{7,0},{8,15},{9,10},{10,... | collective-permute-start | bytes 147464 | tf_op jit(solution)/shard_map/ppermute | solution.py:483
  19.9 3.8 %collective-permute-start.9 = (f32[12,4,128]{2,1,0:T(4,128)S(1)}, f32[12,4,128]{2,1,0:T(4,128)S(1)}, u32[]{:S(2)}, u32[]{:S(2)}) collective-permute-start(f32[12,4,128]{2,1,0:T(4,128)S(1)} %get-tuple-element.32), channel_id=1, source_target_pairs={{0,8},{8,0},{16,24},{24,16},{1,9},{9,1},{17,25},{25,17},{2,10},{10... | collective-permute-start | bytes 73736 | tf_op jit(solution)/shard_map/ppermute | solution.py:485
  24.2 5.2 %collective-permute-start.11 = (f32[18,8,128]{2,1,0:T(8,128)S(1)}, f32[18,8,128]{2,1,0:T(8,128)S(1)}, u32[]{:S(2)}, u32[]{:S(2)}) collective-permute-start(f32[18,8,128]{2,1,0:T(8,128)S(1)} %get-tuple-element.34), channel_id=1, source_target_pairs={{0,1},{1,0},{2,3},{3,2},{4,5},{5,4},{6,7},{7,6},{8,9},{9,8},{10,11... | collective-permute-start | bytes 221192 | tf_op jit(solution)/shard_map/ppermute | solution.py:486
  24.3 5.6 %collective-permute-start.12 = (f32[18,8,128]{2,1,0:T(8,128)S(1)}, f32[18,8,128]{2,1,0:T(8,128)S(1)}, u32[]{:S(2)}, u32[]{:S(2)}) collective-permute-start(f32[18,8,128]{2,1,0:T(8,128)S(1)} %get-tuple-element.35), channel_id=1, source_target_pairs={{0,7},{1,2},{2,1},{3,4},{4,3},{5,6},{6,5},{7,0},{8,15},{9,10},{10,... | collective-permute-start | bytes 221192 | tf_op jit(solution)/shard_map/ppermute | solution.py:483
  25.5 3.8 %collective-permute-start.13 = (f32[12,4,128]{2,1,0:T(4,128)S(1)}, f32[12,4,128]{2,1,0:T(4,128)S(1)}, u32[]{:S(2)}, u32[]{:S(2)}) collective-permute-start(f32[12,4,128]{2,1,0:T(4,128)S(1)} %get-tuple-element.36), channel_id=1, source_target_pairs={{0,8},{8,0},{16,24},{24,16},{1,9},{9,1},{17,25},{25,17},{2,10},{10... | collective-permute-start | bytes 73736 | tf_op jit(solution)/shard_map/ppermute | solution.py:485
